TPU v7x, 32 devices: a whole 2x2x4 slice. The times are simulated.
32 devices in a mesh: atlas: 4 (over y, x), row: 2 (over core), col: 4 (over z).
Axes of the slice: x: 2, y: 2, z: 4, core: 2. Of those that a mesh axis runs over, the one named last changes fastest.
Arguments:
- cells: bfloat16 [4, 64, 1024], P('atlas', None, 'row'), may hold values from -4 to 4
- support: bfloat16 [64, 16384], P(None, 'col'), may hold values from -4 to 4
Outputs:
- cell_dual: float32 [4, 1024], P('atlas', 'row')
- support_dual: float32 [4, 16384], P('atlas', 'col')
- new_support: float32 [64, 16384], P(None, 'col')
All inputs are finite; a program needn't handle non-finite values.
Results may differ from a plain program's by a relative error of at most 0.001.
Values sent between devices are 32-bit elements; how exact they have to be, the bound alone decides.
No kernel may reach another device: no remote copies, remote signals or barrier semaphores. Data moves between devices by JAX's collectives and lax.ppermute only.
A program may use at most 64 MiB of HBM per device.

v0:
```python
import jax
import jax.numpy as jnp
from jax import lax
from jax.sharding import PartitionSpec as P

ITERS = 2


blur = 0.1


def combined_all(value, axis, join):
    pieces = jax.tree.map(lambda part: lax.all_gather(part, axis), value)
    head = jax.tree.map(lambda part: part[0], pieces)
    tail = jax.tree.map(lambda part: part[1:], pieces)
    subtotal, _ = lax.scan(lambda subtotal, slab: (join(subtotal, slab), None), head, tail)
    return subtotal


def lse_pair(first, second):
    top_one, total_one = first
    top_two, total_two = second
    peak = jnp.maximum(top_one, top_two)
    return (peak, total_one * jnp.exp(top_one - peak) + total_two * jnp.exp(top_two - peak))


def shards(cells, support):
    points = cells[0]
    dims, rows = points.shape
    columns = support.shape[1]
    width_block = min(512, columns)
    count = columns // width_block
    points_wide = points.astype(jnp.float32)
    squares_x = jnp.sum(jnp.square(points_wide), axis=0)
    squares_y = jnp.sum(jnp.square(support.astype(jnp.float32)), axis=0)
    total_cells = rows * lax.axis_size("row")
    total_support = columns * lax.axis_size("col")
    atlases = lax.axis_size("atlas")

    def tile_cost(start):
        piece = lax.dynamic_slice_in_dim(support, start, width_block, 1)
        near = lax.dynamic_slice_in_dim(squares_y, start, width_block, 0)
        cross = lax.dot_general(
            points, piece, (((0,), (0,)), ((), ())), preferred_element_type=jnp.float32
        )
        return (squares_x[:, None] + near[None, :] - 2.0 * cross) / dims

    def row_step(dual_g):

        def row_visit(index, carry):
            top, total = carry
            start = index * width_block
            gpart = lax.dynamic_slice_in_dim(dual_g, start, width_block, 0)
            logits = (gpart[None, :] - tile_cost(start)) / blur
            peak = jnp.maximum(top, jnp.max(logits, axis=1))
            total = total * jnp.exp(top - peak) + jnp.sum(jnp.exp(logits - peak[:, None]), axis=1)
            return (peak, total)

        start_carry = (jnp.full((rows,), -jnp.inf, jnp.float32), jnp.zeros((rows,), jnp.float32))
        top, total = lax.fori_loop(0, count, row_visit, start_carry)
        top, total = combined_all((top, total), "col", lse_pair)
        return blur * jnp.log(1.0 / total_cells) - blur * (top + jnp.log(total))

    def column_step(dual_f):

        def column_visit(index, carry):
            top, total = carry
            start = index * width_block
            logits = (dual_f[:, None] - tile_cost(start)) / blur
            peak = jnp.max(logits, axis=0)
            mass = jnp.sum(jnp.exp(logits - peak[None, :]), axis=0)
            return (
                lax.dynamic_update_slice_in_dim(top, peak, start, 0),
                lax.dynamic_update_slice_in_dim(total, mass, start, 0),
            )

        start_carry = (jnp.zeros((columns,), jnp.float32), jnp.zeros((columns,), jnp.float32))
        top, total = lax.fori_loop(0, count, column_visit, start_carry)
        top, total = combined_all((top, total), "row", lse_pair)
        return blur * jnp.log(1.0 / total_support) - blur * (top + jnp.log(total))

    dual_g = jnp.zeros((columns,), jnp.float32)
    dual_f = jnp.zeros((rows,), jnp.float32)
    for step in range(ITERS):
        dual_f = row_step(dual_g)
        dual_g = column_step(dual_f)

    def positions_visit(index, summed):
        start = index * width_block
        gpart = lax.dynamic_slice_in_dim(dual_g, start, width_block, 0)
        plan = jnp.exp((dual_f[:, None] + gpart[None, :] - tile_cost(start)) / blur)
        moved = jnp.dot(points_wide, plan, precision=lax.Precision.HIGHEST) * total_support
        return lax.dynamic_update_slice_in_dim(summed, moved, start, 1)

    terms = lax.fori_loop(0, count, positions_visit, jnp.zeros((dims, columns), jnp.float32))
    summed = lax.psum(terms, ("atlas", "row"))
    updated = summed / atlases
    return (dual_f[None, :], dual_g[None, :], updated)


def solution(mesh):
    in_specs = (P("atlas", None, "row"), P(None, "col"))
    out_specs = (P("atlas", "row"), P("atlas", "col"), P(None, "col"))
    return jax.shard_map(shards, mesh=mesh, in_specs=in_specs, out_specs=out_specs, check_vma=False)
```

profile of v0, /device:TPU:0, one launch (start us, length us, event | category | flops | bytes accessed | tf_op | source)
XLA Modules:
  0.0 182.5 jit_solution(9270883459431666822)
XLA Ops:
  7.3 0.9 multiply_reduce_fusion.1
  8.2 1.2 multiply_reduce_fusion
  9.4 6.2 %while.114 = (s32[]{:T(128)}, f32[512]{0:T(512)S(1)}, f32[512]{0:T(512)S(1)}, f32[512]{0:T(512)S(1)}, f32[4096]{0:T(1024)S(1)}, /*index=5*/bf16[64,4096]{1,0:T(8...) while((s32[]{:T(128)}, f32[512]{0:T(512)S(1)}, ...), condition=%wide.region_5.0_spmd.clone, body=%wide.region_2.0_spmd.clone.sunk | while | flops 35916292 | bytes 2263222 | solution.py:60
  15.6 13.6 %all-gather.8 = f32[4,1,512]{2,1,0:T(1,128)S(1)} all-gather(f32[1,1,512]{2,1,0:T(1,128)S(1)} %bitcast.124), channel_id=2, replica_groups=mesh['atlas'=4,'row'=2,'col'=4] {'col'}, dimensions={0}, use_global_device_ids=true | all-gather | bytes 10240 | tf_op jit(solution)/shard_map/all_gather | solution.py:13
  29.3 0.6 copy-done.4
  29.9 11.9 %all-gather.9 = f32[4,1,512]{2,1,0:T(1,128)S(1)} all-gather(f32[1,1,512]{2,1,0:T(1,128)S(1)} %bitcast.134), channel_id=3, replica_groups=mesh['atlas'=4,'row'=2,'col'=4] {'col'}, dimensions={0}, use_global_device_ids=true | all-gather | bytes 10240 | tf_op jit(solution)/shard_map/all_gather | solution.py:13
  41.8 0.7 slice-done.3
  42.5 0.7 slice-done.2
  43.4 10.0 %while.110 = (s32[]{:T(128)}, f32[4096]{0:T(1024)S(1)}, f32[4096]{0:T(1024)S(1)}, f32[512]{0:T(512)S(1)}, f32[512]{0:T(512)S(1)}, /*index=5*/f32[4096]{0:T(1024)...) while((s32[]{:T(128)}, f32[4096]{0:T(1024)S(1)}, ...), condition=%wide.region_11.12_spmd, body=%wide.region_8.11_spmd.sunk | while | flops 35912708 | bytes 2252979 | solution.py:78
  53.4 1.8 all-gather.3
  55.2 1.8 all-gather.2
  57.0 6.8 %while.115 = (s32[]{:T(128)}, f32[512]{0:T(512)S(1)}, f32[512]{0:T(512)S(1)}, f32[4096]{0:T(1024)S(1)}, f32[512]{0:T(512)S(1)}, /*index=5*/f32[4096]{0:T(1024)S(...) while((s32[]{:T(128)}, f32[512]{0:T(512)S(1)}, ...), condition=%wide.region_15.16_spmd.clone, body=%wide.region_12.0_spmd.clone.sunk | while | flops 35916292 | bytes 2269378 | solution.py:60
  63.9 11.9 %all-gather.10 = f32[4,1,512]{2,1,0:T(1,128)S(1)} all-gather(f32[1,1,512]{2,1,0:T(1,128)S(1)} %bitcast.123), channel_id=6, replica_groups=mesh['atlas'=4,'row'=2,'col'=4] {'col'}, dimensions={0}, use_global_device_ids=true | all-gather | bytes 10240 | tf_op jit(solution)/shard_map/all_gather | solution.py:13
  76.4 11.9 %all-gather.11 = f32[4,1,512]{2,1,0:T(1,128)S(1)} all-gather(f32[1,1,512]{2,1,0:T(1,128)S(1)} %bitcast.133), channel_id=7, replica_groups=mesh['atlas'=4,'row'=2,'col'=4] {'col'}, dimensions={0}, use_global_device_ids=true | all-gather | bytes 10240 | tf_op jit(solution)/shard_map/all_gather | solution.py:13
  88.9 0.7 slice-done.1
  89.6 0.7 slice-done.5
  90.3 0.7 slice-done.4
  91.2 10.0 %while.112 = (s32[]{:T(128)}, f32[4096]{0:T(1024)S(1)}, f32[4096]{0:T(1024)S(1)}, f32[512]{0:T(512)S(1)}, f32[512]{0:T(512)S(1)}, /*index=5*/f32[4096]{0:T(1024)...) while((s32[]{:T(128)}, f32[4096]{0:T(1024)S(1)}, ...), condition=%wide.region_21.22_spmd, body=%wide.region_18.0_spmd.sunk | while | flops 35912708 | bytes 2252979 | solution.py:78
  101.2 1.8 all-gather.7
  103.0 1.8 all-gather.6
  104.9 12.0 %while.113 = (s32[]{:T(128)}, f32[64,4096]{1,0:T(8,128)S(1)}, f32[512]{0:T(512)S(1)}, f32[4096]{0:T(1024)S(1)}, f32[512]{0:T(512)S(1)}, /*index=5*/f32[4096]{0:T...) while((s32[]{:T(128)}, f32[64,4096]{1,0:T(8,128)S(1)}, ...), condition=%wide.region_23.24_spmd, body=%wide.region_22.23_spmd.sunk | while | flops 236748800 | bytes 2506939 | solution.py:95
  105.6 0.8 fusion.86
  107.1 0.8 fusion.86
  108.6 0.8 fusion.86
  110.1 0.8 fusion.86
  111.6 0.8 fusion.86
  113.1 0.8 fusion.86
  114.6 0.8 fusion.86
  116.1 0.8 fusion.86
  117.9 0.7 multiply_subtract_fusion.1
  118.6 54.8 %all-reduce.2.cloned.1.call-done = f32[64,4096]{1,0:T(8,128)} async-done(((f32[64,4096]{1,0:T(8,128)}), f32[64,4096]{1,0:T(8,128)}) %all-reduce.2.cloned.1.call-update) | async-done | bytes 1048592 | tf_op jit(solution)/shard_map/psum | solution.py:96
  173.4 2.3 %broadcast_multiply_fusion = f32[64,4096]{1,0:T(8,128)} fusion(f32[64,4096]{1,0:T(8,128)} %all-reduce.2.cloned.1.call-done), kind=kLoop, calls=%fused_computation.61 | loop fusion | flops 262144 | bytes 2097152 | tf_op jit(solution)/shard_map/div | solution.py:97
  (264 shorter events, 40.7 us)
Async XLA Ops:
  7.2 2.2 %copy-start.1 = (bf16[64,4096]{1,0:T(8,128)(2,1)S(1)}, bf16[64,4096]{1,0:T(8,128)(2,1)}, u32[]{:S(2)}) copy-start(bf16[64,4096]{1,0:T(8,128)(2,1)} %param.17) | copy-start | bytes 1572868
  7.2 166.2 %all-reduce.2.cloned.1.call-start = ((), (), s32[]{:S(2)}) async-start(), calls=%async_computation | async-start | bytes 2097152 | tf_op jit(solution)/shard_map/psum | solution.py:96
  8.2 1.2 copy-start.2
  29.3 0.6 copy-start.4
  41.8 0.7 slice-start.3
  42.5 0.7 slice-start.2
  75.8 0.6 copy-start.3
  88.3 0.6 copy-start.5
  88.9 0.7 slice-start.1
  89.6 0.7 slice-start.5
  90.3 0.7 slice-start.4
  90.3 0.7 slice-start
  116.9 0.6 copy-start.6
  116.9 1.0 copy-start
Sparse Core Ops, SparseCore 0:
  118.0 55.2 all-reduce.1
where the time goes:
time: 183 us; the launch traced here: 182 us
  blocking collectives  56.7 us (31%)
  waiting for transfers between devices  54.8 us (30%)
  matrix products  25.1 us (14%)
  local copies, waits for them, and re-layouts  18.8 us (10%)
  between operations  14.2 us (8%)
  other arithmetic  12 us (7%)
    all_gather x8, blocking collectives, combined_all(): pieces = jax.tree.map(lambda part: lax.all_gather(part, axis), value)  56.7 us
    psum x1, waiting for transfers between devices, shards(): summed = lax.psum(terms, ('atlas', 'row'))  54.8 us
    dot_general x40, matrix products, tile_cost(): lax.dot_general(points, piece, (((0,), (0,)), ((), ())), preferred_elemen...  18.7 us
    dot_general x8, matrix products, positions_visit(): jnp.dot(points_wide, plan, precision=lax.Precision.HIGHEST) * total_support  6.37 us
    dynamic_update_slice x16, local copies, waits for them, and re-layouts, column_visit(): lax.dynamic_update_slice_in_dim(top, peak, start, 0)  4.3 us
    dynamic_update_slice x16, local copies, waits for them, and re-layouts, column_visit(): lax.dynamic_update_slice_in_dim(total, mass, start, 0)  3.85 us
  transfers between devices with their start and end apart: 1, of which 1 were waited for; matrix products, arithmetic and copies ran while one was open for 0% of the time, Pallas kernels for 0%

commit v1 on v0

v1 whole, which is shorter than its diff:
```python
import functools
import math

import jax
import jax.numpy as jnp
from jax import lax
from jax.experimental import pallas as pl
from jax.experimental.pallas import tpu as pltpu
from jax.sharding import PartitionSpec as P


ITERS = 2
blur = 0.1
LANES = 128
SUBLANES = 8
LOG2E = 1.4426950408889634
VMEM = pl.BlockSpec(memory_space=pltpu.VMEM)


def pieces(value):
    high = value.astype(jnp.bfloat16)
    rest = value - high.astype(jnp.float32)
    mid = rest.astype(jnp.bfloat16)
    low = (rest - mid.astype(jnp.float32)).astype(jnp.bfloat16)
    return high, mid, low


def pad_rows(rows, count):
    width = rows[0].shape[1]
    index = lax.broadcasted_iota(jnp.int32, (16, width), 0)
    block = jnp.zeros((16, width), jnp.float32)
    for at, row in enumerate(rows):
        block = jnp.where(index == at, row.astype(jnp.float32), block)
    return block.astype(jnp.bfloat16)


def ones_rows(width):
    index = lax.broadcasted_iota(jnp.int32, (16, width), 0)
    return jnp.where(index < 3, 1.0, 0.0).astype(jnp.bfloat16)


def lane_tiles(width):
    return [slice(at, at + LANES) for at in range(0, width, LANES)]


def first_kernel(scale, x_ref, y_ref, out_ref, left, right, logits, tops, sums):
    dims, rows = x_ref.shape
    columns = y_ref.shape[1]
    block = min(512, columns)
    wide = x_ref[...].astype(jnp.float32) * (2.0 * scale)
    left[...] = jnp.concatenate([*pieces(wide), ones_rows(rows)], axis=0).T
    for start in range(0, columns, block):
        piece = y_ref[:, start : start + block]
        near = jnp.sum(jnp.square(piece.astype(jnp.float32)), axis=0, keepdims=True)
        right[:, start : start + block] = jnp.concatenate(
            [piece, piece, piece, pad_rows(pieces(-scale * near), 3)], axis=0
        )
    for start in range(0, columns, block):
        part = jnp.dot(
            left[...], right[:, start : start + block], preferred_element_type=jnp.float32
        )
        logits[:, start : start + block] = part
        top = functools.reduce(jnp.maximum, [part[:, tile] for tile in lane_tiles(block)])
        tops[...] = top if start == 0 else jnp.maximum(tops[...], top)
    height = min(64, rows)
    for low in range(0, rows, height):
        span = slice(low, low + height)
        top = tops[span, :]
        total = functools.reduce(
            jnp.add, [jnp.exp2(logits[span, tile] - top) for tile in lane_tiles(columns)]
        )
        sums[span, :] = total
    top = tops[...].T
    total = sums[...].T
    peak = jnp.max(top, axis=0, keepdims=True)
    mass = jnp.sum(total * jnp.exp2(top - peak), axis=0, keepdims=True)
    out_ref[...] = peak + jnp.log2(mass)


def second_kernel(scale, points, x_ref, phi_ref, y_ref, e_ref, r_ref, peak_ref, left, right, part_r):
    dims, cells = x_ref.shape
    columns = y_ref.shape[1]
    block = min(512, columns)
    wide = x_ref[...] * (2.0 * scale)
    left[...] = jnp.concatenate([*pieces(wide), pad_rows(pieces(phi_ref[...]), 3)], axis=0).T
    ones = ones_rows(columns)
    y = y_ref[...]
    right[...] = jnp.concatenate([y, y, y, ones], axis=0)
    for start in range(0, columns, block):
        span = slice(start, start + block)
        part = jnp.dot(left[...], right[:, span], preferred_element_type=jnp.float32)
        e_ref[:, span] = part
        peak = jnp.max(part, axis=0, keepdims=True)
        peak_ref[:, span] = peak
        expo = jnp.exp2(e_ref[:, span] - peak)
        e_ref[:, span] = expo
        total = jnp.sum(expo, axis=0, keepdims=True)
        weight = 1.0 / (points * total)
        share = e_ref[:, span] * weight
        row = functools.reduce(jnp.add, [share[:, tile] for tile in lane_tiles(block)])
        part_r[...] = row if start == 0 else part_r[...] + row
    r_ref[...] = jnp.sum(part_r[...].T, axis=0, keepdims=True)


def third_kernel(x_ref, w_ref, e_ref, out_ref, d_ref, tall):
    dims, cells = x_ref.shape
    columns = e_ref.shape[1]
    block = min(512, columns)
    rows = lax.broadcasted_iota(jnp.int32, (16, cells), 0)
    ones = jnp.where(rows == 0, 1.0, 0.0).astype(jnp.bfloat16)
    x = jnp.concatenate([x_ref[...].astype(jnp.bfloat16), ones], axis=0)
    tall[...] = jnp.broadcast_to(w_ref[...], (LANES, cells)).T
    for start in range(0, columns, block):
        parts = []
        for at in range(start, start + block, LANES):
            q = e_ref[:, at : at + LANES] * tall[...]
            parts.append(q)
        q = jnp.concatenate(parts, axis=1)
        high = q.astype(jnp.bfloat16)
        low = (q - high.astype(jnp.float32)).astype(jnp.bfloat16)
        moved = jnp.dot(x, high, preferred_element_type=jnp.float32)
        moved = moved + jnp.dot(x, low, preferred_element_type=jnp.float32)
        total = moved[dims : dims + 1, :]
        d_ref[:, start : start + block] = total
        out_ref[:, start : start + block] = moved[:dims, :] / total


def exchange(value, axis, size, key):
    return lax.ppermute(value, axis, [(at, at ^ key) for at in range(size)])


def partners(value, axis):
    size = lax.axis_size(axis)
    if size & (size - 1) == 0 and size <= 8:
        return [exchange(value, axis, size, key) for key in range(1, size)]
    return [
        lax.ppermute(value, axis, [(at, (at + key) % size) for at in range(size)])
        for key in range(1, size)
    ]


def shards(cells, support):
    own = cells[0]
    dims, rows = own.shape
    columns = support.shape[1]
    row_size = lax.axis_size("row")
    atlases = lax.axis_size("atlas")
    total_cells = rows * row_size
    total_support = columns * lax.axis_size("col")
    share = columns // row_size
    scale = LOG2E / (blur * dims)
    row_at = lax.axis_index("row")
    atlas_at = lax.axis_index("atlas")
    paired = row_size == 2

    def gather_rows(value):
        if paired:
            return jnp.concatenate([value, exchange(value, "row", 2, 1)], axis=-1)
        return lax.all_gather(value, "row", axis=value.ndim - 1, tiled=True)

    def sum_rows(value):
        if paired:
            other = exchange(value, "row", 2, 1)
            return value + jnp.concatenate([other[:, rows:], other[:, :rows]], axis=1)
        return lax.psum(value, "row")

    def own_rows(value):
        if paired:
            return value[:, :rows]
        return lax.dynamic_slice_in_dim(value, row_at * rows, rows, 1)

    everyone = gather_rows(own.astype(jnp.float32))
    mine = lax.dynamic_slice_in_dim(support, row_at * share, share, 1)
    depth = 3 * dims + 16

    lam = pl.pallas_call(
        functools.partial(first_kernel, scale),
        out_shape=jax.ShapeDtypeStruct((1, rows), jnp.float32),
        in_specs=[VMEM, VMEM],
        out_specs=VMEM,
        scratch_shapes=[
            pltpu.VMEM((rows, depth), jnp.bfloat16),
            pltpu.VMEM((depth, columns), jnp.bfloat16),
            pltpu.VMEM((rows, columns), jnp.float32),
            pltpu.VMEM((rows, LANES), jnp.float32),
            pltpu.VMEM((rows, LANES), jnp.float32),
        ],
        compiler_params=pltpu.CompilerParams(vmem_limit_bytes=24 << 20),
        name="first",
    )(own, support)

    others = partners(lam, "col")
    peak = functools.reduce(jnp.maximum, others, lam)
    mass = functools.reduce(jnp.add, [jnp.exp2(one - peak) for one in [lam, *others]])
    phi = -math.log2(total_cells) - (peak + jnp.log2(mass))

    e, r, tops = pl.pallas_call(
        functools.partial(second_kernel, scale, float(total_support)),
        out_shape=(
            jax.ShapeDtypeStruct((total_cells, share), jnp.float32),
            jax.ShapeDtypeStruct((1, total_cells), jnp.float32),
            jax.ShapeDtypeStruct((1, share), jnp.float32),
        ),
        in_specs=[VMEM, VMEM, VMEM],
        out_specs=(VMEM, VMEM, VMEM),
        scratch_shapes=[
            pltpu.VMEM((total_cells, depth), jnp.bfloat16),
            pltpu.VMEM((depth, share), jnp.bfloat16),
            pltpu.VMEM((total_cells, LANES), jnp.float32),
        ],
        compiler_params=pltpu.CompilerParams(vmem_limit_bytes=32 << 20),
        name="second",
    )(everyone, gather_rows(phi), mine)

    r = sum_rows(r)
    r = functools.reduce(jnp.add, partners(r, "col"), r) * total_cells
    far = jnp.sum(jnp.square(own.astype(jnp.float32)), axis=0)[None, :]
    cell_dual = (blur / LOG2E) * (phi + scale * far - jnp.log2(own_rows(r)))

    moved, mass = pl.pallas_call(
        third_kernel,
        out_shape=(
            jax.ShapeDtypeStruct((dims, share), jnp.float32),
            jax.ShapeDtypeStruct((1, share), jnp.float32),
        ),
        in_specs=[VMEM, VMEM, VMEM],
        out_specs=(VMEM, VMEM),
        scratch_shapes=[pltpu.VMEM((total_cells, LANES), jnp.float32)],
        compiler_params=pltpu.CompilerParams(vmem_limit_bytes=24 << 20),
        name="third",
    )(everyone, 1.0 / r, e)

    near = jnp.sum(jnp.square(mine.astype(jnp.float32)), axis=0)[None, :]
    dual_g = (blur / LOG2E) * (scale * near - math.log2(total_support) - tops - jnp.log2(mass))

    piece = share // atlases
    if atlases & (atlases - 1) == 0 and atlases <= 8 and piece % LANES == 0:
        def slab(key):
            return lax.dynamic_slice_in_dim(moved, (atlas_at ^ key) * piece, piece, 1)

        sums = slab(0)
        arrived = [exchange(slab(key), "atlas", atlases, key) for key in range(1, atlases)]
        sums = functools.reduce(jnp.add, arrived, sums) * (1.0 / atlases)
        gathered = [sums, *partners(sums, "atlas")]

        def slot(at):
            chosen = gathered[0]
            for key in range(1, atlases):
                chosen = jnp.where(atlas_at ^ key == at, gathered[key], chosen)
            return chosen

        updated = jnp.concatenate([slot(at) for at in range(atlases)], axis=1)
    else:
        updated = lax.psum(moved, "atlas") * (1.0 / atlases)

    def in_order(value):
        if paired:
            other = exchange(value, "row", 2, 1)
            first = jnp.where(row_at == 0, value, other)
            last = jnp.where(row_at == 0, other, value)
            return jnp.concatenate([first, last], axis=1)
        return lax.all_gather(value, "row", axis=1, tiled=True)

    return (cell_dual, in_order(dual_g), in_order(updated))


def solution(mesh):
    in_specs = (P("atlas", None, "row"), P(None, "col"))
    out_specs = (P("atlas", "row"), P("atlas", "col"), P(None, "col"))
    return jax.shard_map(shards, mesh=mesh, in_specs=in_specs, out_specs=out_specs, check_vma=False)
```

time: 183 us -> 55.3 us (0.30)
  blocking collectives: 56.7 us -> 0 us
  waiting for transfers between devices: 54.8 us -> 15.9 us
  matrix products: 25.1 us -> 0 us
  starting transfers between devices: 0.04 us -> 17.8 us
  between operations: 14.2 us -> 0.81 us
  local copies, waits for them, and re-layouts: 18.8 us -> 8.53 us
  other arithmetic: 12 us -> 4.54 us
  Pallas kernels: 0 us -> 7.31 us
    all_gather x8 -> x0, blocking collectives: 56.7 us -> none  [combined_all(): pieces = jax.tree.map(lambda part: lax.all_gather(part, axis), value)]
    psum x1 -> x0, waiting for transfers between devices: 54.8 us -> none  [shards(): summed = lax.psum(terms, ('atlas', 'row'))]
    dot_general x48 -> x0, matrix products: 25.1 us -> none  [the longest x40 18.7 us: tile_cost(): lax.dot_general(points, piece, (((0,), (0,)), ((), ())), preferred_elemen...]
    ppermute x0 -> x17, starting transfers between devices: none -> 17.8 us  [exchange(): return lax.ppermute(value, axis, [(at, at ^ key) for at in range(size)])]
    ppermute x0 -> x17, waiting for transfers between devices: none -> 15.9 us  [exchange(): return lax.ppermute(value, axis, [(at, at ^ key) for at in range(size)])]
    dynamic_update_slice x32 -> x0, local copies, waits for them, and re-layouts: 8.15 us -> none  [the longest x16 4.3 us: column_visit(): lax.dynamic_update_slice_in_dim(top, peak, start, 0)]
    pallas_call x0 -> x3, Pallas kernels: none -> 7.31 us  [the longest x1 2.95 us: shards(): pl.pallas_call(functools.partial(second_kernel, scale, float(total_suppor...]
    reduce_sum x34 -> x2, other arithmetic: 8.43 us -> 1.9 us  [the longest x1 1.02 us: shards(): near = jnp.sum(jnp.square(mine.astype(jnp.float32)), axis=0)[None, :]]
  transfers between devices with their start and end apart: 1 -> 17, of which waited for: 1 -> 12; matrix products, arithmetic and copies ran while one was open for 0% -> 6% of each run, Pallas kernels for 0% -> 0%
where the time goes in v1:
time: 55.3 us; the launch traced here: 54.9 us
  starting transfers between devices  17.8 us (32%)
  waiting for transfers between devices  15.9 us (29%)
  local copies, waits for them, and re-layouts  8.53 us (15%)
  Pallas kernels  7.31 us (13%)
  other arithmetic  4.54 us (8%)
  between operations  0.81 us (1%)
    ppermute x17, starting transfers between devices, exchange(): return lax.ppermute(value, axis, [(at, at ^ key) for at in range(size)])  17.8 us
    ppermute x17, waiting for transfers between devices, exchange(): return lax.ppermute(value, axis, [(at, at ^ key) for at in range(size)])  15.9 us
    unnamed x8, local copies, waits for them, and re-layouts  8.49 us
    pallas_call x1, Pallas kernels, shards(): pl.pallas_call(functools.partial(second_kernel, scale, float(total_suppor...  2.95 us
    pallas_call x1, Pallas kernels, shards(): pl.pallas_call(functools.partial(first_kernel, scale), out_shape=jax.Shap...  2.42 us
    pallas_call x1, Pallas kernels, shards(): pl.pallas_call(third_kernel, out_shape=(jax.ShapeDtypeStruct((dims, share...  1.94 us
    concatenate x2, other arithmetic, in_order(): return jnp.concatenate([first, last], axis=1)  1.67 us
  transfers between devices with their start and end apart: 17, of which 12 were waited for; matrix products, arithmetic and copies ran while one was open for 6% of the time, Pallas kernels for 0%

profile of v1, /device:TPU:0, one launch (start us, length us, event | category | flops | bytes accessed | tf_op | source)
XLA Modules:
  0.0 54.9 jit_solution(11555822583026478980)
XLA Ops:
  0.6 1.0 %copy-done.2 = bf16[64,4096]{1,0:T(8,128)(2,1)S(1)} copy-done((bf16[64,4096]{1,0:T(8,128)(2,1)S(1)}, bf16[64,4096]{1,0:T(8,128)(2,1)}, u32[]{:S(2)}) %copy-start.2) | copy-done | bytes 524312
  1.7 0.8 %copy-done.3 = bf16[1,64,512]{2,1,0:T(8,128)(2,1)S(1)} copy-done((bf16[1,64,512]{2,1,0:T(8,128)(2,1)S(1)}, bf16[1,64,512]{2,1,0:T(8,128)(2,1)}, u32[]{:S(2)}) %copy-start.3) | copy-done | bytes 65560
  2.5 2.4 %first.1 = f32[1,512]{1,0:T(1,128)S(1)} custom-call(bf16[64,512]{1,0:T(8,128)(2,1)S(1)} %bitcast.5, bf16[64,4096]{1,0:T(8,128)(2,1)S(1)} %copy-done.2), custom_call_target="tpu_custom_call" | custom-call | tf_op jit(solution)/shard_map/first/pallas_call | solution.py:176
  4.9 5.1 %collective-permute-start.2 = (f32[1,512]{1,0:T(1,128)S(1)}, f32[1,512]{1,0:T(1,128)S(1)}, u32[]{:S(2)}, u32[]{:S(2)}) collective-permute-start(f32[1,512]{1,0:T(1,128)S(1)} %first.1), channel_id=1, source_target_pairs={{0,3},{1,2},{2,1},{3,0},{4,7},{5,6},{6,5},{7,4},{8,11},{9,10},{10,... | collective-permute-start | bytes 6152 | tf_op jit(solution)/shard_map/ppermute | solution.py:129
  10.1 0.6 %collective-permute-start = (f32[1,512]{1,0:T(1,128)S(1)}, f32[1,512]{1,0:T(1,128)S(1)}, u32[]{:S(2)}, u32[]{:S(2)}) collective-permute-start(f32[1,512]{1,0:T(1,128)S(1)} %first.1), channel_id=1, source_target_pairs={{0,1},{1,0},{2,3},{3,2},{4,5},{5,4},{6,7},{7,6},{8,9},{9,8},{10,11... | collective-permute-start | bytes 6152 | tf_op jit(solution)/shard_map/ppermute | solution.py:129
  10.8 1.0 %multiply_reduce_fusion = (f32[2048]{0:T(1024)S(1)}, bf16[64,2048]{1,0:T(8,128)(2,1)S(1)}) fusion(bf16[64,4096]{1,0:T(8,128)(2,1)} %y_ref.1, s32[]{:T(128)S(6)} %select_n.113), kind=kLoop, calls=%fused_computation.2 | loop fusion | flops 391168 | bytes 532484 | tf_op jit(solution)/shard_map/reduce_sum | solution.py:233
  11.9 2.7 %collective-permute-done.1 = f32[1,512]{1,0:T(1,128)S(1)} collective-permute-done((f32[1,512]{1,0:T(1,128)S(1)}, f32[1,512]{1,0:T(1,128)S(1)}, u32[]{:S(2)}, u32[]{:S(2)}) %collective-permute-start.1) | collective-permute-done | bytes 2080 | tf_op jit(solution)/shard_map/ppermute | solution.py:129
  14.7 1.1 %collective-permute-done.4 = f32[1,512]{1,0:T(1,128)S(1)} collective-permute-done((f32[1,512]{1,0:T(1,128)S(1)}, f32[1,512]{1,0:T(1,128)S(1)}, u32[]{:S(2)}, u32[]{:S(2)}) %collective-permute-start.4) | collective-permute-done | bytes 2080 | tf_op jit(solution)/shard_map/ppermute | solution.py:129
  15.9 3.0 %second.1 = (f32[1024,2048]{1,0:T(8,128)S(1)}, f32[1,1024]{1,0:T(1,128)S(1)}, f32[1,2048]{1,0:T(1,128)S(1)}) custom-call(f32[64,1024]{1,0:T(8,128)S(1)} %pad_maximum_fusion.2.x_ref, f32[1,1024]{1,0:T(1,128)S(1)} %pad_maximum_fusion.4.phi_ref, bf16[64,2048]{1,0:T(8,128)(2,1)S(1)} %get-tuple-element.14.y_ref), custom_call_target="tpu_custom_call" | custom-call | tf_op jit(solution)/shard_map/second/pallas_call | solution.py:197
  18.8 3.2 %copy-done = f32[1024,2048]{1,0:T(8,128)} copy-done((f32[1024,2048]{1,0:T(8,128)}, f32[1024,2048]{1,0:T(8,128)S(1)}, u32[]{:S(2)}) %copy-start) | copy-done | bytes 8388632
  22.3 0.9 %multiply_reduce_fusion.1 = f32[512]{0:T(512)S(1)} fusion(bf16[1,64,512]{2,1,0:T(8,128)(2,1)} %param.2), kind=kLoop, calls=%fused_computation.11 | loop fusion | flops 97792 | bytes 67584 | tf_op jit(solution)/shard_map/reduce_sum | solution.py:217
  23.3 1.5 %collective-permute-start.8 = (f32[1,1024]{1,0:T(1,128)S(1)}, f32[1,1024]{1,0:T(1,128)S(1)}, u32[]{:S(2)}, u32[]{:S(2)}) collective-permute-start(f32[1,1024]{1,0:T(1,128)S(1)} %maximum_add_fusion), channel_id=1, source_target_pairs={{0,3},{1,2},{2,1},{3,0},{4,7},{5,6},{6,5},{7,4},{8,11},{9,10},{10,... | collective-permute-start | bytes 12296 | tf_op jit(solution)/shard_map/ppermute | solution.py:129
  24.8 0.6 %collective-permute-start.7 = (f32[1,1024]{1,0:T(1,128)S(1)}, f32[1,1024]{1,0:T(1,128)S(1)}, u32[]{:S(2)}, u32[]{:S(2)}) collective-permute-start(f32[1,1024]{1,0:T(1,128)S(1)} %maximum_add_fusion), channel_id=1, source_target_pairs={{0,2},{1,3},{2,0},{3,1},{4,6},{5,7},{6,4},{7,5},{8,10},{9,11},{10,... | collective-permute-start | bytes 12296 | tf_op jit(solution)/shard_map/ppermute | solution.py:129
  25.4 2.3 %collective-permute-start.6 = (f32[1,1024]{1,0:T(1,128)S(1)}, f32[1,1024]{1,0:T(1,128)S(1)}, u32[]{:S(2)}, u32[]{:S(2)}) collective-permute-start(f32[1,1024]{1,0:T(1,128)S(1)} %maximum_add_fusion), channel_id=1, source_target_pairs={{0,1},{1,0},{2,3},{3,2},{4,5},{5,4},{6,7},{7,6},{8,9},{9,8},{10,11... | collective-permute-start | bytes 12296 | tf_op jit(solution)/shard_map/ppermute | solution.py:129
  27.7 1.0 %collective-permute-done.8 = f32[1,1024]{1,0:T(1,128)S(1)} collective-permute-done((f32[1,1024]{1,0:T(1,128)S(1)}, f32[1,1024]{1,0:T(1,128)S(1)}, u32[]{:S(2)}, u32[]{:S(2)}) %collective-permute-start.8) | collective-permute-done | bytes 4128 | tf_op jit(solution)/shard_map/ppermute | solution.py:129
  28.7 0.5 collective-permute-done.7
  29.4 3.4 %copy-done.1 = f32[1024,2048]{1,0:T(8,128)S(1)} copy-done((f32[1024,2048]{1,0:T(8,128)S(1)}, f32[1024,2048]{1,0:T(8,128)}, u32[]{:S(2)}) %copy-start.1) | copy-done | bytes 8388632
  32.7 1.9 %third.1 = (f32[64,2048]{1,0:T(8,128)S(1)}, f32[1,2048]{1,0:T(1,128)S(1)}) custom-call(f32[64,1024]{1,0:T(8,128)S(1)} %pad_maximum_fusion.2.x_ref, f32[1,1024]{1,0:T(1,128)S(1)} %get-tuple-element.15.w_ref, f32[1024,2048]{1,0:T(8,128)S(1)} %copy-done.1), custom_call_target="tpu_custom_call" | custom-call | tf_op jit(solution)/shard_map/third/pallas_call | solution.py:220
  34.7 2.5 %collective-permute-start.12 = (f32[64,512]{1,0:T(8,128)S(1)}, f32[64,512]{1,0:T(8,128)S(1)}, u32[]{:S(2)}, u32[]{:S(2)}) collective-permute-start(f32[64,512]{1,0:T(8,128)S(1)} %get-tuple-element.24), channel_id=1, source_target_pairs={{0,24},{8,16},{16,8},{24,0},{1,25},{9,17},{17,9},{25,1},{2,26},{10... | collective-permute-start | bytes 393224 | tf_op jit(solution)/shard_map/ppermute | solution.py:129
  37.2 0.5 collective-permute-start.11
  37.7 0.5 collective-permute-start.10
  38.4 3.1 %collective-permute-done.12 = f32[64,512]{1,0:T(8,128)S(1)} collective-permute-done((f32[64,512]{1,0:T(8,128)S(1)}, f32[64,512]{1,0:T(8,128)S(1)}, u32[]{:S(2)}, u32[]{:S(2)}) %collective-permute-start.12) | collective-permute-done | bytes 131104 | tf_op jit(solution)/shard_map/ppermute | solution.py:129
  41.5 1.5 %collective-permute-done.11 = f32[64,512]{1,0:T(8,128)S(1)} collective-permute-done((f32[64,512]{1,0:T(8,128)S(1)}, f32[64,512]{1,0:T(8,128)S(1)}, u32[]{:S(2)}, u32[]{:S(2)}) %collective-permute-start.11) | collective-permute-done | bytes 131104 | tf_op jit(solution)/shard_map/ppermute | solution.py:129
  43.1 1.7 %collective-permute-start.13 = (f32[64,512]{1,0:T(8,128)S(1)}, f32[64,512]{1,0:T(8,128)S(1)}, u32[]{:S(2)}, u32[]{:S(2)}) collective-permute-start(f32[64,512]{1,0:T(8,128)S(1)} %add_multiply_fusion), channel_id=1, source_target_pairs={{0,24},{8,16},{16,8},{24,0},{1,25},{9,17},{17,9},{25,1},{2,26},{10... | collective-permute-start | bytes 393224 | tf_op jit(solution)/shard_map/ppermute | solution.py:129
  44.9 1.3 %collective-permute-start.14 = (f32[64,512]{1,0:T(8,128)S(1)}, f32[64,512]{1,0:T(8,128)S(1)}, u32[]{:S(2)}, u32[]{:S(2)}) collective-permute-start(f32[64,512]{1,0:T(8,128)S(1)} %add_multiply_fusion), channel_id=1, source_target_pairs={{0,16},{8,24},{16,0},{24,8},{1,17},{9,25},{17,1},{25,9},{2,18},{10... | collective-permute-start | bytes 393224 | tf_op jit(solution)/shard_map/ppermute | solution.py:129
  46.1 0.6 %collective-permute-start.15 = (f32[64,512]{1,0:T(8,128)S(1)}, f32[64,512]{1,0:T(8,128)S(1)}, u32[]{:S(2)}, u32[]{:S(2)}) collective-permute-start(f32[64,512]{1,0:T(8,128)S(1)} %add_multiply_fusion), channel_id=1, source_target_pairs={{0,8},{8,0},{16,24},{24,16},{1,9},{9,1},{17,25},{25,17},{2,10},{10... | collective-permute-start | bytes 393224 | tf_op jit(solution)/shard_map/ppermute | solution.py:129
  46.7 0.6 %fusion.2 = f32[1,512]{1,0:T(1,128)} fusion(f32[1,1024]{1,0:T(1,128)S(1)} %get-tuple-element.16, f32[1,512]{1,0:T(1,128)S(1)} %add_subtract_fusion, f32[1,512]{1,0:T(1,128)S(1)} %bitcast.7), kind=kLoop, calls=%fused_computation.25 | loop fusion | flops 2048 | bytes 8192 | tf_op jit(solution)/shard_map/mul | solution.py:218
  47.3 2.7 %collective-permute-done.13 = f32[64,512]{1,0:T(8,128)S(1)} collective-permute-done((f32[64,512]{1,0:T(8,128)S(1)}, f32[64,512]{1,0:T(8,128)S(1)}, u32[]{:S(2)}, u32[]{:S(2)}) %collective-permute-start.13) | collective-permute-done | bytes 131104 | tf_op jit(solution)/shard_map/ppermute | solution.py:129
  50.0 1.3 %collective-permute-done.14 = f32[64,512]{1,0:T(8,128)S(1)} collective-permute-done((f32[64,512]{1,0:T(8,128)S(1)}, f32[64,512]{1,0:T(8,128)S(1)}, u32[]{:S(2)}, u32[]{:S(2)}) %collective-permute-start.14) | collective-permute-done | bytes 131104 | tf_op jit(solution)/shard_map/ppermute | solution.py:129
  51.9 0.6 %pad_maximum_fusion.3 = f32[1,4096]{1,0:T(1,128)} fusion(f32[1,2048]{1,0:T(1,128)S(1)} %get-tuple-element.27, f32[1,2048]{1,0:T(1,128)S(1)} %get-tuple-element.26), kind=kLoop, calls=%fused_computation.12 | loop fusion | flops 4096 | bytes 32768 | tf_op jit(solution)/shard_map/concatenate | solution.py:261
  52.5 1.2 %collective-permute-done.16 = f32[64,2048]{1,0:T(8,128)S(1)} collective-permute-done((f32[64,2048]{1,0:T(8,128)S(1)}, f32[64,2048]{1,0:T(8,128)S(1)}, u32[]{:S(2)}, u32[]{:S(2)}) %collective-permute-start.16) | collective-permute-done | bytes 524320 | tf_op jit(solution)/shard_map/ppermute | solution.py:129
  53.9 1.0 %pad_maximum_fusion = f32[64,4096]{1,0:T(8,128)} fusion(f32[64,2048]{1,0:T(8,128)S(1)} %get-tuple-element.18, f32[64,2048]{1,0:T(8,128)S(1)} %get-tuple-element.17), kind=kLoop, calls=%fused_computation | loop fusion | flops 262144 | bytes 2097152 | tf_op jit(solution)/shard_map/concatenate | solution.py:261
  (34 shorter events, 1.5 us)
Async XLA Ops:
  0.6 1.0 %copy-start.2 = (bf16[64,4096]{1,0:T(8,128)(2,1)S(1)}, bf16[64,4096]{1,0:T(8,128)(2,1)}, u32[]{:S(2)}) copy-start(bf16[64,4096]{1,0:T(8,128)(2,1)} %y_ref.1) | copy-start | bytes 1572868
  1.7 0.8 %copy-start.3 = (bf16[1,64,512]{2,1,0:T(8,128)(2,1)S(1)}, bf16[1,64,512]{2,1,0:T(8,128)(2,1)}, u32[]{:S(2)}) copy-start(bf16[1,64,512]{2,1,0:T(8,128)(2,1)} %param.2) | copy-start | bytes 196612
  4.9 6.9 %collective-permute-start.2 = (f32[1,512]{1,0:T(1,128)S(1)}, f32[1,512]{1,0:T(1,128)S(1)}, u32[]{:S(2)}, u32[]{:S(2)}) collective-permute-start(f32[1,512]{1,0:T(1,128)S(1)} %first.1), channel_id=1, source_target_pairs={{0,3},{1,2},{2,1},{3,0},{4,7},{5,6},{6,5},{7,4},{8,11},{9,10},{10,... | collective-permute-start | bytes 6152 | tf_op jit(solution)/shard_map/ppermute | solution.py:129
  10.1 4.5 %collective-permute-start.1 = (f32[1,512]{1,0:T(1,128)S(1)}, f32[1,512]{1,0:T(1,128)S(1)}, u32[]{:S(2)}, u32[]{:S(2)}) collective-permute-start(f32[1,512]{1,0:T(1,128)S(1)} %first.1), channel_id=1, source_target_pairs={{0,2},{1,3},{2,0},{3,1},{4,6},{5,7},{6,4},{7,5},{8,10},{9,11},{10,... | collective-permute-start | bytes 6152 | tf_op jit(solution)/shard_map/ppermute | solution.py:129
  10.1 4.5 %collective-permute-start = (f32[1,512]{1,0:T(1,128)S(1)}, f32[1,512]{1,0:T(1,128)S(1)}, u32[]{:S(2)}, u32[]{:S(2)}) collective-permute-start(f32[1,512]{1,0:T(1,128)S(1)} %first.1), channel_id=1, source_target_pairs={{0,1},{1,0},{2,3},{3,2},{4,5},{5,4},{6,7},{7,6},{8,9},{9,8},{10,11... | collective-permute-start | bytes 6152 | tf_op jit(solution)/shard_map/ppermute | solution.py:129
  10.7 5.1 %collective-permute-start.3 = (f32[64,512]{1,0:T(8,128)S(1)}, f32[64,512]{1,0:T(8,128)S(1)}, u32[]{:S(2)}, u32[]{:S(2)}) collective-permute-start(f32[64,512]{1,0:T(8,128)S(1)} %bitcast_convert_fusion), channel_id=1, source_target_pairs={{0,4},{4,0},{1,5},{5,1},{2,6},{6,2},{3,7},{7,3},{8,12},{12,8},{9,1... | collective-permute-start | bytes 393224 | tf_op jit(solution)/shard_map/ppermute | solution.py:129
  14.6 1.2 %collective-permute-start.4 = (f32[1,512]{1,0:T(1,128)S(1)}, f32[1,512]{1,0:T(1,128)S(1)}, u32[]{:S(2)}, u32[]{:S(2)}) collective-permute-start(f32[1,512]{1,0:T(1,128)S(1)} %add_subtract_fusion), channel_id=1, source_target_pairs={{0,4},{4,0},{1,5},{5,1},{2,6},{6,2},{3,7},{7,3},{8,12},{12,8},{9,1... | collective-permute-start | bytes 6152 | tf_op jit(solution)/shard_map/ppermute | solution.py:129
  18.8 3.3 %copy-start = (f32[1024,2048]{1,0:T(8,128)}, f32[1024,2048]{1,0:T(8,128)S(1)}, u32[]{:S(2)}) copy-start(f32[1024,2048]{1,0:T(8,128)S(1)} %get-tuple-element.10.e_ref) | copy-start | bytes 25165828
  22.1 1.2 %collective-permute-start.5 = (f32[1,1024]{1,0:T(1,128)S(1)}, f32[1,1024]{1,0:T(1,128)S(1)}, u32[]{:S(2)}, u32[]{:S(2)}) collective-permute-start(f32[1,1024]{1,0:T(1,128)S(1)} %get-tuple-element.8), channel_id=1, source_target_pairs={{0,4},{4,0},{1,5},{5,1},{2,6},{6,2},{3,7},{7,3},{8,12},{12,8},{9,1... | collective-permute-start | bytes 12296 | tf_op jit(solution)/shard_map/ppermute | solution.py:129
  23.3 5.5 %collective-permute-start.8 = (f32[1,1024]{1,0:T(1,128)S(1)}, f32[1,1024]{1,0:T(1,128)S(1)}, u32[]{:S(2)}, u32[]{:S(2)}) collective-permute-start(f32[1,1024]{1,0:T(1,128)S(1)} %maximum_add_fusion), channel_id=1, source_target_pairs={{0,3},{1,2},{2,1},{3,0},{4,7},{5,6},{6,5},{7,4},{8,11},{9,10},{10,... | collective-permute-start | bytes 12296 | tf_op jit(solution)/shard_map/ppermute | solution.py:129
  24.8 4.5 %collective-permute-start.7 = (f32[1,1024]{1,0:T(1,128)S(1)}, f32[1,1024]{1,0:T(1,128)S(1)}, u32[]{:S(2)}, u32[]{:S(2)}) collective-permute-start(f32[1,1024]{1,0:T(1,128)S(1)} %maximum_add_fusion), channel_id=1, source_target_pairs={{0,2},{1,3},{2,0},{3,1},{4,6},{5,7},{6,4},{7,5},{8,10},{9,11},{10,... | collective-permute-start | bytes 12296 | tf_op jit(solution)/shard_map/ppermute | solution.py:129
  25.4 3.9 %collective-permute-start.6 = (f32[1,1024]{1,0:T(1,128)S(1)}, f32[1,1024]{1,0:T(1,128)S(1)}, u32[]{:S(2)}, u32[]{:S(2)}) collective-permute-start(f32[1,1024]{1,0:T(1,128)S(1)} %maximum_add_fusion), channel_id=1, source_target_pairs={{0,1},{1,0},{2,3},{3,2},{4,5},{5,4},{6,7},{7,6},{8,9},{9,8},{10,11... | collective-permute-start | bytes 12296 | tf_op jit(solution)/shard_map/ppermute | solution.py:129
  29.3 3.4 %copy-start.1 = (f32[1024,2048]{1,0:T(8,128)S(1)}, f32[1024,2048]{1,0:T(8,128)}, u32[]{:S(2)}) copy-start(f32[1024,2048]{1,0:T(8,128)} %copy-done) | copy-start | bytes 25165828
  34.7 6.8 %collective-permute-start.12 = (f32[64,512]{1,0:T(8,128)S(1)}, f32[64,512]{1,0:T(8,128)S(1)}, u32[]{:S(2)}, u32[]{:S(2)}) collective-permute-start(f32[64,512]{1,0:T(8,128)S(1)} %get-tuple-element.24), channel_id=1, source_target_pairs={{0,24},{8,16},{16,8},{24,0},{1,25},{9,17},{17,9},{25,1},{2,26},{10... | collective-permute-start | bytes 393224 | tf_op jit(solution)/shard_map/ppermute | solution.py:129
  37.2 5.8 %collective-permute-start.11 = (f32[64,512]{1,0:T(8,128)S(1)}, f32[64,512]{1,0:T(8,128)S(1)}, u32[]{:S(2)}, u32[]{:S(2)}) collective-permute-start(f32[64,512]{1,0:T(8,128)S(1)} %get-tuple-element.25), channel_id=1, source_target_pairs={{0,16},{8,24},{16,0},{24,8},{1,17},{9,25},{17,1},{25,9},{2,18},{10... | collective-permute-start | bytes 393224 | tf_op jit(solution)/shard_map/ppermute | solution.py:129
  37.7 5.3 %collective-permute-start.10 = (f32[64,512]{1,0:T(8,128)S(1)}, f32[64,512]{1,0:T(8,128)S(1)}, u32[]{:S(2)}, u32[]{:S(2)}) collective-permute-start(f32[64,512]{1,0:T(8,128)S(1)} %get-tuple-element.23), channel_id=1, source_target_pairs={{0,8},{8,0},{16,24},{24,16},{1,9},{9,1},{17,25},{25,17},{2,10},{10... | collective-permute-start | bytes 393224 | tf_op jit(solution)/shard_map/ppermute | solution.py:129
  38.3 13.6 %collective-permute-start.9 = (f32[1,2048]{1,0:T(1,128)S(1)}, f32[1,2048]{1,0:T(1,128)S(1)}, u32[]{:S(2)}, u32[]{:S(2)}) collective-permute-start(f32[1,2048]{1,0:T(1,128)S(1)} %subtract_multiply_fusion), channel_id=1, source_target_pairs={{0,4},{4,0},{1,5},{5,1},{2,6},{6,2},{3,7},{7,3},{8,12},{12,8},{9,1... | collective-permute-start | bytes 24584 | tf_op jit(solution)/shard_map/ppermute | solution.py:129
  43.1 6.9 %collective-permute-start.13 = (f32[64,512]{1,0:T(8,128)S(1)}, f32[64,512]{1,0:T(8,128)S(1)}, u32[]{:S(2)}, u32[]{:S(2)}) collective-permute-start(f32[64,512]{1,0:T(8,128)S(1)} %add_multiply_fusion), channel_id=1, source_target_pairs={{0,24},{8,16},{16,8},{24,0},{1,25},{9,17},{17,9},{25,1},{2,26},{10... | collective-permute-start | bytes 393224 | tf_op jit(solution)/shard_map/ppermute | solution.py:129
  44.9 6.5 %collective-permute-start.14 = (f32[64,512]{1,0:T(8,128)S(1)}, f32[64,512]{1,0:T(8,128)S(1)}, u32[]{:S(2)}, u32[]{:S(2)}) collective-permute-start(f32[64,512]{1,0:T(8,128)S(1)} %add_multiply_fusion), channel_id=1, source_target_pairs={{0,16},{8,24},{16,0},{24,8},{1,17},{9,25},{17,1},{25,9},{2,18},{10... | collective-permute-start | bytes 393224 | tf_op jit(solution)/shard_map/ppermute | solution.py:129
  46.1 5.5 %collective-permute-start.15 = (f32[64,512]{1,0:T(8,128)S(1)}, f32[64,512]{1,0:T(8,128)S(1)}, u32[]{:S(2)}, u32[]{:S(2)}) collective-permute-start(f32[64,512]{1,0:T(8,128)S(1)} %add_multiply_fusion), channel_id=1, source_target_pairs={{0,8},{8,0},{16,24},{24,16},{1,9},{9,1},{17,25},{25,17},{2,10},{10... | collective-permute-start | bytes 393224 | tf_op jit(solution)/shard_map/ppermute | solution.py:129
  51.8 2.0 %collective-permute-start.16 = (f32[64,2048]{1,0:T(8,128)S(1)}, f32[64,2048]{1,0:T(8,128)S(1)}, u32[]{:S(2)}, u32[]{:S(2)}) collective-permute-start(f32[64,2048]{1,0:T(8,128)S(1)} %pad_maximum_fusion.1), channel_id=1, source_target_pairs={{0,4},{4,0},{1,5},{5,1},{2,6},{6,2},{3,7},{7,3},{8,12},{12,8},{9,1... | collective-permute-start | bytes 1572872 | tf_op jit(solution)/shard_map/ppermute | solution.py:129

commit v2 on v1

v2 whole, which is shorter than its diff:
```python
import functools
import math

import jax
import jax.numpy as jnp
from jax import lax
from jax.experimental import pallas as pl
from jax.experimental.pallas import tpu as pltpu
from jax.sharding import PartitionSpec as P


ITERS = 2
blur = 0.1
LANES = 128
SUBLANES = 8
LOG2E = 1.4426950408889634
VMEM = pl.BlockSpec(memory_space=pltpu.VMEM)


def pieces(value):
    high = value.astype(jnp.bfloat16)
    rest = value - high.astype(jnp.float32)
    mid = rest.astype(jnp.bfloat16)
    low = (rest - mid.astype(jnp.float32)).astype(jnp.bfloat16)
    return high, mid, low


def pad_rows(rows):
    width = rows[0].shape[1]
    index = lax.broadcasted_iota(jnp.int32, (16, width), 0)
    block = jnp.zeros((16, width), jnp.float32)
    for at, row in enumerate(rows):
        block = jnp.where(index == at, row.astype(jnp.float32), block)
    return block.astype(jnp.bfloat16)


def ones_rows(width):
    index = lax.broadcasted_iota(jnp.int32, (16, width), 0)
    return jnp.where(index < 3, 1.0, 0.0).astype(jnp.bfloat16)


def lane_tiles(width):
    return [slice(at, at + LANES) for at in range(0, width, LANES)]


def first_kernel(scale, x_ref, y_ref, out_ref, far_ref, left, right, logits, tops, sums):
    dims, rows = x_ref.shape
    columns = y_ref.shape[1]
    block = min(512, columns)
    x = x_ref[...].astype(jnp.float32)
    far_ref[...] = scale * jnp.sum(jnp.square(x), axis=0, keepdims=True)
    left[...] = jnp.concatenate([*pieces(x * (2.0 * scale)), ones_rows(rows)], axis=0).T
    for start in range(0, columns, block):
        piece = y_ref[:, start : start + block]
        near = jnp.sum(jnp.square(piece.astype(jnp.float32)), axis=0, keepdims=True)
        right[:, start : start + block] = jnp.concatenate(
            [piece, piece, piece, pad_rows(pieces(-scale * near))], axis=0
        )
    for start in range(0, columns, block):
        part = jnp.dot(
            left[...], right[:, start : start + block], preferred_element_type=jnp.float32
        )
        logits[:, start : start + block] = part
        top = functools.reduce(jnp.maximum, [part[:, tile] for tile in lane_tiles(block)])
        tops[...] = top if start == 0 else jnp.maximum(tops[...], top)
    height = min(64, rows)
    for low in range(0, rows, height):
        span = slice(low, low + height)
        top = tops[span, :]
        total = functools.reduce(
            jnp.add, [jnp.exp2(logits[span, tile] - top) for tile in lane_tiles(columns)]
        )
        sums[span, :] = total
    top = tops[...].T
    total = sums[...].T
    peak = jnp.max(top, axis=0, keepdims=True)
    mass = jnp.sum(total * jnp.exp2(top - peak), axis=0, keepdims=True)
    out_ref[...] = peak + jnp.log2(mass)


def second_kernel(scale, points, x_ref, phi_ref, y_ref, e_ref, r_ref, base_ref, left, right, part_r):
    dims, cells = x_ref.shape
    columns = y_ref.shape[1]
    block = min(512, columns)
    wide = x_ref[...] * (2.0 * scale)
    left[...] = jnp.concatenate([*pieces(wide), pad_rows(pieces(phi_ref[...]))], axis=0).T
    y = y_ref[...]
    right[...] = jnp.concatenate([y, y, y, ones_rows(columns)], axis=0)
    near = jnp.sum(jnp.square(y.astype(jnp.float32)), axis=0, keepdims=True)
    base_ref[...] = scale * near - math.log2(points)
    for start in range(0, columns, block):
        span = slice(start, start + block)
        part = jnp.dot(left[...], right[:, span], preferred_element_type=jnp.float32)
        e_ref[:, span] = part
        peak = jnp.max(part, axis=0, keepdims=True)
        base_ref[:, span] = base_ref[:, span] - peak
        expo = jnp.exp2(e_ref[:, span] - peak)
        e_ref[:, span] = expo
        total = jnp.sum(expo, axis=0, keepdims=True)
        weight = 1.0 / (points * total)
        share = e_ref[:, span] * weight
        row = functools.reduce(jnp.add, [share[:, tile] for tile in lane_tiles(block)])
        part_r[...] = row if start == 0 else part_r[...] + row
    r_ref[...] = jnp.sum(part_r[...].T, axis=0, keepdims=True)


def meet_kernel(own_ref, other_ref, out_ref):
    rows = own_ref.shape[1] // 2
    out_ref[:, :rows] = own_ref[:, :rows] + other_ref[:, rows:]
    out_ref[:, rows:] = own_ref[:, rows:] + other_ref[:, :rows]


def third_kernel(key, count, x_ref, e_ref, base_ref, *refs):
    *r_refs, out_ref, g_ref, tall = refs
    dims, cells = x_ref.shape
    width = out_ref.shape[1]
    start = 0
    if key is not None:
        start = pl.multiple_of((lax.axis_index("atlas") ^ key) * width, LANES)
    rows = lax.broadcasted_iota(jnp.int32, (16, cells), 0)
    ones = jnp.where(rows == 0, 1.0, 0.0).astype(jnp.bfloat16)
    x = jnp.concatenate([x_ref[...].astype(jnp.bfloat16), ones], axis=0)
    total = functools.reduce(jnp.add, [ref[...] for ref in r_refs])
    tall[...] = jnp.broadcast_to(1.0 / (count * total), (LANES, cells)).T
    q = e_ref[:, pl.ds(start, width)] * jnp.concatenate([tall[...]] * (width // LANES), axis=1)
    high = q.astype(jnp.bfloat16)
    low = (q - high.astype(jnp.float32)).astype(jnp.bfloat16)
    moved = jnp.dot(x, high, preferred_element_type=jnp.float32)
    moved = moved + jnp.dot(x, low, preferred_element_type=jnp.float32)
    mass = moved[dims : dims + 1, :]
    out_ref[...] = moved[:dims, :] / mass
    g_ref[...] = (blur / LOG2E) * (base_ref[:, pl.ds(start, width)] - jnp.log2(mass))


def assemble_kernel(atlases, *refs):
    own, other, g_own, g_other = refs[:atlases], refs[atlases : 2 * atlases], *refs[2 * atlases : 2 * atlases + 2]
    out_ref, g_ref, sems = refs[2 * atlases + 2 :]
    width = own[0].shape[1]
    atlas = lax.axis_index("atlas")
    row = lax.axis_index("row")
    copies = []
    for half, slabs, duals in ((row, own, g_own), (1 - row, other, g_other)):
        for key in range(atlases):
            start = pl.multiple_of((half * atlases + (atlas ^ key)) * width, LANES)
            copies.append(
                pltpu.make_async_copy(
                    slabs[key], out_ref.at[:, pl.ds(start, width)], sems.at[len(copies)]
                )
            )
            copies[-1].start()
            g_ref[:, pl.ds(start, width)] = duals[:, key * width : (key + 1) * width]
    for copy in copies:
        copy.wait()


def exchange(value, axis, size, key):
    return lax.ppermute(value, axis, [(at, at ^ key) for at in range(size)])


def partners(value, axis):
    size = lax.axis_size(axis)
    if size & (size - 1) == 0 and size <= 8:
        return [exchange(value, axis, size, key) for key in range(1, size)]
    return [
        lax.ppermute(value, axis, [(at, (at + key) % size) for at in range(size)])
        for key in range(1, size)
    ]


def shards(cells, support):
    own = cells[0]
    dims, rows = own.shape
    columns = support.shape[1]
    row_size = lax.axis_size("row")
    atlases = lax.axis_size("atlas")
    total_cells = rows * row_size
    total_support = columns * lax.axis_size("col")
    share = columns // row_size
    scale = LOG2E / (blur * dims)
    row_at = lax.axis_index("row")
    paired = row_size == 2

    def gather_rows(value):
        if paired:
            return jnp.concatenate([value, exchange(value, "row", 2, 1)], axis=-1)
        return lax.all_gather(value, "row", axis=value.ndim - 1, tiled=True)

    def sum_rows(value):
        if paired:
            return pl.pallas_call(
                meet_kernel,
                out_shape=jax.ShapeDtypeStruct(value.shape, jnp.float32),
                in_specs=[VMEM, VMEM],
                out_specs=VMEM,
                compiler_params=pltpu.CompilerParams(vmem_limit_bytes=4 << 20),
                name="meet",
            )(value, exchange(value, "row", 2, 1))
        return lax.psum(value, "row")

    def own_rows(value):
        if paired:
            return value[:, :rows]
        return lax.dynamic_slice_in_dim(value, row_at * rows, rows, 1)

    def all_rows(value):
        return lax.all_gather(value, "row", axis=1, tiled=True)

    everyone = gather_rows(own.astype(jnp.float32))
    mine = lax.dynamic_slice_in_dim(support, row_at * share, share, 1)
    depth = 3 * dims + 16

    def row_vector(width):
        return jax.ShapeDtypeStruct((1, width), jnp.float32)

    lam, far = pl.pallas_call(
        functools.partial(first_kernel, scale),
        out_shape=(row_vector(rows), row_vector(rows)),
        in_specs=[VMEM, VMEM],
        out_specs=(VMEM, VMEM),
        scratch_shapes=[
            pltpu.VMEM((rows, depth), jnp.bfloat16),
            pltpu.VMEM((depth, columns), jnp.bfloat16),
            pltpu.VMEM((rows, columns), jnp.float32),
            pltpu.VMEM((rows, LANES), jnp.float32),
            pltpu.VMEM((rows, LANES), jnp.float32),
        ],
        compiler_params=pltpu.CompilerParams(vmem_limit_bytes=24 << 20),
        name="first",
    )(own, support)

    others = partners(lam, "col")
    peak = functools.reduce(jnp.maximum, others, lam)
    mass = functools.reduce(jnp.add, [jnp.exp2(one - peak) for one in [lam, *others]])
    phi = -math.log2(total_cells) - (peak + jnp.log2(mass))

    e, r, base = pl.pallas_call(
        functools.partial(second_kernel, scale, float(total_support)),
        out_shape=(
            jax.ShapeDtypeStruct((total_cells, share), jnp.float32),
            row_vector(total_cells),
            row_vector(share),
        ),
        in_specs=[VMEM, VMEM, VMEM],
        out_specs=(VMEM, VMEM, VMEM),
        scratch_shapes=[
            pltpu.VMEM((total_cells, depth), jnp.bfloat16),
            pltpu.VMEM((depth, share), jnp.bfloat16),
            pltpu.VMEM((total_cells, LANES), jnp.float32),
        ],
        compiler_params=pltpu.CompilerParams(vmem_limit_bytes=32 << 20),
        name="second",
    )(everyone, gather_rows(phi), mine)

    r = sum_rows(r)
    shares = [r, *partners(r, "col")]

    def third(key, width):
        return pl.pallas_call(
            functools.partial(third_kernel, key, float(total_cells)),
            out_shape=(jax.ShapeDtypeStruct((dims, width), jnp.float32), row_vector(width)),
            in_specs=[VMEM] * (3 + len(shares)),
            out_specs=(VMEM, VMEM),
            scratch_shapes=[pltpu.VMEM((total_cells, LANES), jnp.float32)],
            compiler_params=pltpu.CompilerParams(vmem_limit_bytes=24 << 20),
            name="third",
        )(everyone, e, base, *shares)

    piece = share // atlases
    if paired and atlases & (atlases - 1) == 0 and atlases <= 8 and piece % LANES == 0:

        order = sorted(range(atlases), key=lambda key: (key == 0, -key))
        terms, duals, arrived = [None] * atlases, [None] * atlases, []
        for key in order:
            terms[key], duals[key] = third(key, piece)
            if key:
                arrived.append(exchange(terms[key], "atlas", atlases, key))
        sums = functools.reduce(jnp.add, arrived, terms[0]) * (1.0 / atlases)
        slabs = [sums, *partners(sums, "atlas")]
        duals = jnp.concatenate(duals, axis=1)
        updated, dual_g = pl.pallas_call(
            functools.partial(assemble_kernel, atlases),
            out_shape=(jax.ShapeDtypeStruct((dims, columns), jnp.float32), row_vector(columns)),
            in_specs=[VMEM] * (2 * atlases + 2),
            out_specs=(pl.BlockSpec(memory_space=pl.ANY), VMEM),
            scratch_shapes=[pltpu.SemaphoreType.DMA((2 * atlases,))],
            compiler_params=pltpu.CompilerParams(vmem_limit_bytes=8 << 20),
            name="assemble",
        )(
            *slabs,
            *[exchange(slab, "row", 2, 1) for slab in slabs],
            duals,
            exchange(duals, "row", 2, 1),
        )
    else:
        moved, dual_g = third(None, share)
        updated = all_rows(lax.psum(moved, "atlas") * (1.0 / atlases))
        dual_g = all_rows(dual_g)

    cell_dual = (blur / LOG2E) * (
        phi + far - jnp.log2(total_cells * own_rows(functools.reduce(jnp.add, shares)))
    )

    return (cell_dual, dual_g, updated)


def solution(mesh):
    in_specs = (P("atlas", None, "row"), P(None, "col"))
    out_specs = (P("atlas", "row"), P("atlas", "col"), P(None, "col"))
    return jax.shard_map(shards, mesh=mesh, in_specs=in_specs, out_specs=out_specs, check_vma=False)
```

time: 55.3 us -> 47.6 us (0.86)
  local copies, waits for them, and re-layouts: 8.53 us -> 2.88 us
  other arithmetic: 4.54 us -> 0.71 us
  Pallas kernels: 7.31 us -> 9.84 us
  waiting for transfers between devices: 15.9 us -> 14.2 us
  starting transfers between devices: 17.8 us -> 19 us
    unnamed x8 -> x7, local copies, waits for them, and re-layouts: 8.49 us -> 1.89 us
    pallas_call x2 -> x7, Pallas kernels: 4.36 us -> 6.94 us  [the longest x4 2.89 us: third(): pl.pallas_call(functools.partial(third_kernel, key, float(total_cells)),...]
    reduce_sum x2 -> x0, other arithmetic: 1.9 us -> none  [the longest x1 1.02 us: shards(): near = jnp.sum(jnp.square(mine.astype(jnp.float32)), axis=0)[None, :]]
    ppermute x17 -> x20, waiting for transfers between devices: 15.9 us -> 14.2 us  [exchange(): return lax.ppermute(value, axis, [(at, at ^ key) for at in range(size)])]
    concatenate x3 -> x0, other arithmetic: 1.7 us -> none  [the longest x2 1.67 us: in_order(): return jnp.concatenate([first, last], axis=1)]
    ppermute x17 -> x20, starting transfers between devices: 17.8 us -> 19 us  [exchange(): return lax.ppermute(value, axis, [(at, at ^ key) for at in range(size)])]
    dynamic_slice x1, local copies, waits for them, and re-layouts: 0.04 us -> 0.97 us  [shards(): mine = lax.dynamic_slice_in_dim(support, row_at * share, share, 1)]
  transfers between devices with their start and end apart: 17 -> 20, of which waited for: 12 -> 13; matrix products, arithmetic and copies ran while one was open for 6% -> 3% of each run, Pallas kernels for 0% -> 5%
where the time goes in v2:
time: 47.6 us; the launch traced here: 47.3 us
  starting transfers between devices  19 us (40%)
  waiting for transfers between devices  14.2 us (30%)
  Pallas kernels  9.84 us (21%)
  local copies, waits for them, and re-layouts  2.88 us (6%)
  between operations  0.75 us (2%)
  other arithmetic  0.71 us (1%)
    ppermute x20, starting transfers between devices, exchange(): return lax.ppermute(value, axis, [(at, at ^ key) for at in range(size)])  19 us
    ppermute x20, waiting for transfers between devices, exchange(): return lax.ppermute(value, axis, [(at, at ^ key) for at in range(size)])  14.2 us
    pallas_call x1, Pallas kernels, shards(): pl.pallas_call(functools.partial(second_kernel, scale, float(total_suppor...  2.9 us
    pallas_call x4, Pallas kernels, third(): pl.pallas_call(functools.partial(third_kernel, key, float(total_cells)),...  2.89 us
    pallas_call x1, Pallas kernels, shards(): pl.pallas_call(functools.partial(first_kernel, scale), out_shape=(row_vec...  2.42 us
    unnamed x7, local copies, waits for them, and re-layouts  1.89 us
    pallas_call x1, Pallas kernels, shards(): pl.pallas_call(functools.partial(assemble_kernel, atlases), out_shape=(ja...  1.63 us
    dynamic_slice x1, local copies, waits for them, and re-layouts, shards(): mine = lax.dynamic_slice_in_dim(support, row_at * share, share, 1)  0.97 us
  transfers between devices with their start and end apart: 20, of which 13 were waited for; matrix products, arithmetic and copies ran while one was open for 3% of the time, Pallas kernels for 5%

profile of v2, /device:TPU:0, one launch (start us, length us, event | category | flops | bytes accessed | tf_op | source)
XLA Modules:
  0.0 47.3 jit_solution(2468089614596164568)
XLA Ops:
  0.6 1.0 %copy-done = bf16[64,4096]{1,0:T(8,128)(2,1)S(1)} copy-done((bf16[64,4096]{1,0:T(8,128)(2,1)S(1)}, bf16[64,4096]{1,0:T(8,128)(2,1)}, u32[]{:S(2)}) %copy-start) | copy-done | bytes 524312
  1.7 0.8 %copy-done.1 = bf16[1,64,512]{2,1,0:T(8,128)(2,1)S(1)} copy-done((bf16[1,64,512]{2,1,0:T(8,128)(2,1)S(1)}, bf16[1,64,512]{2,1,0:T(8,128)(2,1)}, u32[]{:S(2)}) %copy-start.1) | copy-done | bytes 65560
  2.5 2.4 %first.1 = (f32[1,512]{1,0:T(1,128)S(1)}, f32[1,512]{1,0:T(1,128)S(1)}) custom-call(bf16[64,512]{1,0:T(8,128)(2,1)S(1)} %bitcast.2, bf16[64,4096]{1,0:T(8,128)(2,1)S(1)} %copy-done), custom_call_target="tpu_custom_call" | custom-call | tf_op jit(solution)/shard_map/first/pallas_call | solution.py:215
  4.9 5.1 %collective-permute-start.2 = (f32[1,512]{1,0:T(1,128)S(1)}, f32[1,512]{1,0:T(1,128)S(1)}, u32[]{:S(2)}, u32[]{:S(2)}) collective-permute-start(f32[1,512]{1,0:T(1,128)S(1)} %get-tuple-element.18), channel_id=1, source_target_pairs={{0,3},{1,2},{2,1},{3,0},{4,7},{5,6},{6,5},{7,4},{8,11},{9,10},{10,... | collective-permute-start | bytes 6152 | tf_op jit(solution)/shard_map/ppermute | solution.py:157
  10.1 0.6 %collective-permute-start = (f32[1,512]{1,0:T(1,128)S(1)}, f32[1,512]{1,0:T(1,128)S(1)}, u32[]{:S(2)}, u32[]{:S(2)}) collective-permute-start(f32[1,512]{1,0:T(1,128)S(1)} %get-tuple-element.18), channel_id=1, source_target_pairs={{0,1},{1,0},{2,3},{3,2},{4,5},{5,4},{6,7},{7,6},{8,9},{9,8},{10,11... | collective-permute-start | bytes 6152 | tf_op jit(solution)/shard_map/ppermute | solution.py:157
  10.8 0.8 %collective-permute-done.2 = f32[1,512]{1,0:T(1,128)S(1)} collective-permute-done((f32[1,512]{1,0:T(1,128)S(1)}, f32[1,512]{1,0:T(1,128)S(1)}, u32[]{:S(2)}, u32[]{:S(2)}) %collective-permute-start.2) | collective-permute-done | bytes 2080 | tf_op jit(solution)/shard_map/ppermute | solution.py:157
  11.6 2.9 %collective-permute-done.1 = f32[1,512]{1,0:T(1,128)S(1)} collective-permute-done((f32[1,512]{1,0:T(1,128)S(1)}, f32[1,512]{1,0:T(1,128)S(1)}, u32[]{:S(2)}, u32[]{:S(2)}) %collective-permute-start.1) | collective-permute-done | bytes 2080 | tf_op jit(solution)/shard_map/ppermute | solution.py:157
  14.7 1.0 %constant_dynamic-slice_fusion.y_ref = bf16[64,2048]{1,0:T(8,128)(2,1)S(1)} fusion(bf16[64,4096]{1,0:T(8,128)(2,1)} %y_ref.1, s32[]{:T(128)S(6)} %select_n.3), kind=kLoop, calls=%fused_computation.13 | loop fusion | bytes 524292 | tf_op jit(solution)/shard_map/dynamic_slice | solution.py:209
  15.9 2.9 %second.1 = (f32[1024,2048]{1,0:T(8,128)S(1)}, f32[1,1024]{1,0:T(1,128)S(1)}, f32[1,2048]{1,0:T(1,128)S(1)}) custom-call(f32[64,1024]{1,0:T(8,128)S(1)} %pad_maximum_fusion.x_ref, f32[1,1024]{1,0:T(1,128)S(1)} %pad_maximum_fusion.1.phi_ref, bf16[64,2048]{1,0:T(8,128)(2,1)S(1)} %constant_dynamic-slice_fusion.y_ref), custom_call_target="tpu_custom_call" | custom-call | tf_op jit(solution)/shard_map/second/pallas_call | solution.py:236
  18.8 0.4 collective-permute-start.5
  19.2 0.8 %collective-permute-done.5.other_ref = f32[1,1024]{1,0:T(1,128)S(1)} collective-permute-done((f32[1,1024]{1,0:T(1,128)S(1)}, f32[1,1024]{1,0:T(1,128)S(1)}, u32[]{:S(2)}, u32[]{:S(2)}) %collective-permute-start.5) | collective-permute-done | bytes 4128 | tf_op jit(solution)/shard_map/ppermute | solution.py:157
  20.0 1.5 %collective-permute-start.8 = (f32[1,1024]{1,0:T(1,128)S(1)}, f32[1,1024]{1,0:T(1,128)S(1)}, u32[]{:S(2)}, u32[]{:S(2)}) collective-permute-start(f32[1,1024]{1,0:T(1,128)S(1)} %meet.1.refs_0_), channel_id=1, source_target_pairs={{0,3},{1,2},{2,1},{3,0},{4,7},{5,6},{6,5},{7,4},{8,11},{9,10},{10,... | collective-permute-start | bytes 12296 | tf_op jit(solution)/shard_map/ppermute | solution.py:157
  21.5 0.6 %collective-permute-start.7 = (f32[1,1024]{1,0:T(1,128)S(1)}, f32[1,1024]{1,0:T(1,128)S(1)}, u32[]{:S(2)}, u32[]{:S(2)}) collective-permute-start(f32[1,1024]{1,0:T(1,128)S(1)} %meet.1.refs_0_), channel_id=1, source_target_pairs={{0,2},{1,3},{2,0},{3,1},{4,6},{5,7},{6,4},{7,5},{8,10},{9,11},{10,... | collective-permute-start | bytes 12296 | tf_op jit(solution)/shard_map/ppermute | solution.py:157
  22.1 2.3 %collective-permute-start.6 = (f32[1,1024]{1,0:T(1,128)S(1)}, f32[1,1024]{1,0:T(1,128)S(1)}, u32[]{:S(2)}, u32[]{:S(2)}) collective-permute-start(f32[1,1024]{1,0:T(1,128)S(1)} %meet.1.refs_0_), channel_id=1, source_target_pairs={{0,1},{1,0},{2,3},{3,2},{4,5},{5,4},{6,7},{7,6},{8,9},{9,8},{10,11... | collective-permute-start | bytes 12296 | tf_op jit(solution)/shard_map/ppermute | solution.py:157
  24.4 1.0 %collective-permute-done.8.refs_3_ = f32[1,1024]{1,0:T(1,128)S(1)} collective-permute-done((f32[1,1024]{1,0:T(1,128)S(1)}, f32[1,1024]{1,0:T(1,128)S(1)}, u32[]{:S(2)}, u32[]{:S(2)}) %collective-permute-start.8) | collective-permute-done | bytes 4128 | tf_op jit(solution)/shard_map/ppermute | solution.py:157
  25.4 0.6 %collective-permute-done.7.refs_2_ = f32[1,1024]{1,0:T(1,128)S(1)} collective-permute-done((f32[1,1024]{1,0:T(1,128)S(1)}, f32[1,1024]{1,0:T(1,128)S(1)}, u32[]{:S(2)}, u32[]{:S(2)}) %collective-permute-start.7) | collective-permute-done | bytes 4128 | tf_op jit(solution)/shard_map/ppermute | solution.py:157
  26.0 0.7 %third.5 = (f32[64,512]{1,0:T(8,128)S(1)}, f32[1,512]{1,0:T(1,128)S(1)}) custom-call(f32[64,1024]{1,0:T(8,128)S(1)} %pad_maximum_fusion.x_ref, f32[1024,2048]{1,0:T(8,128)S(1)} %get-tuple-element.21.e_ref, f32[1,2048]{1,0:T(1,128)S(1)} %get-tuple-element.22.base_ref, f32[1,1024]{1,0:T(1,128)S(1)} %meet.1.refs_0_, ...), custom_call_target="tpu_custom_call" | custom-call | tf_op jit(solution)/shard_map/third/pallas_call | solution.py:258
  26.8 2.5 %collective-permute-start.9 = (f32[64,512]{1,0:T(8,128)S(1)}, f32[64,512]{1,0:T(8,128)S(1)}, u32[]{:S(2)}, u32[]{:S(2)}) collective-permute-start(f32[64,512]{1,0:T(8,128)S(1)} %get-tuple-element.24), channel_id=1, source_target_pairs={{0,24},{8,16},{16,8},{24,0},{1,25},{9,17},{17,9},{25,1},{2,26},{10... | collective-permute-start | bytes 393224 | tf_op jit(solution)/shard_map/ppermute | solution.py:157
  29.3 0.7 %third.6 = (f32[64,512]{1,0:T(8,128)S(1)}, f32[1,512]{1,0:T(1,128)S(1)}) custom-call(f32[64,1024]{1,0:T(8,128)S(1)} %pad_maximum_fusion.x_ref, f32[1024,2048]{1,0:T(8,128)S(1)} %get-tuple-element.21.e_ref, f32[1,2048]{1,0:T(1,128)S(1)} %get-tuple-element.22.base_ref, f32[1,1024]{1,0:T(1,128)S(1)} %meet.1.refs_0_, ...), custom_call_target="tpu_custom_call" | custom-call | tf_op jit(solution)/shard_map/third/pallas_call | solution.py:258
  30.0 0.6 %collective-permute-start.10 = (f32[64,512]{1,0:T(8,128)S(1)}, f32[64,512]{1,0:T(8,128)S(1)}, u32[]{:S(2)}, u32[]{:S(2)}) collective-permute-start(f32[64,512]{1,0:T(8,128)S(1)} %get-tuple-element.25), channel_id=1, source_target_pairs={{0,16},{8,24},{16,0},{24,8},{1,17},{9,25},{17,1},{25,9},{2,18},{10... | collective-permute-start | bytes 393224 | tf_op jit(solution)/shard_map/ppermute | solution.py:157
  30.6 0.7 %third.7 = (f32[64,512]{1,0:T(8,128)S(1)}, f32[1,512]{1,0:T(1,128)S(1)}) custom-call(f32[64,1024]{1,0:T(8,128)S(1)} %pad_maximum_fusion.x_ref, f32[1024,2048]{1,0:T(8,128)S(1)} %get-tuple-element.21.e_ref, f32[1,2048]{1,0:T(1,128)S(1)} %get-tuple-element.22.base_ref, f32[1,1024]{1,0:T(1,128)S(1)} %meet.1.refs_0_, ...), custom_call_target="tpu_custom_call" | custom-call | tf_op jit(solution)/shard_map/third/pallas_call | solution.py:258
  31.3 0.6 %collective-permute-start.11 = (f32[64,512]{1,0:T(8,128)S(1)}, f32[64,512]{1,0:T(8,128)S(1)}, u32[]{:S(2)}, u32[]{:S(2)}) collective-permute-start(f32[64,512]{1,0:T(8,128)S(1)} %get-tuple-element.26), channel_id=1, source_target_pairs={{0,8},{8,0},{16,24},{24,16},{1,9},{9,1},{17,25},{25,17},{2,10},{10... | collective-permute-start | bytes 393224 | tf_op jit(solution)/shard_map/ppermute | solution.py:157
  31.9 0.7 %third.4 = (f32[64,512]{1,0:T(8,128)S(1)}, f32[1,512]{1,0:T(1,128)S(1)}) custom-call(f32[64,1024]{1,0:T(8,128)S(1)} %pad_maximum_fusion.x_ref, f32[1024,2048]{1,0:T(8,128)S(1)} %get-tuple-element.21.e_ref, f32[1,2048]{1,0:T(1,128)S(1)} %get-tuple-element.22.base_ref, f32[1,1024]{1,0:T(1,128)S(1)} %meet.1.refs_0_, ...), custom_call_target="tpu_custom_call" | custom-call | tf_op jit(solution)/shard_map/third/pallas_call | solution.py:258
  32.9 2.6 %collective-permute-done.10 = f32[64,512]{1,0:T(8,128)S(1)} collective-permute-done((f32[64,512]{1,0:T(8,128)S(1)}, f32[64,512]{1,0:T(8,128)S(1)}, u32[]{:S(2)}, u32[]{:S(2)}) %collective-permute-start.10) | collective-permute-done | bytes 131104 | tf_op jit(solution)/shard_map/ppermute | solution.py:157
  35.5 0.8 %collective-permute-done.11 = f32[64,512]{1,0:T(8,128)S(1)} collective-permute-done((f32[64,512]{1,0:T(8,128)S(1)}, f32[64,512]{1,0:T(8,128)S(1)}, u32[]{:S(2)}, u32[]{:S(2)}) %collective-permute-start.11) | collective-permute-done | bytes 131104 | tf_op jit(solution)/shard_map/ppermute | solution.py:157
  36.4 1.5 %collective-permute-start.14 = (f32[64,512]{1,0:T(8,128)S(1)}, f32[64,512]{1,0:T(8,128)S(1)}, u32[]{:S(2)}, u32[]{:S(2)}) collective-permute-start(f32[64,512]{1,0:T(8,128)S(1)} %add_multiply_fusion.refs_0_), channel_id=1, source_target_pairs={{0,24},{8,16},{16,8},{24,0},{1,25},{9,17},{17,9},{25,1},{2,26},{10... | collective-permute-start | bytes 393224 | tf_op jit(solution)/shard_map/ppermute | solution.py:157
  37.9 0.7 %collective-permute-start.13 = (f32[64,512]{1,0:T(8,128)S(1)}, f32[64,512]{1,0:T(8,128)S(1)}, u32[]{:S(2)}, u32[]{:S(2)}) collective-permute-start(f32[64,512]{1,0:T(8,128)S(1)} %add_multiply_fusion.refs_0_), channel_id=1, source_target_pairs={{0,16},{8,24},{16,0},{24,8},{1,17},{9,25},{17,1},{25,9},{2,18},{10... | collective-permute-start | bytes 393224 | tf_op jit(solution)/shard_map/ppermute | solution.py:157
  38.6 1.3 %collective-permute-start.12 = (f32[64,512]{1,0:T(8,128)S(1)}, f32[64,512]{1,0:T(8,128)S(1)}, u32[]{:S(2)}, u32[]{:S(2)}) collective-permute-start(f32[64,512]{1,0:T(8,128)S(1)} %add_multiply_fusion.refs_0_), channel_id=1, source_target_pairs={{0,8},{8,0},{16,24},{24,16},{1,9},{9,1},{17,25},{25,17},{2,10},{10... | collective-permute-start | bytes 393224 | tf_op jit(solution)/shard_map/ppermute | solution.py:157
  40.0 0.5 %collective-permute-start.15 = (f32[64,512]{1,0:T(8,128)S(1)}, f32[64,512]{1,0:T(8,128)S(1)}, u32[]{:S(2)}, u32[]{:S(2)}) collective-permute-start(f32[64,512]{1,0:T(8,128)S(1)} %add_multiply_fusion.refs_0_), channel_id=1, source_target_pairs={{0,4},{4,0},{1,5},{5,1},{2,6},{6,2},{3,7},{7,3},{8,12},{12,8},{9,1... | collective-permute-start | bytes 393224 | tf_op jit(solution)/shard_map/ppermute | solution.py:157
  40.5 3.3 %collective-permute-done.14.refs_3_ = f32[64,512]{1,0:T(8,128)S(1)} collective-permute-done((f32[64,512]{1,0:T(8,128)S(1)}, f32[64,512]{1,0:T(8,128)S(1)}, u32[]{:S(2)}, u32[]{:S(2)}) %collective-permute-start.14) | collective-permute-done | bytes 131104 | tf_op jit(solution)/shard_map/ppermute | solution.py:157
  44.5 0.6 %subtract_multiply_fusion = f32[1,512]{1,0:T(1,128)} fusion(f32[1,512]{1,0:T(1,128)S(1)} %add_subtract_fusion, f32[1,512]{1,0:T(1,128)S(1)} %get-tuple-element.19, f32[1,1024]{1,0:T(1,128)S(1)} %collective-permute-done.8.refs_3_, f32[1,1024]{1,0:T(1,128)S(1)} %collective-permute-done.7.refs_2_, f32[1,1024]{1,0:T(1,128)S(1)} %collective-permute-done.6.refs_1_, ...), kind=kLoop, calls=%fused_computation.11 | loop fusion | flops 4096 | bytes 14336 | tf_op jit(solution)/shard_map/mul | solution.py:299
  45.7 1.6 %assemble.1 = (f32[64,4096]{1,0:T(8,128)}, f32[1,4096]{1,0:T(1,128)}) custom-call(f32[64,512]{1,0:T(8,128)S(1)} %add_multiply_fusion.refs_0_, f32[64,512]{1,0:T(8,128)S(1)} %collective-permute-done.12.refs_1_, f32[64,512]{1,0:T(8,128)S(1)} %collective-permute-done.13.refs_2_, f32[64,512]{1,0:T(8,128)S(1)} %collective-permute-done.14.refs_3_, ...), custom_call_target="tpu_custom_call" | custom-call | tf_op jit(solution)/shard_map/assemble/pallas_call | solution.py:280
  (31 shorter events, 2.0 us)
Async XLA Ops:
  0.6 1.0 %copy-start = (bf16[64,4096]{1,0:T(8,128)(2,1)S(1)}, bf16[64,4096]{1,0:T(8,128)(2,1)}, u32[]{:S(2)}) copy-start(bf16[64,4096]{1,0:T(8,128)(2,1)} %y_ref.1) | copy-start | bytes 1572868
  1.7 0.8 %copy-start.1 = (bf16[1,64,512]{2,1,0:T(8,128)(2,1)S(1)}, bf16[1,64,512]{2,1,0:T(8,128)(2,1)}, u32[]{:S(2)}) copy-start(bf16[1,64,512]{2,1,0:T(8,128)(2,1)} %param.2) | copy-start | bytes 196612
  4.9 6.7 %collective-permute-start.2 = (f32[1,512]{1,0:T(1,128)S(1)}, f32[1,512]{1,0:T(1,128)S(1)}, u32[]{:S(2)}, u32[]{:S(2)}) collective-permute-start(f32[1,512]{1,0:T(1,128)S(1)} %get-tuple-element.18), channel_id=1, source_target_pairs={{0,3},{1,2},{2,1},{3,0},{4,7},{5,6},{6,5},{7,4},{8,11},{9,10},{10,... | collective-permute-start | bytes 6152 | tf_op jit(solution)/shard_map/ppermute | solution.py:157
  10.1 4.5 %collective-permute-start.1 = (f32[1,512]{1,0:T(1,128)S(1)}, f32[1,512]{1,0:T(1,128)S(1)}, u32[]{:S(2)}, u32[]{:S(2)}) collective-permute-start(f32[1,512]{1,0:T(1,128)S(1)} %get-tuple-element.18), channel_id=1, source_target_pairs={{0,2},{1,3},{2,0},{3,1},{4,6},{5,7},{6,4},{7,5},{8,10},{9,11},{10,... | collective-permute-start | bytes 6152 | tf_op jit(solution)/shard_map/ppermute | solution.py:157
  10.1 4.5 %collective-permute-start = (f32[1,512]{1,0:T(1,128)S(1)}, f32[1,512]{1,0:T(1,128)S(1)}, u32[]{:S(2)}, u32[]{:S(2)}) collective-permute-start(f32[1,512]{1,0:T(1,128)S(1)} %get-tuple-element.18), channel_id=1, source_target_pairs={{0,1},{1,0},{2,3},{3,2},{4,5},{5,4},{6,7},{7,6},{8,9},{9,8},{10,11... | collective-permute-start | bytes 6152 | tf_op jit(solution)/shard_map/ppermute | solution.py:157
  10.7 5.1 %collective-permute-start.3 = (f32[64,512]{1,0:T(8,128)S(1)}, f32[64,512]{1,0:T(8,128)S(1)}, u32[]{:S(2)}, u32[]{:S(2)}) collective-permute-start(f32[64,512]{1,0:T(8,128)S(1)} %bitcast_convert_fusion), channel_id=1, source_target_pairs={{0,4},{4,0},{1,5},{5,1},{2,6},{6,2},{3,7},{7,3},{8,12},{12,8},{9,1... | collective-permute-start | bytes 393224 | tf_op jit(solution)/shard_map/ppermute | solution.py:157
  14.6 1.2 %collective-permute-start.4 = (f32[1,512]{1,0:T(1,128)S(1)}, f32[1,512]{1,0:T(1,128)S(1)}, u32[]{:S(2)}, u32[]{:S(2)}) collective-permute-start(f32[1,512]{1,0:T(1,128)S(1)} %add_subtract_fusion), channel_id=1, source_target_pairs={{0,4},{4,0},{1,5},{5,1},{2,6},{6,2},{3,7},{7,3},{8,12},{12,8},{9,1... | collective-permute-start | bytes 6152 | tf_op jit(solution)/shard_map/ppermute | solution.py:157
  18.8 1.2 %collective-permute-start.5 = (f32[1,1024]{1,0:T(1,128)S(1)}, f32[1,1024]{1,0:T(1,128)S(1)}, u32[]{:S(2)}, u32[]{:S(2)}) collective-permute-start(f32[1,1024]{1,0:T(1,128)S(1)} %get-tuple-element.20.own_ref), channel_id=1, source_target_pairs={{0,4},{4,0},{1,5},{5,1},{2,6},{6,2},{3,7},{7,3},{8,12},{12,8},{9,1... | collective-permute-start | bytes 12296 | tf_op jit(solution)/shard_map/ppermute | solution.py:157
  20.0 5.4 %collective-permute-start.8 = (f32[1,1024]{1,0:T(1,128)S(1)}, f32[1,1024]{1,0:T(1,128)S(1)}, u32[]{:S(2)}, u32[]{:S(2)}) collective-permute-start(f32[1,1024]{1,0:T(1,128)S(1)} %meet.1.refs_0_), channel_id=1, source_target_pairs={{0,3},{1,2},{2,1},{3,0},{4,7},{5,6},{6,5},{7,4},{8,11},{9,10},{10,... | collective-permute-start | bytes 12296 | tf_op jit(solution)/shard_map/ppermute | solution.py:157
  21.5 4.5 %collective-permute-start.7 = (f32[1,1024]{1,0:T(1,128)S(1)}, f32[1,1024]{1,0:T(1,128)S(1)}, u32[]{:S(2)}, u32[]{:S(2)}) collective-permute-start(f32[1,1024]{1,0:T(1,128)S(1)} %meet.1.refs_0_), channel_id=1, source_target_pairs={{0,2},{1,3},{2,0},{3,1},{4,6},{5,7},{6,4},{7,5},{8,10},{9,11},{10,... | collective-permute-start | bytes 12296 | tf_op jit(solution)/shard_map/ppermute | solution.py:157
  22.1 3.9 %collective-permute-start.6 = (f32[1,1024]{1,0:T(1,128)S(1)}, f32[1,1024]{1,0:T(1,128)S(1)}, u32[]{:S(2)}, u32[]{:S(2)}) collective-permute-start(f32[1,1024]{1,0:T(1,128)S(1)} %meet.1.refs_0_), channel_id=1, source_target_pairs={{0,1},{1,0},{2,3},{3,2},{4,5},{5,4},{6,7},{7,6},{8,9},{9,8},{10,11... | collective-permute-start | bytes 12296 | tf_op jit(solution)/shard_map/ppermute | solution.py:157
  26.8 6.1 %collective-permute-start.9 = (f32[64,512]{1,0:T(8,128)S(1)}, f32[64,512]{1,0:T(8,128)S(1)}, u32[]{:S(2)}, u32[]{:S(2)}) collective-permute-start(f32[64,512]{1,0:T(8,128)S(1)} %get-tuple-element.24), channel_id=1, source_target_pairs={{0,24},{8,16},{16,8},{24,0},{1,25},{9,17},{17,9},{25,1},{2,26},{10... | collective-permute-start | bytes 393224 | tf_op jit(solution)/shard_map/ppermute | solution.py:157
  30.0 5.5 %collective-permute-start.10 = (f32[64,512]{1,0:T(8,128)S(1)}, f32[64,512]{1,0:T(8,128)S(1)}, u32[]{:S(2)}, u32[]{:S(2)}) collective-permute-start(f32[64,512]{1,0:T(8,128)S(1)} %get-tuple-element.25), channel_id=1, source_target_pairs={{0,16},{8,24},{16,0},{24,8},{1,17},{9,25},{17,1},{25,9},{2,18},{10... | collective-permute-start | bytes 393224 | tf_op jit(solution)/shard_map/ppermute | solution.py:157
  31.3 5.0 %collective-permute-start.11 = (f32[64,512]{1,0:T(8,128)S(1)}, f32[64,512]{1,0:T(8,128)S(1)}, u32[]{:S(2)}, u32[]{:S(2)}) collective-permute-start(f32[64,512]{1,0:T(8,128)S(1)} %get-tuple-element.26), channel_id=1, source_target_pairs={{0,8},{8,0},{16,24},{24,16},{1,9},{9,1},{17,25},{25,17},{2,10},{10... | collective-permute-start | bytes 393224 | tf_op jit(solution)/shard_map/ppermute | solution.py:157
  36.4 7.4 %collective-permute-start.14 = (f32[64,512]{1,0:T(8,128)S(1)}, f32[64,512]{1,0:T(8,128)S(1)}, u32[]{:S(2)}, u32[]{:S(2)}) collective-permute-start(f32[64,512]{1,0:T(8,128)S(1)} %add_multiply_fusion.refs_0_), channel_id=1, source_target_pairs={{0,24},{8,16},{16,8},{24,0},{1,25},{9,17},{17,9},{25,1},{2,26},{10... | collective-permute-start | bytes 393224 | tf_op jit(solution)/shard_map/ppermute | solution.py:157
  37.9 6.1 %collective-permute-start.13 = (f32[64,512]{1,0:T(8,128)S(1)}, f32[64,512]{1,0:T(8,128)S(1)}, u32[]{:S(2)}, u32[]{:S(2)}) collective-permute-start(f32[64,512]{1,0:T(8,128)S(1)} %add_multiply_fusion.refs_0_), channel_id=1, source_target_pairs={{0,16},{8,24},{16,0},{24,8},{1,17},{9,25},{17,1},{25,9},{2,18},{10... | collective-permute-start | bytes 393224 | tf_op jit(solution)/shard_map/ppermute | solution.py:157
  38.6 5.7 %collective-permute-start.12 = (f32[64,512]{1,0:T(8,128)S(1)}, f32[64,512]{1,0:T(8,128)S(1)}, u32[]{:S(2)}, u32[]{:S(2)}) collective-permute-start(f32[64,512]{1,0:T(8,128)S(1)} %add_multiply_fusion.refs_0_), channel_id=1, source_target_pairs={{0,8},{8,0},{16,24},{24,16},{1,9},{9,1},{17,25},{25,17},{2,10},{10... | collective-permute-start | bytes 393224 | tf_op jit(solution)/shard_map/ppermute | solution.py:157
  40.0 5.2 %collective-permute-start.19 = (f32[1,2048]{1,0:T(1,128)S(1)}, f32[1,2048]{1,0:T(1,128)S(1)}, u32[]{:S(2)}, u32[]{:S(2)}) collective-permute-start(f32[1,2048]{1,0:T(1,128)S(1)} %constant_dynamic-update-slice_fusion.refs_8_), channel_id=1, source_target_pairs={{0,4},{4,0},{1,5},{5,1},{2,6},{6,2},{3,7},{7,3},{8,12},{12,8},{9,1... | collective-permute-start | bytes 24584 | tf_op jit(solution)/shard_map/ppermute | solution.py:157
  40.0 5.2 %collective-permute-start.15 = (f32[64,512]{1,0:T(8,128)S(1)}, f32[64,512]{1,0:T(8,128)S(1)}, u32[]{:S(2)}, u32[]{:S(2)}) collective-permute-start(f32[64,512]{1,0:T(8,128)S(1)} %add_multiply_fusion.refs_0_), channel_id=1, source_target_pairs={{0,4},{4,0},{1,5},{5,1},{2,6},{6,2},{3,7},{7,3},{8,12},{12,8},{9,1... | collective-permute-start | bytes 393224 | tf_op jit(solution)/shard_map/ppermute | solution.py:157
  43.8 1.3 %collective-permute-start.18 = (f32[64,512]{1,0:T(8,128)S(1)}, f32[64,512]{1,0:T(8,128)S(1)}, u32[]{:S(2)}, u32[]{:S(2)}) collective-permute-start(f32[64,512]{1,0:T(8,128)S(1)} %collective-permute-done.14.refs_3_), channel_id=1, source_target_pairs={{0,4},{4,0},{1,5},{5,1},{2,6},{6,2},{3,7},{7,3},{8,12},{12,8},{9,1... | collective-permute-start | bytes 393224 | tf_op jit(solution)/shard_map/ppermute | solution.py:157
  44.0 1.3 %collective-permute-start.17 = (f32[64,512]{1,0:T(8,128)S(1)}, f32[64,512]{1,0:T(8,128)S(1)}, u32[]{:S(2)}, u32[]{:S(2)}) collective-permute-start(f32[64,512]{1,0:T(8,128)S(1)} %collective-permute-done.13.refs_2_), channel_id=1, source_target_pairs={{0,4},{4,0},{1,5},{5,1},{2,6},{6,2},{3,7},{7,3},{8,12},{12,8},{9,1... | collective-permute-start | bytes 393224 | tf_op jit(solution)/shard_map/ppermute | solution.py:157
  44.3 1.3 %collective-permute-start.16 = (f32[64,512]{1,0:T(8,128)S(1)}, f32[64,512]{1,0:T(8,128)S(1)}, u32[]{:S(2)}, u32[]{:S(2)}) collective-permute-start(f32[64,512]{1,0:T(8,128)S(1)} %collective-permute-done.12.refs_1_), channel_id=1, source_target_pairs={{0,4},{4,0},{1,5},{5,1},{2,6},{6,2},{3,7},{7,3},{8,12},{12,8},{9,1... | collective-permute-start | bytes 393224 | tf_op jit(solution)/shard_map/ppermute | solution.py:157

commit v3 on v2

--- a/solution.py
+++ b/solution.py
@@ -9,12 +9,12 @@
 from jax.sharding import PartitionSpec as P
 
 
-ITERS = 2
 blur = 0.1
 LANES = 128
 SUBLANES = 8
 LOG2E = 1.4426950408889634
 VMEM = pl.BlockSpec(memory_space=pltpu.VMEM)
+HBM = pl.BlockSpec(memory_space=pltpu.HBM)
 
 
 def pieces(value):
@@ -43,24 +43,32 @@
     return [slice(at, at + LANES) for at in range(0, width, LANES)]
 
 
-def first_kernel(scale, x_ref, y_ref, out_ref, far_ref, left, right, logits, tops, sums):
-    dims, rows = x_ref.shape
+def first_kernel(
+    scale, x_hbm, y_hbm, out_ref, far_ref, x_ref, y_ref, left, right, logits, tops, sums, sems
+):
+    _, rows = x_ref.shape
     columns = y_ref.shape[1]
     block = min(512, columns)
-    x = x_ref[...].astype(jnp.float32)
-    far_ref[...] = scale * jnp.sum(jnp.square(x), axis=0, keepdims=True)
-    left[...] = jnp.concatenate([*pieces(x * (2.0 * scale)), ones_rows(rows)], axis=0).T
-    for start in range(0, columns, block):
-        piece = y_ref[:, start : start + block]
+    starts = range(0, columns, block)
+    copies = [pltpu.make_async_copy(x_hbm, x_ref, sems.at[0])]
+    for at, start in enumerate(starts):
+        span = slice(start, start + block)
+        copies.append(pltpu.make_async_copy(y_hbm.at[:, span], y_ref.at[:, span], sems.at[1 + at]))
+    for copy in copies:
+        copy.start()
+    copies[0].wait()
+    x = x_ref[...]
+    far_ref[...] = scale * jnp.sum(jnp.square(x.astype(jnp.float32)), axis=0, keepdims=True)
+    left[...] = jnp.concatenate([x, ones_rows(rows)], axis=0).T
+    for at, start in enumerate(starts):
+        span = slice(start, start + block)
+        copies[1 + at].wait()
+        piece = y_ref[:, span]
         near = jnp.sum(jnp.square(piece.astype(jnp.float32)), axis=0, keepdims=True)
-        right[:, start : start + block] = jnp.concatenate(
-            [piece, piece, piece, pad_rows(pieces(-scale * near))], axis=0
-        )
-    for start in range(0, columns, block):
-        part = jnp.dot(
-            left[...], right[:, start : start + block], preferred_element_type=jnp.float32
-        )
-        logits[:, start : start + block] = part
+        right[:, span] = jnp.concatenate([piece, pad_rows(pieces(-0.5 * near))], axis=0)
+        part = jnp.dot(left[...], right[:, span], preferred_element_type=jnp.float32)
+        part = part * (2.0 * scale)
+        logits[:, span] = part
         top = functools.reduce(jnp.maximum, [part[:, tile] for tile in lane_tiles(block)])
         tops[...] = top if start == 0 else jnp.maximum(tops[...], top)
     height = min(64, rows)
@@ -79,18 +87,18 @@
 
 
 def second_kernel(scale, points, x_ref, phi_ref, y_ref, e_ref, r_ref, base_ref, left, right, part_r):
-    dims, cells = x_ref.shape
     columns = y_ref.shape[1]
     block = min(512, columns)
-    wide = x_ref[...] * (2.0 * scale)
-    left[...] = jnp.concatenate([*pieces(wide), pad_rows(pieces(phi_ref[...]))], axis=0).T
+    shift = pad_rows(pieces(phi_ref[...] * (0.5 / scale)))
+    left[...] = jnp.concatenate([x_ref[...].astype(jnp.bfloat16), shift], axis=0).T
     y = y_ref[...]
-    right[...] = jnp.concatenate([y, y, y, ones_rows(columns)], axis=0)
+    right[...] = jnp.concatenate([y, ones_rows(columns)], axis=0)
     near = jnp.sum(jnp.square(y.astype(jnp.float32)), axis=0, keepdims=True)
     base_ref[...] = scale * near - math.log2(points)
     for start in range(0, columns, block):
         span = slice(start, start + block)
         part = jnp.dot(left[...], right[:, span], preferred_element_type=jnp.float32)
+        part = part * (2.0 * scale)
         e_ref[:, span] = part
         peak = jnp.max(part, axis=0, keepdims=True)
         base_ref[:, span] = base_ref[:, span] - peak
@@ -110,45 +118,59 @@
     out_ref[:, rows:] = own_ref[:, rows:] + other_ref[:, :rows]
 
 
-def third_kernel(key, count, x_ref, e_ref, base_ref, *refs):
-    *r_refs, out_ref, g_ref, tall = refs
-    dims, cells = x_ref.shape
+def split_kernel(e_ref, after_ref, high_ref, low_ref):
+    del after_ref
+    for tile in lane_tiles(e_ref.shape[1]):
+        e = e_ref[:, tile]
+        high = e.astype(jnp.bfloat16)
+        high_ref[:, tile] = high
+        low_ref[:, tile] = (e - high.astype(jnp.float32)).astype(jnp.bfloat16)
+
+
+def weights_kernel(count, x_ref, *refs):
+    *r_refs, out_ref = refs
+    w = 1.0 / (count * functools.reduce(jnp.add, [ref[...] for ref in r_refs]))
+    wide = x_ref[...] * w
+    high = wide.astype(jnp.bfloat16)
+    low = (wide - high.astype(jnp.float32)).astype(jnp.bfloat16)
+    out_ref[...] = jnp.concatenate([high, pad_rows(pieces(w)), low], axis=0)
+
+
+def third_kernel(key, dims, weights_ref, high_ref, low_ref, base_ref, out_ref, g_ref):
     width = out_ref.shape[1]
     start = 0
     if key is not None:
         start = pl.multiple_of((lax.axis_index("atlas") ^ key) * width, LANES)
-    rows = lax.broadcasted_iota(jnp.int32, (16, cells), 0)
-    ones = jnp.where(rows == 0, 1.0, 0.0).astype(jnp.bfloat16)
-    x = jnp.concatenate([x_ref[...].astype(jnp.bfloat16), ones], axis=0)
-    total = functools.reduce(jnp.add, [ref[...] for ref in r_refs])
-    tall[...] = jnp.broadcast_to(1.0 / (count * total), (LANES, cells)).T
-    q = e_ref[:, pl.ds(start, width)] * jnp.concatenate([tall[...]] * (width // LANES), axis=1)
-    high = q.astype(jnp.bfloat16)
-    low = (q - high.astype(jnp.float32)).astype(jnp.bfloat16)
-    moved = jnp.dot(x, high, preferred_element_type=jnp.float32)
-    moved = moved + jnp.dot(x, low, preferred_element_type=jnp.float32)
-    mass = moved[dims : dims + 1, :]
-    out_ref[...] = moved[:dims, :] / mass
-    g_ref[...] = (blur / LOG2E) * (base_ref[:, pl.ds(start, width)] - jnp.log2(mass))
+    span = pl.ds(start, width)
+    upper = dims + 16
+    moved = jnp.dot(weights_ref[...], high_ref[:, span], preferred_element_type=jnp.float32)
+    rest = jnp.dot(weights_ref[:upper, :], low_ref[:, span], preferred_element_type=jnp.float32)
+    mass = jnp.sum(moved[dims:upper, :] + rest[dims:upper, :], axis=0, keepdims=True)
+    out_ref[...] = (moved[:dims, :] + moved[upper:, :] + rest[:dims, :]) / mass
+    g_ref[...] = (blur / LOG2E) * (base_ref[:, span] - jnp.log2(mass))
 
 
 def assemble_kernel(atlases, *refs):
     own, other, g_own, g_other = refs[:atlases], refs[atlases : 2 * atlases], *refs[2 * atlases : 2 * atlases + 2]
-    out_ref, g_ref, sems = refs[2 * atlases + 2 :]
-    width = own[0].shape[1]
+    out_ref, g_ref, image, sems = refs[2 * atlases + 2 :]
+    dims, width = own[0].shape
     atlas = lax.axis_index("atlas")
     row = lax.axis_index("row")
-    copies = []
+    places = []
     for half, slabs, duals in ((row, own, g_own), (1 - row, other, g_other)):
         for key in range(atlases):
             start = pl.multiple_of((half * atlases + (atlas ^ key)) * width, LANES)
-            copies.append(
-                pltpu.make_async_copy(
-                    slabs[key], out_ref.at[:, pl.ds(start, width)], sems.at[len(copies)]
-                )
-            )
-            copies[-1].start()
+            places.append((slabs[key], start))
             g_ref[:, pl.ds(start, width)] = duals[:, key * width : (key + 1) * width]
+    copies = []
+    for low in range(0, dims, SUBLANES):
+        rows = slice(low, low + SUBLANES)
+        for slab, start in places:
+            image[rows, pl.ds(start, width)] = slab[rows, :]
+        copies.append(
+            pltpu.make_async_copy(image.at[rows, :], out_ref.at[rows, :], sems.at[len(copies)])
+        )
+        copies[-1].start()
     for copy in copies:
         copy.wait()
 
@@ -207,7 +229,7 @@
 
     everyone = gather_rows(own.astype(jnp.float32))
     mine = lax.dynamic_slice_in_dim(support, row_at * share, share, 1)
-    depth = 3 * dims + 16
+    depth = dims + 16
 
     def row_vector(width):
         return jax.ShapeDtypeStruct((1, width), jnp.float32)
@@ -215,16 +237,19 @@
     lam, far = pl.pallas_call(
         functools.partial(first_kernel, scale),
         out_shape=(row_vector(rows), row_vector(rows)),
-        in_specs=[VMEM, VMEM],
+        in_specs=[HBM, HBM],
         out_specs=(VMEM, VMEM),
         scratch_shapes=[
+            pltpu.VMEM((dims, rows), jnp.bfloat16),
+            pltpu.VMEM((dims, columns), jnp.bfloat16),
             pltpu.VMEM((rows, depth), jnp.bfloat16),
             pltpu.VMEM((depth, columns), jnp.bfloat16),
             pltpu.VMEM((rows, columns), jnp.float32),
             pltpu.VMEM((rows, LANES), jnp.float32),
             pltpu.VMEM((rows, LANES), jnp.float32),
+            pltpu.SemaphoreType.DMA((1 + columns // min(512, columns),)),
         ],
-        compiler_params=pltpu.CompilerParams(vmem_limit_bytes=24 << 20),
+        compiler_params=pltpu.CompilerParams(vmem_limit_bytes=56_510_000),
         name="first",
     )(own, support)
 
@@ -254,21 +279,43 @@
     r = sum_rows(r)
     shares = [r, *partners(r, "col")]
 
+    high, low = pl.pallas_call(
+        split_kernel,
+        out_shape=(jax.ShapeDtypeStruct(e.shape, jnp.bfloat16),) * 2,
+        in_specs=[VMEM, VMEM],
+        out_specs=(VMEM, VMEM),
+        compiler_params=pltpu.CompilerParams(vmem_limit_bytes=24 << 20),
+        cost_estimate=pl.CostEstimate(flops=e.size * 4, bytes_accessed=e.size * 8, transcendentals=0),
+        name="split",
+    )(e, r)
+    weights = pl.pallas_call(
+        functools.partial(weights_kernel, float(total_cells)),
+        out_shape=jax.ShapeDtypeStruct((2 * dims + 16, total_cells), jnp.bfloat16),
+        in_specs=[VMEM] * (1 + len(shares)),
+        out_specs=VMEM,
+        compiler_params=pltpu.CompilerParams(vmem_limit_bytes=16 << 20),
+        name="weights",
+    )(everyone, *shares)
+
     def third(key, width):
         return pl.pallas_call(
-            functools.partial(third_kernel, key, float(total_cells)),
+            functools.partial(third_kernel, key, dims),
             out_shape=(jax.ShapeDtypeStruct((dims, width), jnp.float32), row_vector(width)),
-            in_specs=[VMEM] * (3 + len(shares)),
+            in_specs=[VMEM] * 4,
             out_specs=(VMEM, VMEM),
-            scratch_shapes=[pltpu.VMEM((total_cells, LANES), jnp.float32)],
-            compiler_params=pltpu.CompilerParams(vmem_limit_bytes=24 << 20),
+            compiler_params=pltpu.CompilerParams(vmem_limit_bytes=16 << 20),
+            cost_estimate=pl.CostEstimate(
+                flops=2 * (3 * dims + 32) * total_cells * width,
+                bytes_accessed=4 * total_cells * width,
+                transcendentals=0,
+            ),
             name="third",
-        )(everyone, e, base, *shares)
+        )(weights, high, low, base)
 
     piece = share // atlases
     if paired and atlases & (atlases - 1) == 0 and atlases <= 8 and piece % LANES == 0:
 
-        order = sorted(range(atlases), key=lambda key: (key == 0, -key))
+        order = [*range(1, atlases), 0]
         terms, duals, arrived = [None] * atlases, [None] * atlases, []
         for key in order:
             terms[key], duals[key] = third(key, piece)
@@ -281,8 +328,11 @@
             functools.partial(assemble_kernel, atlases),
             out_shape=(jax.ShapeDtypeStruct((dims, columns), jnp.float32), row_vector(columns)),
             in_specs=[VMEM] * (2 * atlases + 2),
-            out_specs=(pl.BlockSpec(memory_space=pl.ANY), VMEM),
-            scratch_shapes=[pltpu.SemaphoreType.DMA((2 * atlases,))],
+            out_specs=(HBM, VMEM),
+            scratch_shapes=[
+                pltpu.VMEM((dims, columns), jnp.float32),
+                pltpu.SemaphoreType.DMA((dims // SUBLANES,)),
+            ],
             compiler_params=pltpu.CompilerParams(vmem_limit_bytes=8 << 20),
             name="assemble",
         )(

time: 47.6 us -> 50.2 us (1.055)
  Pallas kernels: 9.84 us -> 14.5 us
  local copies, waits for them, and re-layouts: 2.88 us -> 1 us
  other arithmetic: 0.71 us -> 1.54 us
  waiting for transfers between devices: 14.2 us -> 13.4 us
    pallas_call x1, Pallas kernels: 2.42 us -> 4.53 us  [shards(): pl.pallas_call(functools.partial(first_kernel, scale), out_shape=(row_vec...]
    pallas_call x4 -> x6, Pallas kernels: 2.89 us -> 4.83 us  [the longest x1 2.66 us: shards(): pl.pallas_call(split_kernel, out_shape=(jax.ShapeDtypeStruct(e.shape, jnp...]
    unnamed x7 -> x3, local copies, waits for them, and re-layouts: 1.89 us -> 0.02 us
    convert_element_type x1, other arithmetic: 0.01 us -> 0.85 us  [shards(): everyone = gather_rows(own.astype(jnp.float32))]
    ppermute x20, waiting for transfers between devices: 14.2 us -> 13.4 us  [exchange(): return lax.ppermute(value, axis, [(at, at ^ key) for at in range(size)])]
    pallas_call x1, Pallas kernels: 2.9 us -> 3.44 us  [shards(): pl.pallas_call(functools.partial(second_kernel, scale, float(total_suppor...]
  transfers between devices with their start and end apart: 20 -> 20, of which waited for: 13 -> 10; matrix products, arithmetic and copies ran while one was open for 3% -> 5% of each run, Pallas kernels for 5% -> 5%
where the time goes in v3:
time: 50.2 us; the launch traced here: 50 us
  starting transfers between devices  18.8 us (37%)
  Pallas kernels  14.5 us (29%)
  waiting for transfers between devices  13.4 us (27%)
  other arithmetic  1.54 us (3%)
  local copies, waits for them, and re-layouts  1 us (2%)
  between operations  0.78 us (2%)
    ppermute x20, starting transfers between devices, exchange(): return lax.ppermute(value, axis, [(at, at ^ key) for at in range(size)])  18.8 us
    ppermute x20, waiting for transfers between devices, exchange(): return lax.ppermute(value, axis, [(at, at ^ key) for at in range(size)])  13.4 us
    pallas_call x1, Pallas kernels, shards(): pl.pallas_call(functools.partial(first_kernel, scale), out_shape=(row_vec...  4.53 us
    pallas_call x1, Pallas kernels, shards(): pl.pallas_call(functools.partial(second_kernel, scale, float(total_suppor...  3.44 us
    pallas_call x1, Pallas kernels, shards(): pl.pallas_call(split_kernel, out_shape=(jax.ShapeDtypeStruct(e.shape, jnp...  2.66 us
    pallas_call x4, Pallas kernels, third(): pl.pallas_call(functools.partial(third_kernel, key, dims), out_shape=(jax...  2.09 us
    pallas_call x1, Pallas kernels, shards(): pl.pallas_call(functools.partial(assemble_kernel, atlases), out_shape=(ja...  1.65 us
  transfers between devices with their start and end apart: 20, of which 10 were waited for; matrix products, arithmetic and copies ran while one was open for 5% of the time, Pallas kernels for 5%

profile of v3, /device:TPU:0, one launch (start us, length us, event | category | flops | bytes accessed | tf_op | source)
XLA Modules:
  0.0 50.0 jit_solution(15848840357213136340)
XLA Ops:
  0.6 4.5 %first.1 = (f32[1,512]{1,0:T(1,128)S(1)}, f32[1,512]{1,0:T(1,128)S(1)}) custom-call(bf16[64,512]{1,0:T(8,128)(2,1)} %bitcast.2, bf16[64,4096]{1,0:T(8,128)(2,1)} %y_hbm.1), custom_call_target="tpu_custom_call" | custom-call | tf_op jit(solution)/shard_map/first/pallas_call | solution.py:237
  5.2 5.1 %collective-permute-start.2 = (f32[1,512]{1,0:T(1,128)S(1)}, f32[1,512]{1,0:T(1,128)S(1)}, u32[]{:S(2)}, u32[]{:S(2)}) collective-permute-start(f32[1,512]{1,0:T(1,128)S(1)} %get-tuple-element.20), channel_id=1, source_target_pairs={{0,3},{1,2},{2,1},{3,0},{4,7},{5,6},{6,5},{7,4},{8,11},{9,10},{10,... | collective-permute-start | bytes 6152 | tf_op jit(solution)/shard_map/ppermute | solution.py:179
  10.3 0.6 %collective-permute-start = (f32[1,512]{1,0:T(1,128)S(1)}, f32[1,512]{1,0:T(1,128)S(1)}, u32[]{:S(2)}, u32[]{:S(2)}) collective-permute-start(f32[1,512]{1,0:T(1,128)S(1)} %get-tuple-element.20), channel_id=1, source_target_pairs={{0,1},{1,0},{2,3},{3,2},{4,5},{5,4},{6,7},{7,6},{8,9},{9,8},{10,11... | collective-permute-start | bytes 6152 | tf_op jit(solution)/shard_map/ppermute | solution.py:179
  11.0 0.8 %bitcast_convert_fusion = f32[64,512]{1,0:T(8,128)S(1)} fusion(bf16[1,64,512]{2,1,0:T(8,128)(2,1)} %param.2), kind=kLoop, calls=%fused_computation.14 | loop fusion | flops 32768 | bytes 196608 | tf_op jit(solution)/shard_map/convert_element_type | solution.py:230
  11.9 2.9 %collective-permute-done.1 = f32[1,512]{1,0:T(1,128)S(1)} collective-permute-done((f32[1,512]{1,0:T(1,128)S(1)}, f32[1,512]{1,0:T(1,128)S(1)}, u32[]{:S(2)}, u32[]{:S(2)}) %collective-permute-start.1) | collective-permute-done | bytes 2080 | tf_op jit(solution)/shard_map/ppermute | solution.py:179
  14.9 1.0 %constant_dynamic-slice_fusion.y_ref = bf16[64,2048]{1,0:T(8,128)(2,1)S(1)} fusion(bf16[64,4096]{1,0:T(8,128)(2,1)} %y_hbm.1, s32[]{:T(128)S(6)} %select_n.3), kind=kLoop, calls=%fused_computation.13 | loop fusion | bytes 524292 | tf_op jit(solution)/shard_map/dynamic_slice | solution.py:231
  16.1 3.4 %second.1 = (f32[1024,2048]{1,0:T(8,128)S(1)}, f32[1,1024]{1,0:T(1,128)S(1)}, f32[1,2048]{1,0:T(1,128)S(1)}) custom-call(f32[64,1024]{1,0:T(8,128)S(1)} %pad_maximum_fusion.x_ref, f32[1,1024]{1,0:T(1,128)S(1)} %pad_maximum_fusion.1.phi_ref, bf16[64,2048]{1,0:T(8,128)(2,1)S(1)} %constant_dynamic-slice_fusion.y_ref), custom_call_target="tpu_custom_call" | custom-call | tf_op jit(solution)/shard_map/second/pallas_call | solution.py:261
  19.5 0.4 collective-permute-start.5
  19.9 0.8 %collective-permute-done.5.other_ref = f32[1,1024]{1,0:T(1,128)S(1)} collective-permute-done((f32[1,1024]{1,0:T(1,128)S(1)}, f32[1,1024]{1,0:T(1,128)S(1)}, u32[]{:S(2)}, u32[]{:S(2)}) %collective-permute-start.5) | collective-permute-done | bytes 4128 | tf_op jit(solution)/shard_map/ppermute | solution.py:179
  20.8 1.5 %collective-permute-start.8 = (f32[1,1024]{1,0:T(1,128)S(1)}, f32[1,1024]{1,0:T(1,128)S(1)}, u32[]{:S(2)}, u32[]{:S(2)}) collective-permute-start(f32[1,1024]{1,0:T(1,128)S(1)} %meet.1.refs_0_.after_ref), channel_id=1, source_target_pairs={{0,3},{1,2},{2,1},{3,0},{4,7},{5,6},{6,5},{7,4},{8,11},{9,10},{10,... | collective-permute-start | bytes 12296 | tf_op jit(solution)/shard_map/ppermute | solution.py:179
  22.2 0.6 %collective-permute-start.7 = (f32[1,1024]{1,0:T(1,128)S(1)}, f32[1,1024]{1,0:T(1,128)S(1)}, u32[]{:S(2)}, u32[]{:S(2)}) collective-permute-start(f32[1,1024]{1,0:T(1,128)S(1)} %meet.1.refs_0_.after_ref), channel_id=1, source_target_pairs={{0,2},{1,3},{2,0},{3,1},{4,6},{5,7},{6,4},{7,5},{8,10},{9,11},{10,... | collective-permute-start | bytes 12296 | tf_op jit(solution)/shard_map/ppermute | solution.py:179
  22.9 2.3 %collective-permute-start.6 = (f32[1,1024]{1,0:T(1,128)S(1)}, f32[1,1024]{1,0:T(1,128)S(1)}, u32[]{:S(2)}, u32[]{:S(2)}) collective-permute-start(f32[1,1024]{1,0:T(1,128)S(1)} %meet.1.refs_0_.after_ref), channel_id=1, source_target_pairs={{0,1},{1,0},{2,3},{3,2},{4,5},{5,4},{6,7},{7,6},{8,9},{9,8},{10,11... | collective-permute-start | bytes 12296 | tf_op jit(solution)/shard_map/ppermute | solution.py:179
  25.2 2.7 %split.1 = (bf16[1024,2048]{1,0:T(8,128)(2,1)S(1)}, bf16[1024,2048]{1,0:T(8,128)(2,1)S(1)}) custom-call(f32[1024,2048]{1,0:T(8,128)S(1)} %get-tuple-element.23.e_ref, f32[1,1024]{1,0:T(1,128)S(1)} %meet.1.refs_0_.after_ref), custom_call_target="tpu_custom_call" | custom-call | flops 8388608 | bytes 16777216 | tf_op jit(solution)/shard_map/split/pallas_call | solution.py:282
  28.0 0.5 %third.7 = (f32[64,512]{1,0:T(8,128)S(1)}, f32[1,512]{1,0:T(1,128)S(1)}) custom-call(bf16[144,1024]{1,0:T(8,128)(2,1)S(1)} %weights.1.weights_ref, bf16[1024,2048]{1,0:T(8,128)(2,1)S(1)} %get-tuple-element.24.high_ref, bf16[1024,2048]{1,0:T(8,128)(2,1)S(1)} %get-tuple-element.25.low_ref, f32[1,2048]{1,0:T(1,128)S(1)} %get-tuple-element.26.base_ref), custom_call_target="tpu_custom_call" | custom-call | flops 234881024 | bytes 2097152 | tf_op jit(solution)/shard_map/third/pallas_call | solution.py:301
  28.5 0.5 %third.6 = (f32[64,512]{1,0:T(8,128)S(1)}, f32[1,512]{1,0:T(1,128)S(1)}) custom-call(bf16[144,1024]{1,0:T(8,128)(2,1)S(1)} %weights.1.weights_ref, bf16[1024,2048]{1,0:T(8,128)(2,1)S(1)} %get-tuple-element.24.high_ref, bf16[1024,2048]{1,0:T(8,128)(2,1)S(1)} %get-tuple-element.25.low_ref, f32[1,2048]{1,0:T(1,128)S(1)} %get-tuple-element.26.base_ref), custom_call_target="tpu_custom_call" | custom-call | flops 234881024 | bytes 2097152 | tf_op jit(solution)/shard_map/third/pallas_call | solution.py:301
  29.0 0.5 %third.5 = (f32[64,512]{1,0:T(8,128)S(1)}, f32[1,512]{1,0:T(1,128)S(1)}) custom-call(bf16[144,1024]{1,0:T(8,128)(2,1)S(1)} %weights.1.weights_ref, bf16[1024,2048]{1,0:T(8,128)(2,1)S(1)} %get-tuple-element.24.high_ref, bf16[1024,2048]{1,0:T(8,128)(2,1)S(1)} %get-tuple-element.25.low_ref, f32[1,2048]{1,0:T(1,128)S(1)} %get-tuple-element.26.base_ref), custom_call_target="tpu_custom_call" | custom-call | flops 234881024 | bytes 2097152 | tf_op jit(solution)/shard_map/third/pallas_call | solution.py:301
  29.5 0.5 %third.4 = (f32[64,512]{1,0:T(8,128)S(1)}, f32[1,512]{1,0:T(1,128)S(1)}) custom-call(bf16[144,1024]{1,0:T(8,128)(2,1)S(1)} %weights.1.weights_ref, bf16[1024,2048]{1,0:T(8,128)(2,1)S(1)} %get-tuple-element.24.high_ref, bf16[1024,2048]{1,0:T(8,128)(2,1)S(1)} %get-tuple-element.25.low_ref, f32[1,2048]{1,0:T(1,128)S(1)} %get-tuple-element.26.base_ref), custom_call_target="tpu_custom_call" | custom-call | flops 234881024 | bytes 2097152 | tf_op jit(solution)/shard_map/third/pallas_call | solution.py:301
  30.1 1.6 %collective-permute-start.9 = (f32[64,512]{1,0:T(8,128)S(1)}, f32[64,512]{1,0:T(8,128)S(1)}, u32[]{:S(2)}, u32[]{:S(2)}) collective-permute-start(f32[64,512]{1,0:T(8,128)S(1)} %get-tuple-element.28), channel_id=1, source_target_pairs={{0,8},{8,0},{16,24},{24,16},{1,9},{9,1},{17,25},{25,17},{2,10},{10... | collective-permute-start | bytes 393224 | tf_op jit(solution)/shard_map/ppermute | solution.py:179
  31.6 1.5 %collective-permute-start.10 = (f32[64,512]{1,0:T(8,128)S(1)}, f32[64,512]{1,0:T(8,128)S(1)}, u32[]{:S(2)}, u32[]{:S(2)}) collective-permute-start(f32[64,512]{1,0:T(8,128)S(1)} %get-tuple-element.29), channel_id=1, source_target_pairs={{0,16},{8,24},{16,0},{24,8},{1,17},{9,25},{17,1},{25,9},{2,18},{10... | collective-permute-start | bytes 393224 | tf_op jit(solution)/shard_map/ppermute | solution.py:179
  33.2 0.5 collective-permute-start.11
  33.6 1.9 %collective-permute-done.9 = f32[64,512]{1,0:T(8,128)S(1)} collective-permute-done((f32[64,512]{1,0:T(8,128)S(1)}, f32[64,512]{1,0:T(8,128)S(1)}, u32[]{:S(2)}, u32[]{:S(2)}) %collective-permute-start.9) | collective-permute-done | bytes 131104 | tf_op jit(solution)/shard_map/ppermute | solution.py:179
  35.6 3.8 %collective-permute-done.10 = f32[64,512]{1,0:T(8,128)S(1)} collective-permute-done((f32[64,512]{1,0:T(8,128)S(1)}, f32[64,512]{1,0:T(8,128)S(1)}, u32[]{:S(2)}, u32[]{:S(2)}) %collective-permute-start.10) | collective-permute-done | bytes 131104 | tf_op jit(solution)/shard_map/ppermute | solution.py:179
  39.5 1.2 %collective-permute-start.14 = (f32[64,512]{1,0:T(8,128)S(1)}, f32[64,512]{1,0:T(8,128)S(1)}, u32[]{:S(2)}, u32[]{:S(2)}) collective-permute-start(f32[64,512]{1,0:T(8,128)S(1)} %add_multiply_fusion.refs_0_), channel_id=1, source_target_pairs={{0,24},{8,16},{16,8},{24,0},{1,25},{9,17},{17,9},{25,1},{2,26},{10... | collective-permute-start | bytes 393224 | tf_op jit(solution)/shard_map/ppermute | solution.py:179
  40.7 1.2 %collective-permute-start.13 = (f32[64,512]{1,0:T(8,128)S(1)}, f32[64,512]{1,0:T(8,128)S(1)}, u32[]{:S(2)}, u32[]{:S(2)}) collective-permute-start(f32[64,512]{1,0:T(8,128)S(1)} %add_multiply_fusion.refs_0_), channel_id=1, source_target_pairs={{0,16},{8,24},{16,0},{24,8},{1,17},{9,25},{17,1},{25,9},{2,18},{10... | collective-permute-start | bytes 393224 | tf_op jit(solution)/shard_map/ppermute | solution.py:179
  41.9 1.1 %collective-permute-start.12 = (f32[64,512]{1,0:T(8,128)S(1)}, f32[64,512]{1,0:T(8,128)S(1)}, u32[]{:S(2)}, u32[]{:S(2)}) collective-permute-start(f32[64,512]{1,0:T(8,128)S(1)} %add_multiply_fusion.refs_0_), channel_id=1, source_target_pairs={{0,8},{8,0},{16,24},{24,16},{1,9},{9,1},{17,25},{25,17},{2,10},{10... | collective-permute-start | bytes 393224 | tf_op jit(solution)/shard_map/ppermute | solution.py:179
  43.0 0.5 %collective-permute-start.15 = (f32[64,512]{1,0:T(8,128)S(1)}, f32[64,512]{1,0:T(8,128)S(1)}, u32[]{:S(2)}, u32[]{:S(2)}) collective-permute-start(f32[64,512]{1,0:T(8,128)S(1)} %add_multiply_fusion.refs_0_), channel_id=1, source_target_pairs={{0,4},{4,0},{1,5},{5,1},{2,6},{6,2},{3,7},{7,3},{8,12},{12,8},{9,1... | collective-permute-start | bytes 393224 | tf_op jit(solution)/shard_map/ppermute | solution.py:179
  43.5 1.9 %collective-permute-done.14.refs_3_ = f32[64,512]{1,0:T(8,128)S(1)} collective-permute-done((f32[64,512]{1,0:T(8,128)S(1)}, f32[64,512]{1,0:T(8,128)S(1)}, u32[]{:S(2)}, u32[]{:S(2)}) %collective-permute-start.14) | collective-permute-done | bytes 131104 | tf_op jit(solution)/shard_map/ppermute | solution.py:179
  45.5 1.3 %collective-permute-done.13.refs_2_ = f32[64,512]{1,0:T(8,128)S(1)} collective-permute-done((f32[64,512]{1,0:T(8,128)S(1)}, f32[64,512]{1,0:T(8,128)S(1)}, u32[]{:S(2)}, u32[]{:S(2)}) %collective-permute-start.13) | collective-permute-done | bytes 131104 | tf_op jit(solution)/shard_map/ppermute | solution.py:179
  46.9 0.4 collective-permute-start.16
  47.3 0.6 %subtract_multiply_fusion = f32[1,512]{1,0:T(1,128)} fusion(f32[1,512]{1,0:T(1,128)S(1)} %add_subtract_fusion, f32[1,512]{1,0:T(1,128)S(1)} %get-tuple-element.21, f32[1,1024]{1,0:T(1,128)S(1)} %collective-permute-done.8.refs_3_, f32[1,1024]{1,0:T(1,128)S(1)} %collective-permute-done.7.refs_2_, f32[1,1024]{1,0:T(1,128)S(1)} %collective-permute-done.6.refs_1_, ...), kind=kLoop, calls=%fused_computation.11 | loop fusion | flops 4096 | bytes 14336 | tf_op jit(solution)/shard_map/mul | solution.py:349
  47.9 0.2 collective-permute-done.17.refs_6_
  48.3 1.7 %assemble.1 = (f32[64,4096]{1,0:T(8,128)}, f32[1,4096]{1,0:T(1,128)}) custom-call(f32[64,512]{1,0:T(8,128)S(1)} %add_multiply_fusion.refs_0_, f32[64,512]{1,0:T(8,128)S(1)} %collective-permute-done.12.refs_1_, f32[64,512]{1,0:T(8,128)S(1)} %collective-permute-done.13.refs_2_, f32[64,512]{1,0:T(8,128)S(1)} %collective-permute-done.14.refs_3_, ...), custom_call_target="tpu_custom_call" | custom-call | tf_op jit(solution)/shard_map/assemble/pallas_call | solution.py:327
  (29 shorter events, 0.8 us)
Async XLA Ops:
  5.2 6.7 %collective-permute-start.2 = (f32[1,512]{1,0:T(1,128)S(1)}, f32[1,512]{1,0:T(1,128)S(1)}, u32[]{:S(2)}, u32[]{:S(2)}) collective-permute-start(f32[1,512]{1,0:T(1,128)S(1)} %get-tuple-element.20), channel_id=1, source_target_pairs={{0,3},{1,2},{2,1},{3,0},{4,7},{5,6},{6,5},{7,4},{8,11},{9,10},{10,... | collective-permute-start | bytes 6152 | tf_op jit(solution)/shard_map/ppermute | solution.py:179
  10.3 4.5 %collective-permute-start.1 = (f32[1,512]{1,0:T(1,128)S(1)}, f32[1,512]{1,0:T(1,128)S(1)}, u32[]{:S(2)}, u32[]{:S(2)}) collective-permute-start(f32[1,512]{1,0:T(1,128)S(1)} %get-tuple-element.20), channel_id=1, source_target_pairs={{0,2},{1,3},{2,0},{3,1},{4,6},{5,7},{6,4},{7,5},{8,10},{9,11},{10,... | collective-permute-start | bytes 6152 | tf_op jit(solution)/shard_map/ppermute | solution.py:179
  10.3 4.5 %collective-permute-start = (f32[1,512]{1,0:T(1,128)S(1)}, f32[1,512]{1,0:T(1,128)S(1)}, u32[]{:S(2)}, u32[]{:S(2)}) collective-permute-start(f32[1,512]{1,0:T(1,128)S(1)} %get-tuple-element.20), channel_id=1, source_target_pairs={{0,1},{1,0},{2,3},{3,2},{4,5},{5,4},{6,7},{7,6},{8,9},{9,8},{10,11... | collective-permute-start | bytes 6152 | tf_op jit(solution)/shard_map/ppermute | solution.py:179
  11.8 4.3 %collective-permute-start.3 = (f32[64,512]{1,0:T(8,128)S(1)}, f32[64,512]{1,0:T(8,128)S(1)}, u32[]{:S(2)}, u32[]{:S(2)}) collective-permute-start(f32[64,512]{1,0:T(8,128)S(1)} %bitcast_convert_fusion), channel_id=1, source_target_pairs={{0,4},{4,0},{1,5},{5,1},{2,6},{6,2},{3,7},{7,3},{8,12},{12,8},{9,1... | collective-permute-start | bytes 393224 | tf_op jit(solution)/shard_map/ppermute | solution.py:179
  14.8 1.2 %collective-permute-start.4 = (f32[1,512]{1,0:T(1,128)S(1)}, f32[1,512]{1,0:T(1,128)S(1)}, u32[]{:S(2)}, u32[]{:S(2)}) collective-permute-start(f32[1,512]{1,0:T(1,128)S(1)} %add_subtract_fusion), channel_id=1, source_target_pairs={{0,4},{4,0},{1,5},{5,1},{2,6},{6,2},{3,7},{7,3},{8,12},{12,8},{9,1... | collective-permute-start | bytes 6152 | tf_op jit(solution)/shard_map/ppermute | solution.py:179
  19.5 1.2 %collective-permute-start.5 = (f32[1,1024]{1,0:T(1,128)S(1)}, f32[1,1024]{1,0:T(1,128)S(1)}, u32[]{:S(2)}, u32[]{:S(2)}) collective-permute-start(f32[1,1024]{1,0:T(1,128)S(1)} %get-tuple-element.22.own_ref), channel_id=1, source_target_pairs={{0,4},{4,0},{1,5},{5,1},{2,6},{6,2},{3,7},{7,3},{8,12},{12,8},{9,1... | collective-permute-start | bytes 12296 | tf_op jit(solution)/shard_map/ppermute | solution.py:179
  20.8 7.1 %collective-permute-start.8 = (f32[1,1024]{1,0:T(1,128)S(1)}, f32[1,1024]{1,0:T(1,128)S(1)}, u32[]{:S(2)}, u32[]{:S(2)}) collective-permute-start(f32[1,1024]{1,0:T(1,128)S(1)} %meet.1.refs_0_.after_ref), channel_id=1, source_target_pairs={{0,3},{1,2},{2,1},{3,0},{4,7},{5,6},{6,5},{7,4},{8,11},{9,10},{10,... | collective-permute-start | bytes 12296 | tf_op jit(solution)/shard_map/ppermute | solution.py:179
  22.2 5.6 %collective-permute-start.7 = (f32[1,1024]{1,0:T(1,128)S(1)}, f32[1,1024]{1,0:T(1,128)S(1)}, u32[]{:S(2)}, u32[]{:S(2)}) collective-permute-start(f32[1,1024]{1,0:T(1,128)S(1)} %meet.1.refs_0_.after_ref), channel_id=1, source_target_pairs={{0,2},{1,3},{2,0},{3,1},{4,6},{5,7},{6,4},{7,5},{8,10},{9,11},{10,... | collective-permute-start | bytes 12296 | tf_op jit(solution)/shard_map/ppermute | solution.py:179
  22.9 5.0 %collective-permute-start.6 = (f32[1,1024]{1,0:T(1,128)S(1)}, f32[1,1024]{1,0:T(1,128)S(1)}, u32[]{:S(2)}, u32[]{:S(2)}) collective-permute-start(f32[1,1024]{1,0:T(1,128)S(1)} %meet.1.refs_0_.after_ref), channel_id=1, source_target_pairs={{0,1},{1,0},{2,3},{3,2},{4,5},{5,4},{6,7},{7,6},{8,9},{9,8},{10,11... | collective-permute-start | bytes 12296 | tf_op jit(solution)/shard_map/ppermute | solution.py:179
  30.1 5.5 %collective-permute-start.9 = (f32[64,512]{1,0:T(8,128)S(1)}, f32[64,512]{1,0:T(8,128)S(1)}, u32[]{:S(2)}, u32[]{:S(2)}) collective-permute-start(f32[64,512]{1,0:T(8,128)S(1)} %get-tuple-element.28), channel_id=1, source_target_pairs={{0,8},{8,0},{16,24},{24,16},{1,9},{9,1},{17,25},{25,17},{2,10},{10... | collective-permute-start | bytes 393224 | tf_op jit(solution)/shard_map/ppermute | solution.py:179
  31.6 7.8 %collective-permute-start.10 = (f32[64,512]{1,0:T(8,128)S(1)}, f32[64,512]{1,0:T(8,128)S(1)}, u32[]{:S(2)}, u32[]{:S(2)}) collective-permute-start(f32[64,512]{1,0:T(8,128)S(1)} %get-tuple-element.29), channel_id=1, source_target_pairs={{0,16},{8,24},{16,0},{24,8},{1,17},{9,25},{17,1},{25,9},{2,18},{10... | collective-permute-start | bytes 393224 | tf_op jit(solution)/shard_map/ppermute | solution.py:179
  33.2 6.3 %collective-permute-start.11 = (f32[64,512]{1,0:T(8,128)S(1)}, f32[64,512]{1,0:T(8,128)S(1)}, u32[]{:S(2)}, u32[]{:S(2)}) collective-permute-start(f32[64,512]{1,0:T(8,128)S(1)} %get-tuple-element.30), channel_id=1, source_target_pairs={{0,24},{8,16},{16,8},{24,0},{1,25},{9,17},{17,9},{25,1},{2,26},{10... | collective-permute-start | bytes 393224 | tf_op jit(solution)/shard_map/ppermute | solution.py:179
  39.5 6.0 %collective-permute-start.14 = (f32[64,512]{1,0:T(8,128)S(1)}, f32[64,512]{1,0:T(8,128)S(1)}, u32[]{:S(2)}, u32[]{:S(2)}) collective-permute-start(f32[64,512]{1,0:T(8,128)S(1)} %add_multiply_fusion.refs_0_), channel_id=1, source_target_pairs={{0,24},{8,16},{16,8},{24,0},{1,25},{9,17},{17,9},{25,1},{2,26},{10... | collective-permute-start | bytes 393224 | tf_op jit(solution)/shard_map/ppermute | solution.py:179
  40.7 6.1 %collective-permute-start.13 = (f32[64,512]{1,0:T(8,128)S(1)}, f32[64,512]{1,0:T(8,128)S(1)}, u32[]{:S(2)}, u32[]{:S(2)}) collective-permute-start(f32[64,512]{1,0:T(8,128)S(1)} %add_multiply_fusion.refs_0_), channel_id=1, source_target_pairs={{0,16},{8,24},{16,0},{24,8},{1,17},{9,25},{17,1},{25,9},{2,18},{10... | collective-permute-start | bytes 393224 | tf_op jit(solution)/shard_map/ppermute | solution.py:179
  41.9 5.0 %collective-permute-start.12 = (f32[64,512]{1,0:T(8,128)S(1)}, f32[64,512]{1,0:T(8,128)S(1)}, u32[]{:S(2)}, u32[]{:S(2)}) collective-permute-start(f32[64,512]{1,0:T(8,128)S(1)} %add_multiply_fusion.refs_0_), channel_id=1, source_target_pairs={{0,8},{8,0},{16,24},{24,16},{1,9},{9,1},{17,25},{25,17},{2,10},{10... | collective-permute-start | bytes 393224 | tf_op jit(solution)/shard_map/ppermute | solution.py:179
  43.0 4.9 %collective-permute-start.19 = (f32[1,2048]{1,0:T(1,128)S(1)}, f32[1,2048]{1,0:T(1,128)S(1)}, u32[]{:S(2)}, u32[]{:S(2)}) collective-permute-start(f32[1,2048]{1,0:T(1,128)S(1)} %constant_dynamic-update-slice_fusion.refs_8_), channel_id=1, source_target_pairs={{0,4},{4,0},{1,5},{5,1},{2,6},{6,2},{3,7},{7,3},{8,12},{12,8},{9,1... | collective-permute-start | bytes 24584 | tf_op jit(solution)/shard_map/ppermute | solution.py:179
  43.0 4.9 %collective-permute-start.15 = (f32[64,512]{1,0:T(8,128)S(1)}, f32[64,512]{1,0:T(8,128)S(1)}, u32[]{:S(2)}, u32[]{:S(2)}) collective-permute-start(f32[64,512]{1,0:T(8,128)S(1)} %add_multiply_fusion.refs_0_), channel_id=1, source_target_pairs={{0,4},{4,0},{1,5},{5,1},{2,6},{6,2},{3,7},{7,3},{8,12},{12,8},{9,1... | collective-permute-start | bytes 393224 | tf_op jit(solution)/shard_map/ppermute | solution.py:179
  45.5 2.4 %collective-permute-start.18 = (f32[64,512]{1,0:T(8,128)S(1)}, f32[64,512]{1,0:T(8,128)S(1)}, u32[]{:S(2)}, u32[]{:S(2)}) collective-permute-start(f32[64,512]{1,0:T(8,128)S(1)} %collective-permute-done.14.refs_3_), channel_id=1, source_target_pairs={{0,4},{4,0},{1,5},{5,1},{2,6},{6,2},{3,7},{7,3},{8,12},{12,8},{9,1... | collective-permute-start | bytes 393224 | tf_op jit(solution)/shard_map/ppermute | solution.py:179
  46.8 1.3 %collective-permute-start.17 = (f32[64,512]{1,0:T(8,128)S(1)}, f32[64,512]{1,0:T(8,128)S(1)}, u32[]{:S(2)}, u32[]{:S(2)}) collective-permute-start(f32[64,512]{1,0:T(8,128)S(1)} %collective-permute-done.13.refs_2_), channel_id=1, source_target_pairs={{0,4},{4,0},{1,5},{5,1},{2,6},{6,2},{3,7},{7,3},{8,12},{12,8},{9,1... | collective-permute-start | bytes 393224 | tf_op jit(solution)/shard_map/ppermute | solution.py:179
  46.9 1.5 %collective-permute-start.16 = (f32[64,512]{1,0:T(8,128)S(1)}, f32[64,512]{1,0:T(8,128)S(1)}, u32[]{:S(2)}, u32[]{:S(2)}) collective-permute-start(f32[64,512]{1,0:T(8,128)S(1)} %collective-permute-done.12.refs_1_), channel_id=1, source_target_pairs={{0,4},{4,0},{1,5},{5,1},{2,6},{6,2},{3,7},{7,3},{8,12},{12,8},{9,1... | collective-permute-start | bytes 393224 | tf_op jit(solution)/shard_map/ppermute | solution.py:179

commit v4 on v3

--- a/solution.py
+++ b/solution.py
@@ -50,24 +50,32 @@
     columns = y_ref.shape[1]
     block = min(512, columns)
     starts = range(0, columns, block)
-    copies = [pltpu.make_async_copy(x_hbm, x_ref, sems.at[0])]
+    first_copy = pltpu.make_async_copy(x_hbm, x_ref, sems.at[0])
+    first_copy.start()
+    waits = {}
+    count = sems.shape[0] - 1
+    for at in range(count):
+        span = slice(at * columns // count, (at + 1) * columns // count)
+        waits[at * len(starts) // count] = pltpu.make_async_copy(
+            y_hbm.at[:, span], y_ref.at[:, span], sems.at[1 + at]
+        )
+    for copy in waits.values():
+        copy.start()
+    first_copy.wait()
+    x = x_ref[...]
+    far_ref[...] = scale * jnp.sum(jnp.square(x.astype(jnp.float32)), axis=0, keepdims=True)
+    wide = x.astype(jnp.float32) * (2.0 * scale)
+    left[...] = jnp.concatenate([*pieces(wide), ones_rows(rows)], axis=0).T
     for at, start in enumerate(starts):
         span = slice(start, start + block)
-        copies.append(pltpu.make_async_copy(y_hbm.at[:, span], y_ref.at[:, span], sems.at[1 + at]))
-    for copy in copies:
-        copy.start()
-    copies[0].wait()
-    x = x_ref[...]
-    far_ref[...] = scale * jnp.sum(jnp.square(x.astype(jnp.float32)), axis=0, keepdims=True)
-    left[...] = jnp.concatenate([x, ones_rows(rows)], axis=0).T
-    for at, start in enumerate(starts):
-        span = slice(start, start + block)
-        copies[1 + at].wait()
+        if at in waits:
+            waits[at].wait()
         piece = y_ref[:, span]
         near = jnp.sum(jnp.square(piece.astype(jnp.float32)), axis=0, keepdims=True)
-        right[:, span] = jnp.concatenate([piece, pad_rows(pieces(-0.5 * near))], axis=0)
+        right[:, span] = jnp.concatenate(
+            [piece, piece, piece, pad_rows(pieces(-scale * near))], axis=0
+        )
         part = jnp.dot(left[...], right[:, span], preferred_element_type=jnp.float32)
-        part = part * (2.0 * scale)
         logits[:, span] = part
         top = functools.reduce(jnp.maximum, [part[:, tile] for tile in lane_tiles(block)])
         tops[...] = top if start == 0 else jnp.maximum(tops[...], top)
@@ -89,16 +97,15 @@
 def second_kernel(scale, points, x_ref, phi_ref, y_ref, e_ref, r_ref, base_ref, left, right, part_r):
     columns = y_ref.shape[1]
     block = min(512, columns)
-    shift = pad_rows(pieces(phi_ref[...] * (0.5 / scale)))
-    left[...] = jnp.concatenate([x_ref[...].astype(jnp.bfloat16), shift], axis=0).T
+    wide = x_ref[...] * (2.0 * scale)
+    left[...] = jnp.concatenate([*pieces(wide), pad_rows(pieces(phi_ref[...]))], axis=0).T
     y = y_ref[...]
-    right[...] = jnp.concatenate([y, ones_rows(columns)], axis=0)
+    right[...] = jnp.concatenate([y, y, y, ones_rows(columns)], axis=0)
     near = jnp.sum(jnp.square(y.astype(jnp.float32)), axis=0, keepdims=True)
     base_ref[...] = scale * near - math.log2(points)
     for start in range(0, columns, block):
         span = slice(start, start + block)
         part = jnp.dot(left[...], right[:, span], preferred_element_type=jnp.float32)
-        part = part * (2.0 * scale)
         e_ref[:, span] = part
         peak = jnp.max(part, axis=0, keepdims=True)
         base_ref[:, span] = base_ref[:, span] - peak
@@ -120,11 +127,15 @@
 
 def split_kernel(e_ref, after_ref, high_ref, low_ref):
     del after_ref
-    for tile in lane_tiles(e_ref.shape[1]):
-        e = e_ref[:, tile]
+    height = min(32, e_ref.shape[0])
+
+    @pl.loop(0, e_ref.shape[0] // height)
+    def _(at):
+        span = pl.ds(pl.multiple_of(at * height, height), height)
+        e = e_ref[span, :]
         high = e.astype(jnp.bfloat16)
-        high_ref[:, tile] = high
-        low_ref[:, tile] = (e - high.astype(jnp.float32)).astype(jnp.bfloat16)
+        high_ref[span, :] = high
+        low_ref[span, :] = (e - high.astype(jnp.float32)).astype(jnp.bfloat16)
 
 
 def weights_kernel(count, x_ref, *refs):
@@ -152,7 +163,7 @@
 
 def assemble_kernel(atlases, *refs):
     own, other, g_own, g_other = refs[:atlases], refs[atlases : 2 * atlases], *refs[2 * atlases : 2 * atlases + 2]
-    out_ref, g_ref, image, sems = refs[2 * atlases + 2 :]
+    out_ref, g_hbm, image, g_ref, sems = refs[2 * atlases + 2 :]
     dims, width = own[0].shape
     atlas = lax.axis_index("atlas")
     row = lax.axis_index("row")
@@ -162,7 +173,8 @@
             start = pl.multiple_of((half * atlases + (atlas ^ key)) * width, LANES)
             places.append((slabs[key], start))
             g_ref[:, pl.ds(start, width)] = duals[:, key * width : (key + 1) * width]
-    copies = []
+    copies = [pltpu.make_async_copy(g_ref, g_hbm, sems.at[0])]
+    copies[0].start()
     for low in range(0, dims, SUBLANES):
         rows = slice(low, low + SUBLANES)
         for slab, start in places:
@@ -229,7 +241,7 @@
 
     everyone = gather_rows(own.astype(jnp.float32))
     mine = lax.dynamic_slice_in_dim(support, row_at * share, share, 1)
-    depth = dims + 16
+    depth = 3 * dims + 16
 
     def row_vector(width):
         return jax.ShapeDtypeStruct((1, width), jnp.float32)
@@ -247,7 +259,7 @@
             pltpu.VMEM((rows, columns), jnp.float32),
             pltpu.VMEM((rows, LANES), jnp.float32),
             pltpu.VMEM((rows, LANES), jnp.float32),
-            pltpu.SemaphoreType.DMA((1 + columns // min(512, columns),)),
+            pltpu.SemaphoreType.DMA((3 if columns % 1024 == 0 else 2,)),
         ],
         compiler_params=pltpu.CompilerParams(vmem_limit_bytes=56_510_000),
         name="first",
@@ -315,7 +327,7 @@
     piece = share // atlases
     if paired and atlases & (atlases - 1) == 0 and atlases <= 8 and piece % LANES == 0:
 
-        order = [*range(1, atlases), 0]
+        order = [*range(atlases - 1, 0, -1), 0]
         terms, duals, arrived = [None] * atlases, [None] * atlases, []
         for key in order:
             terms[key], duals[key] = third(key, piece)
@@ -328,10 +340,11 @@
             functools.partial(assemble_kernel, atlases),
             out_shape=(jax.ShapeDtypeStruct((dims, columns), jnp.float32), row_vector(columns)),
             in_specs=[VMEM] * (2 * atlases + 2),
-            out_specs=(HBM, VMEM),
+            out_specs=(HBM, HBM),
             scratch_shapes=[
                 pltpu.VMEM((dims, columns), jnp.float32),
-                pltpu.SemaphoreType.DMA((dims // SUBLANES,)),
+                pltpu.VMEM((1, columns), jnp.float32),
+                pltpu.SemaphoreType.DMA((1 + dims // SUBLANES,)),
             ],
             compiler_params=pltpu.CompilerParams(vmem_limit_bytes=8 << 20),
             name="assemble",

time: 50.2 us -> 47.5 us (0.946)
  Pallas kernels: 14.5 us -> 11.1 us
  waiting for transfers between devices: 13.4 us -> 14.2 us
    pallas_call x1, Pallas kernels: 2.66 us -> 1.41 us  [shards(): pl.pallas_call(split_kernel, out_shape=(jax.ShapeDtypeStruct(e.shape, jnp...]
    pallas_call x1, Pallas kernels: 4.53 us -> 3.53 us  [shards(): pl.pallas_call(functools.partial(first_kernel, scale), out_shape=(row_vec...]
    ppermute x20, waiting for transfers between devices: 13.4 us -> 14.2 us  [exchange(): return lax.ppermute(value, axis, [(at, at ^ key) for at in range(size)])]
    pallas_call x1, Pallas kernels: 1.65 us -> 1.06 us  [shards(): pl.pallas_call(functools.partial(assemble_kernel, atlases), out_shape=(ja...]
    pallas_call x1, Pallas kernels: 3.44 us -> 2.91 us  [shards(): pl.pallas_call(functools.partial(second_kernel, scale, float(total_suppor...]
  transfers between devices with their start and end apart: 20 -> 20, of which waited for: 10 -> 12; matrix products, arithmetic and copies ran while one was open for 5% -> 5% of each run, Pallas kernels for 5% -> 3%
where the time goes in v4:
time: 47.5 us; the launch traced here: 47.3 us
  starting transfers between devices  18.7 us (39%)
  waiting for transfers between devices  14.2 us (30%)
  Pallas kernels  11.1 us (23%)
  other arithmetic  1.54 us (3%)
  local copies, waits for them, and re-layouts  1 us (2%)
  between operations  0.77 us (2%)
    ppermute x20, starting transfers between devices, exchange(): return lax.ppermute(value, axis, [(at, at ^ key) for at in range(size)])  18.7 us
    ppermute x20, waiting for transfers between devices, exchange(): return lax.ppermute(value, axis, [(at, at ^ key) for at in range(size)])  14.2 us
    pallas_call x1, Pallas kernels, shards(): pl.pallas_call(functools.partial(first_kernel, scale), out_shape=(row_vec...  3.53 us
    pallas_call x1, Pallas kernels, shards(): pl.pallas_call(functools.partial(second_kernel, scale, float(total_suppor...  2.91 us
    pallas_call x4, Pallas kernels, third(): pl.pallas_call(functools.partial(third_kernel, key, dims), out_shape=(jax...  2.09 us
    pallas_call x1, Pallas kernels, shards(): pl.pallas_call(split_kernel, out_shape=(jax.ShapeDtypeStruct(e.shape, jnp...  1.41 us
    pallas_call x1, Pallas kernels, shards(): pl.pallas_call(functools.partial(assemble_kernel, atlases), out_shape=(ja...  1.06 us
    dynamic_slice x1, local copies, waits for them, and re-layouts, shards(): mine = lax.dynamic_slice_in_dim(support, row_at * share, share, 1)  0.97 us
  transfers between devices with their start and end apart: 20, of which 12 were waited for; matrix products, arithmetic and copies ran while one was open for 5% of the time, Pallas kernels for 3%

profile of v4, /device:TPU:0, one launch (start us, length us, event | category | flops | bytes accessed | tf_op | source)
XLA Modules:
  0.0 47.3 jit_solution(2508761537159847824)
XLA Ops:
  0.6 3.5 %first.1 = (f32[1,512]{1,0:T(1,128)S(1)}, f32[1,512]{1,0:T(1,128)S(1)}) custom-call(bf16[64,512]{1,0:T(8,128)(2,1)} %bitcast.2, bf16[64,4096]{1,0:T(8,128)(2,1)} %y_hbm.1), custom_call_target="tpu_custom_call" | custom-call | tf_op jit(solution)/shard_map/first/pallas_call | solution.py:249
  4.2 5.1 %collective-permute-start.2 = (f32[1,512]{1,0:T(1,128)S(1)}, f32[1,512]{1,0:T(1,128)S(1)}, u32[]{:S(2)}, u32[]{:S(2)}) collective-permute-start(f32[1,512]{1,0:T(1,128)S(1)} %get-tuple-element.20), channel_id=1, source_target_pairs={{0,3},{1,2},{2,1},{3,0},{4,7},{5,6},{6,5},{7,4},{8,11},{9,10},{10,... | collective-permute-start | bytes 6152 | tf_op jit(solution)/shard_map/ppermute | solution.py:191
  9.3 0.6 %collective-permute-start = (f32[1,512]{1,0:T(1,128)S(1)}, f32[1,512]{1,0:T(1,128)S(1)}, u32[]{:S(2)}, u32[]{:S(2)}) collective-permute-start(f32[1,512]{1,0:T(1,128)S(1)} %get-tuple-element.20), channel_id=1, source_target_pairs={{0,1},{1,0},{2,3},{3,2},{4,5},{5,4},{6,7},{7,6},{8,9},{9,8},{10,11... | collective-permute-start | bytes 6152 | tf_op jit(solution)/shard_map/ppermute | solution.py:191
  10.0 0.8 %bitcast_convert_fusion = f32[64,512]{1,0:T(8,128)S(1)} fusion(bf16[1,64,512]{2,1,0:T(8,128)(2,1)} %param.2), kind=kLoop, calls=%fused_computation.14 | loop fusion | flops 32768 | bytes 196608 | tf_op jit(solution)/shard_map/convert_element_type | solution.py:242
  10.9 2.9 %collective-permute-done.1 = f32[1,512]{1,0:T(1,128)S(1)} collective-permute-done((f32[1,512]{1,0:T(1,128)S(1)}, f32[1,512]{1,0:T(1,128)S(1)}, u32[]{:S(2)}, u32[]{:S(2)}) %collective-permute-start.1) | collective-permute-done | bytes 2080 | tf_op jit(solution)/shard_map/ppermute | solution.py:191
  13.9 1.0 %constant_dynamic-slice_fusion.y_ref = bf16[64,2048]{1,0:T(8,128)(2,1)S(1)} fusion(bf16[64,4096]{1,0:T(8,128)(2,1)} %y_hbm.1, s32[]{:T(128)S(6)} %select_n.3), kind=kLoop, calls=%fused_computation.13 | loop fusion | bytes 524292 | tf_op jit(solution)/shard_map/dynamic_slice | solution.py:243
  15.1 2.9 %second.1 = (f32[1024,2048]{1,0:T(8,128)S(1)}, f32[1,1024]{1,0:T(1,128)S(1)}, f32[1,2048]{1,0:T(1,128)S(1)}) custom-call(f32[64,1024]{1,0:T(8,128)S(1)} %pad_maximum_fusion.x_ref, f32[1,1024]{1,0:T(1,128)S(1)} %pad_maximum_fusion.1.phi_ref, bf16[64,2048]{1,0:T(8,128)(2,1)S(1)} %constant_dynamic-slice_fusion.y_ref), custom_call_target="tpu_custom_call" | custom-call | tf_op jit(solution)/shard_map/second/pallas_call | solution.py:273
  18.0 0.4 collective-permute-start.5
  18.4 0.8 %collective-permute-done.5.other_ref = f32[1,1024]{1,0:T(1,128)S(1)} collective-permute-done((f32[1,1024]{1,0:T(1,128)S(1)}, f32[1,1024]{1,0:T(1,128)S(1)}, u32[]{:S(2)}, u32[]{:S(2)}) %collective-permute-start.5) | collective-permute-done | bytes 4128 | tf_op jit(solution)/shard_map/ppermute | solution.py:191
  19.3 1.5 %collective-permute-start.8 = (f32[1,1024]{1,0:T(1,128)S(1)}, f32[1,1024]{1,0:T(1,128)S(1)}, u32[]{:S(2)}, u32[]{:S(2)}) collective-permute-start(f32[1,1024]{1,0:T(1,128)S(1)} %meet.1.refs_0_.after_ref), channel_id=1, source_target_pairs={{0,3},{1,2},{2,1},{3,0},{4,7},{5,6},{6,5},{7,4},{8,11},{9,10},{10,... | collective-permute-start | bytes 12296 | tf_op jit(solution)/shard_map/ppermute | solution.py:191
  20.7 0.6 %collective-permute-start.7 = (f32[1,1024]{1,0:T(1,128)S(1)}, f32[1,1024]{1,0:T(1,128)S(1)}, u32[]{:S(2)}, u32[]{:S(2)}) collective-permute-start(f32[1,1024]{1,0:T(1,128)S(1)} %meet.1.refs_0_.after_ref), channel_id=1, source_target_pairs={{0,2},{1,3},{2,0},{3,1},{4,6},{5,7},{6,4},{7,5},{8,10},{9,11},{10,... | collective-permute-start | bytes 12296 | tf_op jit(solution)/shard_map/ppermute | solution.py:191
  21.4 2.3 %collective-permute-start.6 = (f32[1,1024]{1,0:T(1,128)S(1)}, f32[1,1024]{1,0:T(1,128)S(1)}, u32[]{:S(2)}, u32[]{:S(2)}) collective-permute-start(f32[1,1024]{1,0:T(1,128)S(1)} %meet.1.refs_0_.after_ref), channel_id=1, source_target_pairs={{0,1},{1,0},{2,3},{3,2},{4,5},{5,4},{6,7},{7,6},{8,9},{9,8},{10,11... | collective-permute-start | bytes 12296 | tf_op jit(solution)/shard_map/ppermute | solution.py:191
  23.7 1.4 %split.1 = (bf16[1024,2048]{1,0:T(8,128)(2,1)S(1)}, bf16[1024,2048]{1,0:T(8,128)(2,1)S(1)}) custom-call(f32[1024,2048]{1,0:T(8,128)S(1)} %get-tuple-element.23.e_ref, f32[1,1024]{1,0:T(1,128)S(1)} %meet.1.refs_0_.after_ref), custom_call_target="tpu_custom_call" | custom-call | flops 8388608 | bytes 16777216 | tf_op jit(solution)/shard_map/split/pallas_call | solution.py:294
  25.4 0.5 %third.7 = (f32[64,512]{1,0:T(8,128)S(1)}, f32[1,512]{1,0:T(1,128)S(1)}) custom-call(bf16[144,1024]{1,0:T(8,128)(2,1)S(1)} %weights.1.weights_ref, bf16[1024,2048]{1,0:T(8,128)(2,1)S(1)} %get-tuple-element.24.high_ref, bf16[1024,2048]{1,0:T(8,128)(2,1)S(1)} %get-tuple-element.25.low_ref, f32[1,2048]{1,0:T(1,128)S(1)} %get-tuple-element.26.base_ref), custom_call_target="tpu_custom_call" | custom-call | flops 234881024 | bytes 2097152 | tf_op jit(solution)/shard_map/third/pallas_call | solution.py:313
  25.9 0.5 %third.6 = (f32[64,512]{1,0:T(8,128)S(1)}, f32[1,512]{1,0:T(1,128)S(1)}) custom-call(bf16[144,1024]{1,0:T(8,128)(2,1)S(1)} %weights.1.weights_ref, bf16[1024,2048]{1,0:T(8,128)(2,1)S(1)} %get-tuple-element.24.high_ref, bf16[1024,2048]{1,0:T(8,128)(2,1)S(1)} %get-tuple-element.25.low_ref, f32[1,2048]{1,0:T(1,128)S(1)} %get-tuple-element.26.base_ref), custom_call_target="tpu_custom_call" | custom-call | flops 234881024 | bytes 2097152 | tf_op jit(solution)/shard_map/third/pallas_call | solution.py:313
  26.4 0.5 %third.5 = (f32[64,512]{1,0:T(8,128)S(1)}, f32[1,512]{1,0:T(1,128)S(1)}) custom-call(bf16[144,1024]{1,0:T(8,128)(2,1)S(1)} %weights.1.weights_ref, bf16[1024,2048]{1,0:T(8,128)(2,1)S(1)} %get-tuple-element.24.high_ref, bf16[1024,2048]{1,0:T(8,128)(2,1)S(1)} %get-tuple-element.25.low_ref, f32[1,2048]{1,0:T(1,128)S(1)} %get-tuple-element.26.base_ref), custom_call_target="tpu_custom_call" | custom-call | flops 234881024 | bytes 2097152 | tf_op jit(solution)/shard_map/third/pallas_call | solution.py:313
  27.0 0.5 %third.4 = (f32[64,512]{1,0:T(8,128)S(1)}, f32[1,512]{1,0:T(1,128)S(1)}) custom-call(bf16[144,1024]{1,0:T(8,128)(2,1)S(1)} %weights.1.weights_ref, bf16[1024,2048]{1,0:T(8,128)(2,1)S(1)} %get-tuple-element.24.high_ref, bf16[1024,2048]{1,0:T(8,128)(2,1)S(1)} %get-tuple-element.25.low_ref, f32[1,2048]{1,0:T(1,128)S(1)} %get-tuple-element.26.base_ref), custom_call_target="tpu_custom_call" | custom-call | flops 234881024 | bytes 2097152 | tf_op jit(solution)/shard_map/third/pallas_call | solution.py:313
  27.5 2.5 %collective-permute-start.9 = (f32[64,512]{1,0:T(8,128)S(1)}, f32[64,512]{1,0:T(8,128)S(1)}, u32[]{:S(2)}, u32[]{:S(2)}) collective-permute-start(f32[64,512]{1,0:T(8,128)S(1)} %get-tuple-element.28), channel_id=1, source_target_pairs={{0,24},{8,16},{16,8},{24,0},{1,25},{9,17},{17,9},{25,1},{2,26},{10... | collective-permute-start | bytes 393224 | tf_op jit(solution)/shard_map/ppermute | solution.py:191
  30.0 0.5 %collective-permute-start.10 = (f32[64,512]{1,0:T(8,128)S(1)}, f32[64,512]{1,0:T(8,128)S(1)}, u32[]{:S(2)}, u32[]{:S(2)}) collective-permute-start(f32[64,512]{1,0:T(8,128)S(1)} %get-tuple-element.29), channel_id=1, source_target_pairs={{0,16},{8,24},{16,0},{24,8},{1,17},{9,25},{17,1},{25,9},{2,18},{10... | collective-permute-start | bytes 393224 | tf_op jit(solution)/shard_map/ppermute | solution.py:191
  30.5 0.5 %collective-permute-start.11 = (f32[64,512]{1,0:T(8,128)S(1)}, f32[64,512]{1,0:T(8,128)S(1)}, u32[]{:S(2)}, u32[]{:S(2)}) collective-permute-start(f32[64,512]{1,0:T(8,128)S(1)} %get-tuple-element.30), channel_id=1, source_target_pairs={{0,8},{8,0},{16,24},{24,16},{1,9},{9,1},{17,25},{25,17},{2,10},{10... | collective-permute-start | bytes 393224 | tf_op jit(solution)/shard_map/ppermute | solution.py:191
  31.1 3.0 %collective-permute-done.9 = f32[64,512]{1,0:T(8,128)S(1)} collective-permute-done((f32[64,512]{1,0:T(8,128)S(1)}, f32[64,512]{1,0:T(8,128)S(1)}, u32[]{:S(2)}, u32[]{:S(2)}) %collective-permute-start.9) | collective-permute-done | bytes 131104 | tf_op jit(solution)/shard_map/ppermute | solution.py:191
  34.0 2.0 %collective-permute-done.10 = f32[64,512]{1,0:T(8,128)S(1)} collective-permute-done((f32[64,512]{1,0:T(8,128)S(1)}, f32[64,512]{1,0:T(8,128)S(1)}, u32[]{:S(2)}, u32[]{:S(2)}) %collective-permute-start.10) | collective-permute-done | bytes 131104 | tf_op jit(solution)/shard_map/ppermute | solution.py:191
  36.1 1.7 %collective-permute-start.14 = (f32[64,512]{1,0:T(8,128)S(1)}, f32[64,512]{1,0:T(8,128)S(1)}, u32[]{:S(2)}, u32[]{:S(2)}) collective-permute-start(f32[64,512]{1,0:T(8,128)S(1)} %add_multiply_fusion.refs_0_), channel_id=1, source_target_pairs={{0,24},{8,16},{16,8},{24,0},{1,25},{9,17},{17,9},{25,1},{2,26},{10... | collective-permute-start | bytes 393224 | tf_op jit(solution)/shard_map/ppermute | solution.py:191
  37.8 1.3 %collective-permute-start.13 = (f32[64,512]{1,0:T(8,128)S(1)}, f32[64,512]{1,0:T(8,128)S(1)}, u32[]{:S(2)}, u32[]{:S(2)}) collective-permute-start(f32[64,512]{1,0:T(8,128)S(1)} %add_multiply_fusion.refs_0_), channel_id=1, source_target_pairs={{0,16},{8,24},{16,0},{24,8},{1,17},{9,25},{17,1},{25,9},{2,18},{10... | collective-permute-start | bytes 393224 | tf_op jit(solution)/shard_map/ppermute | solution.py:191
  39.2 0.5 %collective-permute-start.12 = (f32[64,512]{1,0:T(8,128)S(1)}, f32[64,512]{1,0:T(8,128)S(1)}, u32[]{:S(2)}, u32[]{:S(2)}) collective-permute-start(f32[64,512]{1,0:T(8,128)S(1)} %add_multiply_fusion.refs_0_), channel_id=1, source_target_pairs={{0,8},{8,0},{16,24},{24,16},{1,9},{9,1},{17,25},{25,17},{2,10},{10... | collective-permute-start | bytes 393224 | tf_op jit(solution)/shard_map/ppermute | solution.py:191
  39.7 0.5 %collective-permute-start.15 = (f32[64,512]{1,0:T(8,128)S(1)}, f32[64,512]{1,0:T(8,128)S(1)}, u32[]{:S(2)}, u32[]{:S(2)}) collective-permute-start(f32[64,512]{1,0:T(8,128)S(1)} %add_multiply_fusion.refs_0_), channel_id=1, source_target_pairs={{0,4},{4,0},{1,5},{5,1},{2,6},{6,2},{3,7},{7,3},{8,12},{12,8},{9,1... | collective-permute-start | bytes 393224 | tf_op jit(solution)/shard_map/ppermute | solution.py:191
  40.2 3.1 %collective-permute-done.14.refs_3_ = f32[64,512]{1,0:T(8,128)S(1)} collective-permute-done((f32[64,512]{1,0:T(8,128)S(1)}, f32[64,512]{1,0:T(8,128)S(1)}, u32[]{:S(2)}, u32[]{:S(2)}) %collective-permute-start.14) | collective-permute-done | bytes 131104 | tf_op jit(solution)/shard_map/ppermute | solution.py:191
  43.3 1.4 %collective-permute-done.13.refs_2_ = f32[64,512]{1,0:T(8,128)S(1)} collective-permute-done((f32[64,512]{1,0:T(8,128)S(1)}, f32[64,512]{1,0:T(8,128)S(1)}, u32[]{:S(2)}, u32[]{:S(2)}) %collective-permute-start.13) | collective-permute-done | bytes 131104 | tf_op jit(solution)/shard_map/ppermute | solution.py:191
  44.9 0.4 collective-permute-start.16
  45.2 0.6 %subtract_multiply_fusion = f32[1,512]{1,0:T(1,128)} fusion(f32[1,512]{1,0:T(1,128)S(1)} %add_subtract_fusion, f32[1,512]{1,0:T(1,128)S(1)} %get-tuple-element.21, f32[1,1024]{1,0:T(1,128)S(1)} %collective-permute-done.8.refs_3_, f32[1,1024]{1,0:T(1,128)S(1)} %collective-permute-done.7.refs_2_, f32[1,1024]{1,0:T(1,128)S(1)} %collective-permute-done.6.refs_1_, ...), kind=kLoop, calls=%fused_computation.11 | loop fusion | flops 4096 | bytes 14336 | tf_op jit(solution)/shard_map/mul | solution.py:362
  45.8 0.2 collective-permute-done.17.refs_6_
  46.2 1.1 %assemble.1 = (f32[64,4096]{1,0:T(8,128)}, f32[1,4096]{1,0:T(1,128)}) custom-call(f32[64,512]{1,0:T(8,128)S(1)} %add_multiply_fusion.refs_0_, f32[64,512]{1,0:T(8,128)S(1)} %collective-permute-done.12.refs_1_, f32[64,512]{1,0:T(8,128)S(1)} %collective-permute-done.13.refs_2_, f32[64,512]{1,0:T(8,128)S(1)} %collective-permute-done.14.refs_3_, ...), custom_call_target="tpu_custom_call" | custom-call | tf_op jit(solution)/shard_map/assemble/pallas_call | solution.py:339
  (29 shorter events, 1.2 us)
Async XLA Ops:
  4.2 6.7 %collective-permute-start.2 = (f32[1,512]{1,0:T(1,128)S(1)}, f32[1,512]{1,0:T(1,128)S(1)}, u32[]{:S(2)}, u32[]{:S(2)}) collective-permute-start(f32[1,512]{1,0:T(1,128)S(1)} %get-tuple-element.20), channel_id=1, source_target_pairs={{0,3},{1,2},{2,1},{3,0},{4,7},{5,6},{6,5},{7,4},{8,11},{9,10},{10,... | collective-permute-start | bytes 6152 | tf_op jit(solution)/shard_map/ppermute | solution.py:191
  9.3 4.5 %collective-permute-start.1 = (f32[1,512]{1,0:T(1,128)S(1)}, f32[1,512]{1,0:T(1,128)S(1)}, u32[]{:S(2)}, u32[]{:S(2)}) collective-permute-start(f32[1,512]{1,0:T(1,128)S(1)} %get-tuple-element.20), channel_id=1, source_target_pairs={{0,2},{1,3},{2,0},{3,1},{4,6},{5,7},{6,4},{7,5},{8,10},{9,11},{10,... | collective-permute-start | bytes 6152 | tf_op jit(solution)/shard_map/ppermute | solution.py:191
  9.3 4.5 %collective-permute-start = (f32[1,512]{1,0:T(1,128)S(1)}, f32[1,512]{1,0:T(1,128)S(1)}, u32[]{:S(2)}, u32[]{:S(2)}) collective-permute-start(f32[1,512]{1,0:T(1,128)S(1)} %get-tuple-element.20), channel_id=1, source_target_pairs={{0,1},{1,0},{2,3},{3,2},{4,5},{5,4},{6,7},{7,6},{8,9},{9,8},{10,11... | collective-permute-start | bytes 6152 | tf_op jit(solution)/shard_map/ppermute | solution.py:191
  10.8 4.3 %collective-permute-start.3 = (f32[64,512]{1,0:T(8,128)S(1)}, f32[64,512]{1,0:T(8,128)S(1)}, u32[]{:S(2)}, u32[]{:S(2)}) collective-permute-start(f32[64,512]{1,0:T(8,128)S(1)} %bitcast_convert_fusion), channel_id=1, source_target_pairs={{0,4},{4,0},{1,5},{5,1},{2,6},{6,2},{3,7},{7,3},{8,12},{12,8},{9,1... | collective-permute-start | bytes 393224 | tf_op jit(solution)/shard_map/ppermute | solution.py:191
  13.8 1.2 %collective-permute-start.4 = (f32[1,512]{1,0:T(1,128)S(1)}, f32[1,512]{1,0:T(1,128)S(1)}, u32[]{:S(2)}, u32[]{:S(2)}) collective-permute-start(f32[1,512]{1,0:T(1,128)S(1)} %add_subtract_fusion), channel_id=1, source_target_pairs={{0,4},{4,0},{1,5},{5,1},{2,6},{6,2},{3,7},{7,3},{8,12},{12,8},{9,1... | collective-permute-start | bytes 6152 | tf_op jit(solution)/shard_map/ppermute | solution.py:191
  18.0 1.2 %collective-permute-start.5 = (f32[1,1024]{1,0:T(1,128)S(1)}, f32[1,1024]{1,0:T(1,128)S(1)}, u32[]{:S(2)}, u32[]{:S(2)}) collective-permute-start(f32[1,1024]{1,0:T(1,128)S(1)} %get-tuple-element.22.own_ref), channel_id=1, source_target_pairs={{0,4},{4,0},{1,5},{5,1},{2,6},{6,2},{3,7},{7,3},{8,12},{12,8},{9,1... | collective-permute-start | bytes 12296 | tf_op jit(solution)/shard_map/ppermute | solution.py:191
  19.3 5.8 %collective-permute-start.8 = (f32[1,1024]{1,0:T(1,128)S(1)}, f32[1,1024]{1,0:T(1,128)S(1)}, u32[]{:S(2)}, u32[]{:S(2)}) collective-permute-start(f32[1,1024]{1,0:T(1,128)S(1)} %meet.1.refs_0_.after_ref), channel_id=1, source_target_pairs={{0,3},{1,2},{2,1},{3,0},{4,7},{5,6},{6,5},{7,4},{8,11},{9,10},{10,... | collective-permute-start | bytes 12296 | tf_op jit(solution)/shard_map/ppermute | solution.py:191
  20.7 4.5 %collective-permute-start.7 = (f32[1,1024]{1,0:T(1,128)S(1)}, f32[1,1024]{1,0:T(1,128)S(1)}, u32[]{:S(2)}, u32[]{:S(2)}) collective-permute-start(f32[1,1024]{1,0:T(1,128)S(1)} %meet.1.refs_0_.after_ref), channel_id=1, source_target_pairs={{0,2},{1,3},{2,0},{3,1},{4,6},{5,7},{6,4},{7,5},{8,10},{9,11},{10,... | collective-permute-start | bytes 12296 | tf_op jit(solution)/shard_map/ppermute | solution.py:191
  21.4 3.9 %collective-permute-start.6 = (f32[1,1024]{1,0:T(1,128)S(1)}, f32[1,1024]{1,0:T(1,128)S(1)}, u32[]{:S(2)}, u32[]{:S(2)}) collective-permute-start(f32[1,1024]{1,0:T(1,128)S(1)} %meet.1.refs_0_.after_ref), channel_id=1, source_target_pairs={{0,1},{1,0},{2,3},{3,2},{4,5},{5,4},{6,7},{7,6},{8,9},{9,8},{10,11... | collective-permute-start | bytes 12296 | tf_op jit(solution)/shard_map/ppermute | solution.py:191
  27.5 6.5 %collective-permute-start.9 = (f32[64,512]{1,0:T(8,128)S(1)}, f32[64,512]{1,0:T(8,128)S(1)}, u32[]{:S(2)}, u32[]{:S(2)}) collective-permute-start(f32[64,512]{1,0:T(8,128)S(1)} %get-tuple-element.28), channel_id=1, source_target_pairs={{0,24},{8,16},{16,8},{24,0},{1,25},{9,17},{17,9},{25,1},{2,26},{10... | collective-permute-start | bytes 393224 | tf_op jit(solution)/shard_map/ppermute | solution.py:191
  30.0 6.0 %collective-permute-start.10 = (f32[64,512]{1,0:T(8,128)S(1)}, f32[64,512]{1,0:T(8,128)S(1)}, u32[]{:S(2)}, u32[]{:S(2)}) collective-permute-start(f32[64,512]{1,0:T(8,128)S(1)} %get-tuple-element.29), channel_id=1, source_target_pairs={{0,16},{8,24},{16,0},{24,8},{1,17},{9,25},{17,1},{25,9},{2,18},{10... | collective-permute-start | bytes 393224 | tf_op jit(solution)/shard_map/ppermute | solution.py:191
  30.5 5.6 %collective-permute-start.11 = (f32[64,512]{1,0:T(8,128)S(1)}, f32[64,512]{1,0:T(8,128)S(1)}, u32[]{:S(2)}, u32[]{:S(2)}) collective-permute-start(f32[64,512]{1,0:T(8,128)S(1)} %get-tuple-element.30), channel_id=1, source_target_pairs={{0,8},{8,0},{16,24},{24,16},{1,9},{9,1},{17,25},{25,17},{2,10},{10... | collective-permute-start | bytes 393224 | tf_op jit(solution)/shard_map/ppermute | solution.py:191
  36.1 7.2 %collective-permute-start.14 = (f32[64,512]{1,0:T(8,128)S(1)}, f32[64,512]{1,0:T(8,128)S(1)}, u32[]{:S(2)}, u32[]{:S(2)}) collective-permute-start(f32[64,512]{1,0:T(8,128)S(1)} %add_multiply_fusion.refs_0_), channel_id=1, source_target_pairs={{0,24},{8,16},{16,8},{24,0},{1,25},{9,17},{17,9},{25,1},{2,26},{10... | collective-permute-start | bytes 393224 | tf_op jit(solution)/shard_map/ppermute | solution.py:191
  37.8 6.9 %collective-permute-start.13 = (f32[64,512]{1,0:T(8,128)S(1)}, f32[64,512]{1,0:T(8,128)S(1)}, u32[]{:S(2)}, u32[]{:S(2)}) collective-permute-start(f32[64,512]{1,0:T(8,128)S(1)} %add_multiply_fusion.refs_0_), channel_id=1, source_target_pairs={{0,16},{8,24},{16,0},{24,8},{1,17},{9,25},{17,1},{25,9},{2,18},{10... | collective-permute-start | bytes 393224 | tf_op jit(solution)/shard_map/ppermute | solution.py:191
  39.2 5.7 %collective-permute-start.12 = (f32[64,512]{1,0:T(8,128)S(1)}, f32[64,512]{1,0:T(8,128)S(1)}, u32[]{:S(2)}, u32[]{:S(2)}) collective-permute-start(f32[64,512]{1,0:T(8,128)S(1)} %add_multiply_fusion.refs_0_), channel_id=1, source_target_pairs={{0,8},{8,0},{16,24},{24,16},{1,9},{9,1},{17,25},{25,17},{2,10},{10... | collective-permute-start | bytes 393224 | tf_op jit(solution)/shard_map/ppermute | solution.py:191
  39.7 6.1 %collective-permute-start.19 = (f32[1,2048]{1,0:T(1,128)S(1)}, f32[1,2048]{1,0:T(1,128)S(1)}, u32[]{:S(2)}, u32[]{:S(2)}) collective-permute-start(f32[1,2048]{1,0:T(1,128)S(1)} %constant_dynamic-update-slice_fusion.refs_8_), channel_id=1, source_target_pairs={{0,4},{4,0},{1,5},{5,1},{2,6},{6,2},{3,7},{7,3},{8,12},{12,8},{9,1... | collective-permute-start | bytes 24584 | tf_op jit(solution)/shard_map/ppermute | solution.py:191
  39.7 6.1 %collective-permute-start.15 = (f32[64,512]{1,0:T(8,128)S(1)}, f32[64,512]{1,0:T(8,128)S(1)}, u32[]{:S(2)}, u32[]{:S(2)}) collective-permute-start(f32[64,512]{1,0:T(8,128)S(1)} %add_multiply_fusion.refs_0_), channel_id=1, source_target_pairs={{0,4},{4,0},{1,5},{5,1},{2,6},{6,2},{3,7},{7,3},{8,12},{12,8},{9,1... | collective-permute-start | bytes 393224 | tf_op jit(solution)/shard_map/ppermute | solution.py:191
  43.3 2.5 %collective-permute-start.18 = (f32[64,512]{1,0:T(8,128)S(1)}, f32[64,512]{1,0:T(8,128)S(1)}, u32[]{:S(2)}, u32[]{:S(2)}) collective-permute-start(f32[64,512]{1,0:T(8,128)S(1)} %collective-permute-done.14.refs_3_), channel_id=1, source_target_pairs={{0,4},{4,0},{1,5},{5,1},{2,6},{6,2},{3,7},{7,3},{8,12},{12,8},{9,1... | collective-permute-start | bytes 393224 | tf_op jit(solution)/shard_map/ppermute | solution.py:191
  44.7 1.3 %collective-permute-start.17 = (f32[64,512]{1,0:T(8,128)S(1)}, f32[64,512]{1,0:T(8,128)S(1)}, u32[]{:S(2)}, u32[]{:S(2)}) collective-permute-start(f32[64,512]{1,0:T(8,128)S(1)} %collective-permute-done.13.refs_2_), channel_id=1, source_target_pairs={{0,4},{4,0},{1,5},{5,1},{2,6},{6,2},{3,7},{7,3},{8,12},{12,8},{9,1... | collective-permute-start | bytes 393224 | tf_op jit(solution)/shard_map/ppermute | solution.py:191
  44.9 1.4 %collective-permute-start.16 = (f32[64,512]{1,0:T(8,128)S(1)}, f32[64,512]{1,0:T(8,128)S(1)}, u32[]{:S(2)}, u32[]{:S(2)}) collective-permute-start(f32[64,512]{1,0:T(8,128)S(1)} %collective-permute-done.12.refs_1_), channel_id=1, source_target_pairs={{0,4},{4,0},{1,5},{5,1},{2,6},{6,2},{3,7},{7,3},{8,12},{12,8},{9,1... | collective-permute-start | bytes 393224 | tf_op jit(solution)/shard_map/ppermute | solution.py:191

commit v5 on v4

--- a/solution.py
+++ b/solution.py
@@ -39,12 +39,18 @@
     return jnp.where(index < 3, 1.0, 0.0).astype(jnp.bfloat16)
 
 
+def fold(join, value):
+    return functools.reduce(
+        join, [value[low : low + SUBLANES] for low in range(0, value.shape[0], SUBLANES)]
+    )
+
+
 def lane_tiles(width):
     return [slice(at, at + LANES) for at in range(0, width, LANES)]
 
 
 def first_kernel(
-    scale, x_hbm, y_hbm, out_ref, far_ref, x_ref, y_ref, left, right, logits, tops, sums, sems
+    scale, x_hbm, y_hbm, out_ref, far_ref, mine_ref, wide_ref, x_ref, y_ref, left, right, logits, tops, sums, sems
 ):
     _, rows = x_ref.shape
     columns = y_ref.shape[1]
@@ -63,6 +69,7 @@
         copy.start()
     first_copy.wait()
     x = x_ref[...]
+    wide_ref[...] = x.astype(jnp.float32)
     far_ref[...] = scale * jnp.sum(jnp.square(x.astype(jnp.float32)), axis=0, keepdims=True)
     wide = x.astype(jnp.float32) * (2.0 * scale)
     left[...] = jnp.concatenate([*pieces(wide), ones_rows(rows)], axis=0).T
@@ -79,6 +86,9 @@
         logits[:, span] = part
         top = functools.reduce(jnp.maximum, [part[:, tile] for tile in lane_tiles(block)])
         tops[...] = top if start == 0 else jnp.maximum(tops[...], top)
+    share = mine_ref.shape[1]
+    mine = pl.multiple_of(lax.axis_index("row") * share, share)
+    mine_ref[...] = y_ref[:, pl.ds(mine, share)]
     height = min(64, rows)
     for low in range(0, rows, height):
         span = slice(low, low + height)
@@ -94,11 +104,15 @@
     out_ref[...] = peak + jnp.log2(mass)
 
 
-def second_kernel(scale, points, x_ref, phi_ref, y_ref, e_ref, r_ref, base_ref, left, right, part_r):
-    columns = y_ref.shape[1]
-    block = min(512, columns)
+def logit_block(scale, x_ref, phi_ref, left):
     wide = x_ref[...] * (2.0 * scale)
     left[...] = jnp.concatenate([*pieces(wide), pad_rows(pieces(phi_ref[...]))], axis=0).T
+
+
+def half_kernel(scale, points, x_ref, phi_ref, y_ref, b_ref, peak_ref, base_ref, right, left):
+    columns = b_ref.shape[1]
+    block = min(256, columns)
+    logit_block(scale, x_ref, phi_ref, left)
     y = y_ref[...]
     right[...] = jnp.concatenate([y, y, y, ones_rows(columns)], axis=0)
     near = jnp.sum(jnp.square(y.astype(jnp.float32)), axis=0, keepdims=True)
@@ -106,16 +120,37 @@
     for start in range(0, columns, block):
         span = slice(start, start + block)
         part = jnp.dot(left[...], right[:, span], preferred_element_type=jnp.float32)
-        e_ref[:, span] = part
-        peak = jnp.max(part, axis=0, keepdims=True)
-        base_ref[:, span] = base_ref[:, span] - peak
-        expo = jnp.exp2(e_ref[:, span] - peak)
-        e_ref[:, span] = expo
-        total = jnp.sum(expo, axis=0, keepdims=True)
-        weight = 1.0 / (points * total)
-        share = e_ref[:, span] * weight
-        row = functools.reduce(jnp.add, [share[:, tile] for tile in lane_tiles(block)])
-        part_r[...] = row if start == 0 else part_r[...] + row
+        b_ref[:, span] = part
+        peak_ref[:, span] = jnp.max(fold(jnp.maximum, part), axis=0, keepdims=True)
+
+
+def second_kernel(
+    scale, points, b_ref, top_ref, near_ref, right, x_ref, phi_ref, e_ref, r_ref, base_ref, left, part_r
+):
+    half = b_ref.shape[0]
+    cells, columns = e_ref.shape
+    block = min(256, columns)
+    height = min(64, half)
+    logit_block(scale, x_ref, phi_ref, left)
+    for start in range(0, columns, block):
+        span = slice(start, start + block)
+        part = jnp.dot(left[...], right[:, span], preferred_element_type=jnp.float32)
+        e_ref[half:, span] = part
+        peak = jnp.max(fold(jnp.maximum, part), axis=0, keepdims=True)
+        peak = jnp.maximum(peak, top_ref[:, span])
+        base_ref[:, span] = near_ref[:, span] - peak
+        total = None
+        for low in range(0, cells, SUBLANES):
+            rows = slice(low, low + SUBLANES)
+            expo = jnp.exp2((b_ref if low < half else e_ref)[rows, span] - peak)
+            e_ref[rows, span] = expo
+            total = expo if total is None else total + expo
+        weight = 1.0 / (points * jnp.sum(total, axis=0, keepdims=True))
+        for low in range(0, cells, height):
+            rows = slice(low, low + height)
+            share = e_ref[rows, span] * weight
+            row = functools.reduce(jnp.add, [share[:, tile] for tile in lane_tiles(block)])
+            part_r[rows, :] = row if start == 0 else part_r[rows, :] + row
     r_ref[...] = jnp.sum(part_r[...].T, axis=0, keepdims=True)
 
 
@@ -138,10 +173,10 @@
         low_ref[span, :] = (e - high.astype(jnp.float32)).astype(jnp.bfloat16)
 
 
-def weights_kernel(count, x_ref, *refs):
+def weights_kernel(count, own_ref, other_ref, *refs):
     *r_refs, out_ref = refs
     w = 1.0 / (count * functools.reduce(jnp.add, [ref[...] for ref in r_refs]))
-    wide = x_ref[...] * w
+    wide = jnp.concatenate([own_ref[...], other_ref[...]], axis=1) * w
     high = wide.astype(jnp.bfloat16)
     low = (wide - high.astype(jnp.float32)).astype(jnp.bfloat16)
     out_ref[...] = jnp.concatenate([high, pad_rows(pieces(w)), low], axis=0)
@@ -214,10 +249,11 @@
     row_at = lax.axis_index("row")
     paired = row_size == 2
 
-    def gather_rows(value):
+    def halves(value):
         if paired:
-            return jnp.concatenate([value, exchange(value, "row", 2, 1)], axis=-1)
-        return lax.all_gather(value, "row", axis=value.ndim - 1, tiled=True)
+            return value, exchange(value, "row", 2, 1)
+        value = lax.all_gather(value, "row", axis=value.ndim - 1, tiled=True)
+        return jnp.split(value, 2, axis=-1)
 
     def sum_rows(value):
         if paired:
@@ -239,18 +275,22 @@
     def all_rows(value):
         return lax.all_gather(value, "row", axis=1, tiled=True)
 
-    everyone = gather_rows(own.astype(jnp.float32))
-    mine = lax.dynamic_slice_in_dim(support, row_at * share, share, 1)
+    half = total_cells // 2
     depth = 3 * dims + 16
 
     def row_vector(width):
         return jax.ShapeDtypeStruct((1, width), jnp.float32)
 
-    lam, far = pl.pallas_call(
+    lam, far, mine, some = pl.pallas_call(
         functools.partial(first_kernel, scale),
-        out_shape=(row_vector(rows), row_vector(rows)),
+        out_shape=(
+            row_vector(rows),
+            row_vector(rows),
+            jax.ShapeDtypeStruct((dims, share), jnp.bfloat16),
+            jax.ShapeDtypeStruct((dims, rows), jnp.float32),
+        ),
         in_specs=[HBM, HBM],
-        out_specs=(VMEM, VMEM),
+        out_specs=(VMEM,) * 4,
         scratch_shapes=[
             pltpu.VMEM((dims, rows), jnp.bfloat16),
             pltpu.VMEM((dims, columns), jnp.bfloat16),
@@ -261,15 +301,34 @@
             pltpu.VMEM((rows, LANES), jnp.float32),
             pltpu.SemaphoreType.DMA((3 if columns % 1024 == 0 else 2,)),
         ],
-        compiler_params=pltpu.CompilerParams(vmem_limit_bytes=56_510_000),
+        compiler_params=pltpu.CompilerParams(vmem_limit_bytes=24 << 20),
         name="first",
-    )(own, support)
+    )(
+        pltpu.with_memory_space_constraint(own, pltpu.HBM),
+        pltpu.with_memory_space_constraint(support, pltpu.HBM),
+    )
 
     others = partners(lam, "col")
+    some, rest = halves(some)
     peak = functools.reduce(jnp.maximum, others, lam)
     mass = functools.reduce(jnp.add, [jnp.exp2(one - peak) for one in [lam, *others]])
     phi = -math.log2(total_cells) - (peak + jnp.log2(mass))
 
+    phi_some, phi_rest = halves(phi)
+    logits, tops, near, right = pl.pallas_call(
+        functools.partial(half_kernel, scale, float(total_support)),
+        out_shape=(
+            jax.ShapeDtypeStruct((half, share), jnp.float32),
+            row_vector(share),
+            row_vector(share),
+            jax.ShapeDtypeStruct((depth, share), jnp.bfloat16),
+        ),
+        in_specs=[VMEM] * 3,
+        out_specs=(VMEM,) * 4,
+        scratch_shapes=[pltpu.VMEM((half, depth), jnp.bfloat16)],
+        compiler_params=pltpu.CompilerParams(vmem_limit_bytes=24 << 20),
+        name="half",
+    )(some, phi_some, mine)
     e, r, base = pl.pallas_call(
         functools.partial(second_kernel, scale, float(total_support)),
         out_shape=(
@@ -277,16 +336,15 @@
             row_vector(total_cells),
             row_vector(share),
         ),
-        in_specs=[VMEM, VMEM, VMEM],
+        in_specs=[VMEM] * 6,
         out_specs=(VMEM, VMEM, VMEM),
         scratch_shapes=[
-            pltpu.VMEM((total_cells, depth), jnp.bfloat16),
-            pltpu.VMEM((depth, share), jnp.bfloat16),
+            pltpu.VMEM((half, depth), jnp.bfloat16),
             pltpu.VMEM((total_cells, LANES), jnp.float32),
         ],
         compiler_params=pltpu.CompilerParams(vmem_limit_bytes=32 << 20),
         name="second",
-    )(everyone, gather_rows(phi), mine)
+    )(logits, tops, near, right, rest, phi_rest)
 
     r = sum_rows(r)
     shares = [r, *partners(r, "col")]
@@ -303,11 +361,11 @@
     weights = pl.pallas_call(
         functools.partial(weights_kernel, float(total_cells)),
         out_shape=jax.ShapeDtypeStruct((2 * dims + 16, total_cells), jnp.bfloat16),
-        in_specs=[VMEM] * (1 + len(shares)),
+        in_specs=[VMEM] * (2 + len(shares)),
         out_specs=VMEM,
         compiler_params=pltpu.CompilerParams(vmem_limit_bytes=16 << 20),
         name="weights",
-    )(everyone, *shares)
+    )(some, rest, *shares)
 
     def third(key, width):
         return pl.pallas_call(

time: 47.5 us -> 46.9 us (0.987)
  waiting for transfers between devices: 14.2 us -> 15.2 us
  local copies, waits for them, and re-layouts: 1 us -> 0.02 us
  other arithmetic: 1.54 us -> 0.67 us
  Pallas kernels: 11.1 us -> 11.7 us
    ppermute x20, waiting for transfers between devices: 14.2 us -> 15.2 us  [exchange(): return lax.ppermute(value, axis, [(at, at ^ key) for at in range(size)])]
    dynamic_slice x1 -> x0, local copies, waits for them, and re-layouts: 0.97 us -> none  [shards(): mine = lax.dynamic_slice_in_dim(support, row_at * share, share, 1)]
    convert_element_type x1 -> x0, other arithmetic: 0.85 us -> none  [shards(): everyone = gather_rows(own.astype(jnp.float32))]
    pallas_call x0 -> x1, Pallas kernels: none -> 0.8 us  [shards(): pl.pallas_call(functools.partial(half_kernel, scale, float(total_support)...]
  transfers between devices with their start and end apart: 20 -> 20, of which waited for: 12 -> 13; matrix products, arithmetic and copies ran while one was open for 5% -> 1% of each run, Pallas kernels for 3% -> 5%
where the time goes in v5:
time: 46.9 us; the launch traced here: 46.7 us
  starting transfers between devices  18.4 us (39%)
  waiting for transfers between devices  15.2 us (32%)
  Pallas kernels  11.7 us (25%)
  between operations  0.74 us (2%)
  other arithmetic  0.67 us (1%)
    ppermute x20, starting transfers between devices, exchange(): return lax.ppermute(value, axis, [(at, at ^ key) for at in range(size)])  18.4 us
    ppermute x20, waiting for transfers between devices, exchange(): return lax.ppermute(value, axis, [(at, at ^ key) for at in range(size)])  15.2 us
    pallas_call x1, Pallas kernels, shards(): pl.pallas_call(functools.partial(first_kernel, scale), out_shape=(row_vec...  3.53 us
    pallas_call x1, Pallas kernels, shards(): pl.pallas_call(functools.partial(second_kernel, scale, float(total_suppor...  2.74 us
    pallas_call x4, Pallas kernels, third(): pl.pallas_call(functools.partial(third_kernel, key, dims), out_shape=(jax...  2.1 us
    pallas_call x1, Pallas kernels, shards(): pl.pallas_call(split_kernel, out_shape=(jax.ShapeDtypeStruct(e.shape, jnp...  1.41 us
    pallas_call x1, Pallas kernels, shards(): pl.pallas_call(functools.partial(assemble_kernel, atlases), out_shape=(ja...  1.06 us
  transfers between devices with their start and end apart: 20, of which 13 were waited for; matrix products, arithmetic and copies ran while one was open for 1% of the time, Pallas kernels for 5%

profile of v5, /device:TPU:0, one launch (start us, length us, event | category | flops | bytes accessed | tf_op | source)
XLA Modules:
  0.0 46.7 jit_solution(14711386102435945800)
XLA Ops:
  0.6 3.5 %first.1 = (f32[1,512]{1,0:T(1,128)S(1)}, f32[1,512]{1,0:T(1,128)S(1)}, bf16[64,2048]{1,0:T(8,128)(2,1)S(1)}, f32[64,512]{1,0:T(8,128)S(1)}) custom-call(bf16[64,512]{1,0:T(8,128)(2,1)} %bitcast.1, bf16[64,4096]{1,0:T(8,128)(2,1)} %y_hbm.1), custom_call_target="tpu_custom_call" | custom-call | tf_op jit(solution)/shard_map/first/pallas_call | solution.py:284
  4.2 5.1 %collective-permute-start.2 = (f32[1,512]{1,0:T(1,128)S(1)}, f32[1,512]{1,0:T(1,128)S(1)}, u32[]{:S(2)}, u32[]{:S(2)}) collective-permute-start(f32[1,512]{1,0:T(1,128)S(1)} %get-tuple-element.26), channel_id=1, source_target_pairs={{0,3},{1,2},{2,1},{3,0},{4,7},{5,6},{6,5},{7,4},{8,11},{9,10},{10,... | collective-permute-start | bytes 6152 | tf_op jit(solution)/shard_map/ppermute | solution.py:226
  9.3 0.6 %collective-permute-start = (f32[1,512]{1,0:T(1,128)S(1)}, f32[1,512]{1,0:T(1,128)S(1)}, u32[]{:S(2)}, u32[]{:S(2)}) collective-permute-start(f32[1,512]{1,0:T(1,128)S(1)} %get-tuple-element.26), channel_id=1, source_target_pairs={{0,1},{1,0},{2,3},{3,2},{4,5},{5,4},{6,7},{7,6},{8,9},{9,8},{10,11... | collective-permute-start | bytes 6152 | tf_op jit(solution)/shard_map/ppermute | solution.py:226
  10.0 0.9 %collective-permute-done.2 = f32[1,512]{1,0:T(1,128)S(1)} collective-permute-done((f32[1,512]{1,0:T(1,128)S(1)}, f32[1,512]{1,0:T(1,128)S(1)}, u32[]{:S(2)}, u32[]{:S(2)}) %collective-permute-start.2) | collective-permute-done | bytes 2080 | tf_op jit(solution)/shard_map/ppermute | solution.py:226
  10.9 2.9 %collective-permute-done.1 = f32[1,512]{1,0:T(1,128)S(1)} collective-permute-done((f32[1,512]{1,0:T(1,128)S(1)}, f32[1,512]{1,0:T(1,128)S(1)}, u32[]{:S(2)}, u32[]{:S(2)}) %collective-permute-start.1) | collective-permute-done | bytes 2080 | tf_op jit(solution)/shard_map/ppermute | solution.py:226
  13.9 0.8 %half.1 = (f32[512,2048]{1,0:T(8,128)S(1)}, f32[1,2048]{1,0:T(1,128)S(1)}, f32[1,2048]{1,0:T(1,128)S(1)}, bf16[208,2048]{1,0:T(8,128)(2,1)S(1)}) custom-call(f32[64,512]{1,0:T(8,128)S(1)} %get-tuple-element.28.x_ref.own_ref, f32[1,512]{1,0:T(1,128)S(1)} %add_subtract_fusion.phi_ref, bf16[64,2048]{1,0:T(8,128)(2,1)S(1)} %get-tuple-element.29.y_ref), custom_call_target="tpu_custom_call" | custom-call | tf_op jit(solution)/shard_map/half/pallas_call | solution.py:318
  14.7 0.3 collective-permute-done.4.phi_ref
  15.1 2.7 %second.1 = (f32[1024,2048]{1,0:T(8,128)S(1)}, f32[1,1024]{1,0:T(1,128)S(1)}, f32[1,2048]{1,0:T(1,128)S(1)}) custom-call(f32[512,2048]{1,0:T(8,128)S(1)} %get-tuple-element.30.b_ref, f32[1,2048]{1,0:T(1,128)S(1)} %get-tuple-element.31.top_ref, f32[1,2048]{1,0:T(1,128)S(1)} %get-tuple-element.32.near_ref, bf16[208,2048]{1,0:T(8,128)(2,1)S(1)} %get-tuple-element.33.right, ...), custom_call_target="tpu_custom_call" | custom-call | tf_op jit(solution)/shard_map/second/pallas_call | solution.py:332
  18.0 1.0 %collective-permute-done.5.other_ref = f32[1,1024]{1,0:T(1,128)S(1)} collective-permute-done((f32[1,1024]{1,0:T(1,128)S(1)}, f32[1,1024]{1,0:T(1,128)S(1)}, u32[]{:S(2)}, u32[]{:S(2)}) %collective-permute-start.5) | collective-permute-done | bytes 4128 | tf_op jit(solution)/shard_map/ppermute | solution.py:226
  19.0 1.5 %collective-permute-start.8 = (f32[1,1024]{1,0:T(1,128)S(1)}, f32[1,1024]{1,0:T(1,128)S(1)}, u32[]{:S(2)}, u32[]{:S(2)}) collective-permute-start(f32[1,1024]{1,0:T(1,128)S(1)} %meet.1.refs_0_.after_ref), channel_id=1, source_target_pairs={{0,3},{1,2},{2,1},{3,0},{4,7},{5,6},{6,5},{7,4},{8,11},{9,10},{10,... | collective-permute-start | bytes 12296 | tf_op jit(solution)/shard_map/ppermute | solution.py:226
  20.5 0.6 %collective-permute-start.7 = (f32[1,1024]{1,0:T(1,128)S(1)}, f32[1,1024]{1,0:T(1,128)S(1)}, u32[]{:S(2)}, u32[]{:S(2)}) collective-permute-start(f32[1,1024]{1,0:T(1,128)S(1)} %meet.1.refs_0_.after_ref), channel_id=1, source_target_pairs={{0,2},{1,3},{2,0},{3,1},{4,6},{5,7},{6,4},{7,5},{8,10},{9,11},{10,... | collective-permute-start | bytes 12296 | tf_op jit(solution)/shard_map/ppermute | solution.py:226
  21.1 2.3 %collective-permute-start.6 = (f32[1,1024]{1,0:T(1,128)S(1)}, f32[1,1024]{1,0:T(1,128)S(1)}, u32[]{:S(2)}, u32[]{:S(2)}) collective-permute-start(f32[1,1024]{1,0:T(1,128)S(1)} %meet.1.refs_0_.after_ref), channel_id=1, source_target_pairs={{0,1},{1,0},{2,3},{3,2},{4,5},{5,4},{6,7},{7,6},{8,9},{9,8},{10,11... | collective-permute-start | bytes 12296 | tf_op jit(solution)/shard_map/ppermute | solution.py:226
  23.4 1.4 %split.1 = (bf16[1024,2048]{1,0:T(8,128)(2,1)S(1)}, bf16[1024,2048]{1,0:T(8,128)(2,1)S(1)}) custom-call(f32[1024,2048]{1,0:T(8,128)S(1)} %get-tuple-element.35.e_ref, f32[1,1024]{1,0:T(1,128)S(1)} %meet.1.refs_0_.after_ref), custom_call_target="tpu_custom_call" | custom-call | flops 8388608 | bytes 16777216 | tf_op jit(solution)/shard_map/split/pallas_call | solution.py:352
  25.1 0.5 %third.7 = (f32[64,512]{1,0:T(8,128)S(1)}, f32[1,512]{1,0:T(1,128)S(1)}) custom-call(bf16[144,1024]{1,0:T(8,128)(2,1)S(1)} %weights.1.weights_ref, bf16[1024,2048]{1,0:T(8,128)(2,1)S(1)} %get-tuple-element.36.high_ref, bf16[1024,2048]{1,0:T(8,128)(2,1)S(1)} %get-tuple-element.37.low_ref, f32[1,2048]{1,0:T(1,128)S(1)} %get-tuple-element.38.base_ref), custom_call_target="tpu_custom_call" | custom-call | flops 234881024 | bytes 2097152 | tf_op jit(solution)/shard_map/third/pallas_call | solution.py:371
  25.7 0.5 %third.6 = (f32[64,512]{1,0:T(8,128)S(1)}, f32[1,512]{1,0:T(1,128)S(1)}) custom-call(bf16[144,1024]{1,0:T(8,128)(2,1)S(1)} %weights.1.weights_ref, bf16[1024,2048]{1,0:T(8,128)(2,1)S(1)} %get-tuple-element.36.high_ref, bf16[1024,2048]{1,0:T(8,128)(2,1)S(1)} %get-tuple-element.37.low_ref, f32[1,2048]{1,0:T(1,128)S(1)} %get-tuple-element.38.base_ref), custom_call_target="tpu_custom_call" | custom-call | flops 234881024 | bytes 2097152 | tf_op jit(solution)/shard_map/third/pallas_call | solution.py:371
  26.2 0.5 %third.5 = (f32[64,512]{1,0:T(8,128)S(1)}, f32[1,512]{1,0:T(1,128)S(1)}) custom-call(bf16[144,1024]{1,0:T(8,128)(2,1)S(1)} %weights.1.weights_ref, bf16[1024,2048]{1,0:T(8,128)(2,1)S(1)} %get-tuple-element.36.high_ref, bf16[1024,2048]{1,0:T(8,128)(2,1)S(1)} %get-tuple-element.37.low_ref, f32[1,2048]{1,0:T(1,128)S(1)} %get-tuple-element.38.base_ref), custom_call_target="tpu_custom_call" | custom-call | flops 234881024 | bytes 2097152 | tf_op jit(solution)/shard_map/third/pallas_call | solution.py:371
  26.7 0.5 %third.4 = (f32[64,512]{1,0:T(8,128)S(1)}, f32[1,512]{1,0:T(1,128)S(1)}) custom-call(bf16[144,1024]{1,0:T(8,128)(2,1)S(1)} %weights.1.weights_ref, bf16[1024,2048]{1,0:T(8,128)(2,1)S(1)} %get-tuple-element.36.high_ref, bf16[1024,2048]{1,0:T(8,128)(2,1)S(1)} %get-tuple-element.37.low_ref, f32[1,2048]{1,0:T(1,128)S(1)} %get-tuple-element.38.base_ref), custom_call_target="tpu_custom_call" | custom-call | flops 234881024 | bytes 2097152 | tf_op jit(solution)/shard_map/third/pallas_call | solution.py:371
  27.3 2.5 %collective-permute-start.9 = (f32[64,512]{1,0:T(8,128)S(1)}, f32[64,512]{1,0:T(8,128)S(1)}, u32[]{:S(2)}, u32[]{:S(2)}) collective-permute-start(f32[64,512]{1,0:T(8,128)S(1)} %get-tuple-element.40), channel_id=1, source_target_pairs={{0,24},{8,16},{16,8},{24,0},{1,25},{9,17},{17,9},{25,1},{2,26},{10... | collective-permute-start | bytes 393224 | tf_op jit(solution)/shard_map/ppermute | solution.py:226
  29.8 0.5 %collective-permute-start.10 = (f32[64,512]{1,0:T(8,128)S(1)}, f32[64,512]{1,0:T(8,128)S(1)}, u32[]{:S(2)}, u32[]{:S(2)}) collective-permute-start(f32[64,512]{1,0:T(8,128)S(1)} %get-tuple-element.41), channel_id=1, source_target_pairs={{0,16},{8,24},{16,0},{24,8},{1,17},{9,25},{17,1},{25,9},{2,18},{10... | collective-permute-start | bytes 393224 | tf_op jit(solution)/shard_map/ppermute | solution.py:226
  30.3 0.5 %collective-permute-start.11 = (f32[64,512]{1,0:T(8,128)S(1)}, f32[64,512]{1,0:T(8,128)S(1)}, u32[]{:S(2)}, u32[]{:S(2)}) collective-permute-start(f32[64,512]{1,0:T(8,128)S(1)} %get-tuple-element.42), channel_id=1, source_target_pairs={{0,8},{8,0},{16,24},{24,16},{1,9},{9,1},{17,25},{25,17},{2,10},{10... | collective-permute-start | bytes 393224 | tf_op jit(solution)/shard_map/ppermute | solution.py:226
  30.8 3.1 %collective-permute-done.9 = f32[64,512]{1,0:T(8,128)S(1)} collective-permute-done((f32[64,512]{1,0:T(8,128)S(1)}, f32[64,512]{1,0:T(8,128)S(1)}, u32[]{:S(2)}, u32[]{:S(2)}) %collective-permute-start.9) | collective-permute-done | bytes 131104 | tf_op jit(solution)/shard_map/ppermute | solution.py:226
  34.0 1.6 %collective-permute-done.10 = f32[64,512]{1,0:T(8,128)S(1)} collective-permute-done((f32[64,512]{1,0:T(8,128)S(1)}, f32[64,512]{1,0:T(8,128)S(1)}, u32[]{:S(2)}, u32[]{:S(2)}) %collective-permute-start.10) | collective-permute-done | bytes 131104 | tf_op jit(solution)/shard_map/ppermute | solution.py:226
  35.7 1.7 %collective-permute-start.14 = (f32[64,512]{1,0:T(8,128)S(1)}, f32[64,512]{1,0:T(8,128)S(1)}, u32[]{:S(2)}, u32[]{:S(2)}) collective-permute-start(f32[64,512]{1,0:T(8,128)S(1)} %add_multiply_fusion.refs_0_), channel_id=1, source_target_pairs={{0,24},{8,16},{16,8},{24,0},{1,25},{9,17},{17,9},{25,1},{2,26},{10... | collective-permute-start | bytes 393224 | tf_op jit(solution)/shard_map/ppermute | solution.py:226
  37.5 1.3 %collective-permute-start.13 = (f32[64,512]{1,0:T(8,128)S(1)}, f32[64,512]{1,0:T(8,128)S(1)}, u32[]{:S(2)}, u32[]{:S(2)}) collective-permute-start(f32[64,512]{1,0:T(8,128)S(1)} %add_multiply_fusion.refs_0_), channel_id=1, source_target_pairs={{0,16},{8,24},{16,0},{24,8},{1,17},{9,25},{17,1},{25,9},{2,18},{10... | collective-permute-start | bytes 393224 | tf_op jit(solution)/shard_map/ppermute | solution.py:226
  38.8 0.5 %collective-permute-start.12 = (f32[64,512]{1,0:T(8,128)S(1)}, f32[64,512]{1,0:T(8,128)S(1)}, u32[]{:S(2)}, u32[]{:S(2)}) collective-permute-start(f32[64,512]{1,0:T(8,128)S(1)} %add_multiply_fusion.refs_0_), channel_id=1, source_target_pairs={{0,8},{8,0},{16,24},{24,16},{1,9},{9,1},{17,25},{25,17},{2,10},{10... | collective-permute-start | bytes 393224 | tf_op jit(solution)/shard_map/ppermute | solution.py:226
  39.3 0.5 %collective-permute-start.15 = (f32[64,512]{1,0:T(8,128)S(1)}, f32[64,512]{1,0:T(8,128)S(1)}, u32[]{:S(2)}, u32[]{:S(2)}) collective-permute-start(f32[64,512]{1,0:T(8,128)S(1)} %add_multiply_fusion.refs_0_), channel_id=1, source_target_pairs={{0,4},{4,0},{1,5},{5,1},{2,6},{6,2},{3,7},{7,3},{8,12},{12,8},{9,1... | collective-permute-start | bytes 393224 | tf_op jit(solution)/shard_map/ppermute | solution.py:226
  39.8 2.9 %collective-permute-done.14.refs_3_ = f32[64,512]{1,0:T(8,128)S(1)} collective-permute-done((f32[64,512]{1,0:T(8,128)S(1)}, f32[64,512]{1,0:T(8,128)S(1)}, u32[]{:S(2)}, u32[]{:S(2)}) %collective-permute-start.14) | collective-permute-done | bytes 131104 | tf_op jit(solution)/shard_map/ppermute | solution.py:226
  42.7 1.4 %collective-permute-done.13.refs_2_ = f32[64,512]{1,0:T(8,128)S(1)} collective-permute-done((f32[64,512]{1,0:T(8,128)S(1)}, f32[64,512]{1,0:T(8,128)S(1)}, u32[]{:S(2)}, u32[]{:S(2)}) %collective-permute-start.13) | collective-permute-done | bytes 131104 | tf_op jit(solution)/shard_map/ppermute | solution.py:226
  44.3 0.3 collective-permute-start.16
  44.6 0.6 %subtract_multiply_fusion = f32[1,512]{1,0:T(1,128)} fusion(f32[1,512]{1,0:T(1,128)S(1)} %add_subtract_fusion.phi_ref, f32[1,512]{1,0:T(1,128)S(1)} %get-tuple-element.27, f32[1,1024]{1,0:T(1,128)S(1)} %collective-permute-done.8.refs_3_, f32[1,1024]{1,0:T(1,128)S(1)} %collective-permute-done.7.refs_2_, f32[1,1024]{1,0:T(1,128)S(1)} %collective-permute-done.6.refs_1_, ...), kind=kLoop, calls=%fused_computation.9 | loop fusion | flops 4096 | bytes 14336 | tf_op jit(solution)/shard_map/mul | solution.py:420
  45.4 0.2 collective-permute-done.16.refs_5_
  45.7 1.1 %assemble.1 = (f32[64,4096]{1,0:T(8,128)}, f32[1,4096]{1,0:T(1,128)}) custom-call(f32[64,512]{1,0:T(8,128)S(1)} %add_multiply_fusion.refs_0_, f32[64,512]{1,0:T(8,128)S(1)} %collective-permute-done.12.refs_1_, f32[64,512]{1,0:T(8,128)S(1)} %collective-permute-done.13.refs_2_, f32[64,512]{1,0:T(8,128)S(1)} %collective-permute-done.14.refs_3_, ...), custom_call_target="tpu_custom_call" | custom-call | tf_op jit(solution)/shard_map/assemble/pallas_call | solution.py:397
  (26 shorter events, 1.3 us)
Async XLA Ops:
  4.2 6.7 %collective-permute-start.2 = (f32[1,512]{1,0:T(1,128)S(1)}, f32[1,512]{1,0:T(1,128)S(1)}, u32[]{:S(2)}, u32[]{:S(2)}) collective-permute-start(f32[1,512]{1,0:T(1,128)S(1)} %get-tuple-element.26), channel_id=1, source_target_pairs={{0,3},{1,2},{2,1},{3,0},{4,7},{5,6},{6,5},{7,4},{8,11},{9,10},{10,... | collective-permute-start | bytes 6152 | tf_op jit(solution)/shard_map/ppermute | solution.py:226
  9.3 4.5 %collective-permute-start.1 = (f32[1,512]{1,0:T(1,128)S(1)}, f32[1,512]{1,0:T(1,128)S(1)}, u32[]{:S(2)}, u32[]{:S(2)}) collective-permute-start(f32[1,512]{1,0:T(1,128)S(1)} %get-tuple-element.26), channel_id=1, source_target_pairs={{0,2},{1,3},{2,0},{3,1},{4,6},{5,7},{6,4},{7,5},{8,10},{9,11},{10,... | collective-permute-start | bytes 6152 | tf_op jit(solution)/shard_map/ppermute | solution.py:226
  9.3 4.5 %collective-permute-start = (f32[1,512]{1,0:T(1,128)S(1)}, f32[1,512]{1,0:T(1,128)S(1)}, u32[]{:S(2)}, u32[]{:S(2)}) collective-permute-start(f32[1,512]{1,0:T(1,128)S(1)} %get-tuple-element.26), channel_id=1, source_target_pairs={{0,1},{1,0},{2,3},{3,2},{4,5},{5,4},{6,7},{7,6},{8,9},{9,8},{10,11... | collective-permute-start | bytes 6152 | tf_op jit(solution)/shard_map/ppermute | solution.py:226
  10.0 5.1 %collective-permute-start.3 = (f32[64,512]{1,0:T(8,128)S(1)}, f32[64,512]{1,0:T(8,128)S(1)}, u32[]{:S(2)}, u32[]{:S(2)}) collective-permute-start(f32[64,512]{1,0:T(8,128)S(1)} %get-tuple-element.28.x_ref.own_ref), channel_id=1, source_target_pairs={{0,4},{4,0},{1,5},{5,1},{2,6},{6,2},{3,7},{7,3},{8,12},{12,8},{9,1... | collective-permute-start | bytes 393224 | tf_op jit(solution)/shard_map/ppermute | solution.py:226
  13.8 1.2 %collective-permute-start.4 = (f32[1,512]{1,0:T(1,128)S(1)}, f32[1,512]{1,0:T(1,128)S(1)}, u32[]{:S(2)}, u32[]{:S(2)}) collective-permute-start(f32[1,512]{1,0:T(1,128)S(1)} %add_subtract_fusion.phi_ref), channel_id=1, source_target_pairs={{0,4},{4,0},{1,5},{5,1},{2,6},{6,2},{3,7},{7,3},{8,12},{12,8},{9,1... | collective-permute-start | bytes 6152 | tf_op jit(solution)/shard_map/ppermute | solution.py:226
  17.8 1.2 %collective-permute-start.5 = (f32[1,1024]{1,0:T(1,128)S(1)}, f32[1,1024]{1,0:T(1,128)S(1)}, u32[]{:S(2)}, u32[]{:S(2)}) collective-permute-start(f32[1,1024]{1,0:T(1,128)S(1)} %get-tuple-element.34.own_ref), channel_id=1, source_target_pairs={{0,4},{4,0},{1,5},{5,1},{2,6},{6,2},{3,7},{7,3},{8,12},{12,8},{9,1... | collective-permute-start | bytes 12296 | tf_op jit(solution)/shard_map/ppermute | solution.py:226
  19.0 5.8 %collective-permute-start.8 = (f32[1,1024]{1,0:T(1,128)S(1)}, f32[1,1024]{1,0:T(1,128)S(1)}, u32[]{:S(2)}, u32[]{:S(2)}) collective-permute-start(f32[1,1024]{1,0:T(1,128)S(1)} %meet.1.refs_0_.after_ref), channel_id=1, source_target_pairs={{0,3},{1,2},{2,1},{3,0},{4,7},{5,6},{6,5},{7,4},{8,11},{9,10},{10,... | collective-permute-start | bytes 12296 | tf_op jit(solution)/shard_map/ppermute | solution.py:226
  20.5 4.5 %collective-permute-start.7 = (f32[1,1024]{1,0:T(1,128)S(1)}, f32[1,1024]{1,0:T(1,128)S(1)}, u32[]{:S(2)}, u32[]{:S(2)}) collective-permute-start(f32[1,1024]{1,0:T(1,128)S(1)} %meet.1.refs_0_.after_ref), channel_id=1, source_target_pairs={{0,2},{1,3},{2,0},{3,1},{4,6},{5,7},{6,4},{7,5},{8,10},{9,11},{10,... | collective-permute-start | bytes 12296 | tf_op jit(solution)/shard_map/ppermute | solution.py:226
  21.1 3.9 %collective-permute-start.6 = (f32[1,1024]{1,0:T(1,128)S(1)}, f32[1,1024]{1,0:T(1,128)S(1)}, u32[]{:S(2)}, u32[]{:S(2)}) collective-permute-start(f32[1,1024]{1,0:T(1,128)S(1)} %meet.1.refs_0_.after_ref), channel_id=1, source_target_pairs={{0,1},{1,0},{2,3},{3,2},{4,5},{5,4},{6,7},{7,6},{8,9},{9,8},{10,11... | collective-permute-start | bytes 12296 | tf_op jit(solution)/shard_map/ppermute | solution.py:226
  27.3 6.7 %collective-permute-start.9 = (f32[64,512]{1,0:T(8,128)S(1)}, f32[64,512]{1,0:T(8,128)S(1)}, u32[]{:S(2)}, u32[]{:S(2)}) collective-permute-start(f32[64,512]{1,0:T(8,128)S(1)} %get-tuple-element.40), channel_id=1, source_target_pairs={{0,24},{8,16},{16,8},{24,0},{1,25},{9,17},{17,9},{25,1},{2,26},{10... | collective-permute-start | bytes 393224 | tf_op jit(solution)/shard_map/ppermute | solution.py:226
  29.8 5.8 %collective-permute-start.10 = (f32[64,512]{1,0:T(8,128)S(1)}, f32[64,512]{1,0:T(8,128)S(1)}, u32[]{:S(2)}, u32[]{:S(2)}) collective-permute-start(f32[64,512]{1,0:T(8,128)S(1)} %get-tuple-element.41), channel_id=1, source_target_pairs={{0,16},{8,24},{16,0},{24,8},{1,17},{9,25},{17,1},{25,9},{2,18},{10... | collective-permute-start | bytes 393224 | tf_op jit(solution)/shard_map/ppermute | solution.py:226
  30.3 5.4 %collective-permute-start.11 = (f32[64,512]{1,0:T(8,128)S(1)}, f32[64,512]{1,0:T(8,128)S(1)}, u32[]{:S(2)}, u32[]{:S(2)}) collective-permute-start(f32[64,512]{1,0:T(8,128)S(1)} %get-tuple-element.42), channel_id=1, source_target_pairs={{0,8},{8,0},{16,24},{24,16},{1,9},{9,1},{17,25},{25,17},{2,10},{10... | collective-permute-start | bytes 393224 | tf_op jit(solution)/shard_map/ppermute | solution.py:226
  35.7 7.0 %collective-permute-start.14 = (f32[64,512]{1,0:T(8,128)S(1)}, f32[64,512]{1,0:T(8,128)S(1)}, u32[]{:S(2)}, u32[]{:S(2)}) collective-permute-start(f32[64,512]{1,0:T(8,128)S(1)} %add_multiply_fusion.refs_0_), channel_id=1, source_target_pairs={{0,24},{8,16},{16,8},{24,0},{1,25},{9,17},{17,9},{25,1},{2,26},{10... | collective-permute-start | bytes 393224 | tf_op jit(solution)/shard_map/ppermute | solution.py:226
  37.5 6.6 %collective-permute-start.13 = (f32[64,512]{1,0:T(8,128)S(1)}, f32[64,512]{1,0:T(8,128)S(1)}, u32[]{:S(2)}, u32[]{:S(2)}) collective-permute-start(f32[64,512]{1,0:T(8,128)S(1)} %add_multiply_fusion.refs_0_), channel_id=1, source_target_pairs={{0,16},{8,24},{16,0},{24,8},{1,17},{9,25},{17,1},{25,9},{2,18},{10... | collective-permute-start | bytes 393224 | tf_op jit(solution)/shard_map/ppermute | solution.py:226
  38.8 5.5 %collective-permute-start.12 = (f32[64,512]{1,0:T(8,128)S(1)}, f32[64,512]{1,0:T(8,128)S(1)}, u32[]{:S(2)}, u32[]{:S(2)}) collective-permute-start(f32[64,512]{1,0:T(8,128)S(1)} %add_multiply_fusion.refs_0_), channel_id=1, source_target_pairs={{0,8},{8,0},{16,24},{24,16},{1,9},{9,1},{17,25},{25,17},{2,10},{10... | collective-permute-start | bytes 393224 | tf_op jit(solution)/shard_map/ppermute | solution.py:226
  39.3 5.9 %collective-permute-start.19 = (f32[1,2048]{1,0:T(1,128)S(1)}, f32[1,2048]{1,0:T(1,128)S(1)}, u32[]{:S(2)}, u32[]{:S(2)}) collective-permute-start(f32[1,2048]{1,0:T(1,128)S(1)} %constant_dynamic-update-slice_fusion.refs_8_), channel_id=1, source_target_pairs={{0,4},{4,0},{1,5},{5,1},{2,6},{6,2},{3,7},{7,3},{8,12},{12,8},{9,1... | collective-permute-start | bytes 24584 | tf_op jit(solution)/shard_map/ppermute | solution.py:226
  39.3 5.9 %collective-permute-start.15 = (f32[64,512]{1,0:T(8,128)S(1)}, f32[64,512]{1,0:T(8,128)S(1)}, u32[]{:S(2)}, u32[]{:S(2)}) collective-permute-start(f32[64,512]{1,0:T(8,128)S(1)} %add_multiply_fusion.refs_0_), channel_id=1, source_target_pairs={{0,4},{4,0},{1,5},{5,1},{2,6},{6,2},{3,7},{7,3},{8,12},{12,8},{9,1... | collective-permute-start | bytes 393224 | tf_op jit(solution)/shard_map/ppermute | solution.py:226
  42.7 2.5 %collective-permute-start.18 = (f32[64,512]{1,0:T(8,128)S(1)}, f32[64,512]{1,0:T(8,128)S(1)}, u32[]{:S(2)}, u32[]{:S(2)}) collective-permute-start(f32[64,512]{1,0:T(8,128)S(1)} %collective-permute-done.14.refs_3_), channel_id=1, source_target_pairs={{0,4},{4,0},{1,5},{5,1},{2,6},{6,2},{3,7},{7,3},{8,12},{12,8},{9,1... | collective-permute-start | bytes 393224 | tf_op jit(solution)/shard_map/ppermute | solution.py:226
  44.1 1.3 %collective-permute-start.17 = (f32[64,512]{1,0:T(8,128)S(1)}, f32[64,512]{1,0:T(8,128)S(1)}, u32[]{:S(2)}, u32[]{:S(2)}) collective-permute-start(f32[64,512]{1,0:T(8,128)S(1)} %collective-permute-done.13.refs_2_), channel_id=1, source_target_pairs={{0,4},{4,0},{1,5},{5,1},{2,6},{6,2},{3,7},{7,3},{8,12},{12,8},{9,1... | collective-permute-start | bytes 393224 | tf_op jit(solution)/shard_map/ppermute | solution.py:226
  44.3 1.3 %collective-permute-start.16 = (f32[64,512]{1,0:T(8,128)S(1)}, f32[64,512]{1,0:T(8,128)S(1)}, u32[]{:S(2)}, u32[]{:S(2)}) collective-permute-start(f32[64,512]{1,0:T(8,128)S(1)} %collective-permute-done.12.refs_1_), channel_id=1, source_target_pairs={{0,4},{4,0},{1,5},{5,1},{2,6},{6,2},{3,7},{7,3},{8,12},{12,8},{9,1... | collective-permute-start | bytes 393224 | tf_op jit(solution)/shard_map/ppermute | solution.py:226

commit v6 on v5

--- a/solution.py
+++ b/solution.py
@@ -109,7 +109,19 @@
     left[...] = jnp.concatenate([*pieces(wide), pad_rows(pieces(phi_ref[...]))], axis=0).T
 
 
-def half_kernel(scale, points, x_ref, phi_ref, y_ref, b_ref, peak_ref, base_ref, right, left):
+def exponentials(ref, span, peak):
+    total = None
+    for low in range(0, ref.shape[0], SUBLANES):
+        rows = slice(low, low + SUBLANES)
+        expo = jnp.exp2(ref[rows, span] - peak)
+        ref[rows, span] = expo
+        total = expo if total is None else total + expo
+    return jnp.sum(total, axis=0, keepdims=True)
+
+
+def half_kernel(
+    scale, points, x_ref, phi_ref, y_ref, b_ref, peak_ref, sum_ref, base_ref, right, left
+):
     columns = b_ref.shape[1]
     block = min(256, columns)
     logit_block(scale, x_ref, phi_ref, left)
@@ -121,36 +133,36 @@
         span = slice(start, start + block)
         part = jnp.dot(left[...], right[:, span], preferred_element_type=jnp.float32)
         b_ref[:, span] = part
-        peak_ref[:, span] = jnp.max(fold(jnp.maximum, part), axis=0, keepdims=True)
+        peak = jnp.max(fold(jnp.maximum, part), axis=0, keepdims=True)
+        peak_ref[:, span] = peak
+        sum_ref[:, span] = exponentials(b_ref, span, peak)
 
 
 def second_kernel(
-    scale, points, b_ref, top_ref, near_ref, right, x_ref, phi_ref, e_ref, r_ref, base_ref, left, part_r
+    scale, points, b_ref, top_ref, sum_ref, near_ref, right, x_ref, phi_ref,
+    e_ref, factor_ref, r_ref, base_ref, left, part_r,
 ):
-    half = b_ref.shape[0]
-    cells, columns = e_ref.shape
+    half, columns = e_ref.shape
     block = min(256, columns)
     height = min(64, half)
     logit_block(scale, x_ref, phi_ref, left)
     for start in range(0, columns, block):
         span = slice(start, start + block)
         part = jnp.dot(left[...], right[:, span], preferred_element_type=jnp.float32)
-        e_ref[half:, span] = part
+        e_ref[:, span] = part
         peak = jnp.max(fold(jnp.maximum, part), axis=0, keepdims=True)
         peak = jnp.maximum(peak, top_ref[:, span])
         base_ref[:, span] = near_ref[:, span] - peak
-        total = None
-        for low in range(0, cells, SUBLANES):
-            rows = slice(low, low + SUBLANES)
-            expo = jnp.exp2((b_ref if low < half else e_ref)[rows, span] - peak)
-            e_ref[rows, span] = expo
-            total = expo if total is None else total + expo
-        weight = 1.0 / (points * jnp.sum(total, axis=0, keepdims=True))
-        for low in range(0, cells, height):
-            rows = slice(low, low + height)
-            share = e_ref[rows, span] * weight
-            row = functools.reduce(jnp.add, [share[:, tile] for tile in lane_tiles(block)])
-            part_r[rows, :] = row if start == 0 else part_r[rows, :] + row
+        factor = jnp.exp2(top_ref[:, span] - peak)
+        factor_ref[:, span] = factor
+        total = exponentials(e_ref, span, peak) + factor * sum_ref[:, span]
+        weight = 1.0 / (points * total)
+        for at, (ref, share) in enumerate(((b_ref, factor * weight), (e_ref, weight))):
+            for low in range(0, half, height):
+                held = ref[low : low + height, span] * share
+                row = functools.reduce(jnp.add, [held[:, tile] for tile in lane_tiles(block)])
+                rows = slice(at * half + low, at * half + low + height)
+                part_r[rows, :] = row if start == 0 else part_r[rows, :] + row
     r_ref[...] = jnp.sum(part_r[...].T, axis=0, keepdims=True)
 
 
@@ -160,17 +172,26 @@
     out_ref[:, rows:] = own_ref[:, rows:] + other_ref[:, :rows]
 
 
-def split_kernel(e_ref, after_ref, high_ref, low_ref):
+def split_kernel(b_ref, e_ref, factor_ref, after_ref, high_ref, low_ref):
     del after_ref
-    height = min(32, e_ref.shape[0])
-
-    @pl.loop(0, e_ref.shape[0] // height)
-    def _(at):
-        span = pl.ds(pl.multiple_of(at * height, height), height)
-        e = e_ref[span, :]
+    half = e_ref.shape[0]
+    height = min(32, half)
+
+    def put(at, e):
+        span = pl.ds(pl.multiple_of(at, height), height)
         high = e.astype(jnp.bfloat16)
         high_ref[span, :] = high
         low_ref[span, :] = (e - high.astype(jnp.float32)).astype(jnp.bfloat16)
+
+    @pl.loop(0, half // height)
+    def _(at):
+        low = pl.multiple_of(at * height, height)
+        put(low, b_ref[pl.ds(low, height), :] * factor_ref[...])
+
+    @pl.loop(0, half // height)
+    def _(at):
+        low = pl.multiple_of(at * height, height)
+        put(half + low, e_ref[pl.ds(low, height), :])
 
 
 def weights_kernel(count, own_ref, other_ref, *refs):
@@ -315,49 +336,51 @@
     phi = -math.log2(total_cells) - (peak + jnp.log2(mass))
 
     phi_some, phi_rest = halves(phi)
-    logits, tops, near, right = pl.pallas_call(
+    some_e, tops, masses, near, right = pl.pallas_call(
         functools.partial(half_kernel, scale, float(total_support)),
         out_shape=(
             jax.ShapeDtypeStruct((half, share), jnp.float32),
             row_vector(share),
             row_vector(share),
+            row_vector(share),
             jax.ShapeDtypeStruct((depth, share), jnp.bfloat16),
         ),
         in_specs=[VMEM] * 3,
-        out_specs=(VMEM,) * 4,
+        out_specs=(VMEM,) * 5,
         scratch_shapes=[pltpu.VMEM((half, depth), jnp.bfloat16)],
         compiler_params=pltpu.CompilerParams(vmem_limit_bytes=24 << 20),
         name="half",
     )(some, phi_some, mine)
-    e, r, base = pl.pallas_call(
+    rest_e, factor, r, base = pl.pallas_call(
         functools.partial(second_kernel, scale, float(total_support)),
         out_shape=(
-            jax.ShapeDtypeStruct((total_cells, share), jnp.float32),
+            jax.ShapeDtypeStruct((half, share), jnp.float32),
+            row_vector(share),
             row_vector(total_cells),
             row_vector(share),
         ),
-        in_specs=[VMEM] * 6,
-        out_specs=(VMEM, VMEM, VMEM),
+        in_specs=[VMEM] * 7,
+        out_specs=(VMEM,) * 4,
         scratch_shapes=[
             pltpu.VMEM((half, depth), jnp.bfloat16),
             pltpu.VMEM((total_cells, LANES), jnp.float32),
         ],
         compiler_params=pltpu.CompilerParams(vmem_limit_bytes=32 << 20),
         name="second",
-    )(logits, tops, near, right, rest, phi_rest)
+    )(some_e, tops, masses, near, right, rest, phi_rest)
 
     r = sum_rows(r)
     shares = [r, *partners(r, "col")]
 
     high, low = pl.pallas_call(
         split_kernel,
-        out_shape=(jax.ShapeDtypeStruct(e.shape, jnp.bfloat16),) * 2,
-        in_specs=[VMEM, VMEM],
+        out_shape=(jax.ShapeDtypeStruct((total_cells, share), jnp.bfloat16),) * 2,
+        in_specs=[VMEM] * 4,
         out_specs=(VMEM, VMEM),
         compiler_params=pltpu.CompilerParams(vmem_limit_bytes=24 << 20),
-        cost_estimate=pl.CostEstimate(flops=e.size * 4, bytes_accessed=e.size * 8, transcendentals=0),
+        cost_estimate=pl.CostEstimate(flops=total_cells * share * 4, bytes_accessed=total_cells * share * 8, transcendentals=0),
         name="split",
-    )(e, r)
+    )(some_e, rest_e, factor, r)
     weights = pl.pallas_call(
         functools.partial(weights_kernel, float(total_cells)),
         out_shape=jax.ShapeDtypeStruct((2 * dims + 16, total_cells), jnp.bfloat16),

time: 46.9 us -> 46.9 us (level)
    pallas_call x1, Pallas kernels: 2.74 us -> 1.86 us  [shards(): pl.pallas_call(functools.partial(second_kernel, scale, float(total_suppor...]
    pallas_call x1, Pallas kernels: 0.8 us -> 1.34 us  [shards(): pl.pallas_call(functools.partial(half_kernel, scale, float(total_support)...]
  transfers between devices with their start and end apart: 20 -> 20, of which waited for: 13 -> 12; matrix products, arithmetic and copies ran while one was open for 1% -> 1% of each run, Pallas kernels for 5% -> 6%
where the time goes in v6:
time: 46.9 us; the launch traced here: 46.8 us
  starting transfers between devices  18.8 us (40%)
  waiting for transfers between devices  15 us (32%)
  Pallas kernels  11.5 us (25%)
  between operations  0.74 us (2%)
  other arithmetic  0.67 us (1%)
    ppermute x20, starting transfers between devices, exchange(): return lax.ppermute(value, axis, [(at, at ^ key) for at in range(size)])  18.8 us
    ppermute x20, waiting for transfers between devices, exchange(): return lax.ppermute(value, axis, [(at, at ^ key) for at in range(size)])  15 us
    pallas_call x1, Pallas kernels, shards(): pl.pallas_call(functools.partial(first_kernel, scale), out_shape=(row_vec...  3.53 us
    pallas_call x4, Pallas kernels, third(): pl.pallas_call(functools.partial(third_kernel, key, dims), out_shape=(jax...  2.1 us
    pallas_call x1, Pallas kernels, shards(): pl.pallas_call(functools.partial(second_kernel, scale, float(total_suppor...  1.86 us
    pallas_call x1, Pallas kernels, shards(): pl.pallas_call(split_kernel, out_shape=(jax.ShapeDtypeStruct((total_cells...  1.48 us
    pallas_call x1, Pallas kernels, shards(): pl.pallas_call(functools.partial(half_kernel, scale, float(total_support)...  1.34 us
    pallas_call x1, Pallas kernels, shards(): pl.pallas_call(functools.partial(assemble_kernel, atlases), out_shape=(ja...  1.06 us
  transfers between devices with their start and end apart: 20, of which 12 were waited for; matrix products, arithmetic and copies ran while one was open for 1% of the time, Pallas kernels for 6%

profile of v6, /device:TPU:0, one launch (start us, length us, event | category | flops | bytes accessed | tf_op | source)
XLA Modules:
  0.0 46.8 jit_solution(5692536051255090839)
XLA Ops:
  0.6 3.5 %first.1 = (f32[1,512]{1,0:T(1,128)S(1)}, f32[1,512]{1,0:T(1,128)S(1)}, bf16[64,2048]{1,0:T(8,128)(2,1)S(1)}, f32[64,512]{1,0:T(8,128)S(1)}) custom-call(bf16[64,512]{1,0:T(8,128)(2,1)} %bitcast.1, bf16[64,4096]{1,0:T(8,128)(2,1)} %y_hbm.1), custom_call_target="tpu_custom_call" | custom-call | tf_op jit(solution)/shard_map/first/pallas_call | solution.py:305
  4.2 5.1 %collective-permute-start.2 = (f32[1,512]{1,0:T(1,128)S(1)}, f32[1,512]{1,0:T(1,128)S(1)}, u32[]{:S(2)}, u32[]{:S(2)}) collective-permute-start(f32[1,512]{1,0:T(1,128)S(1)} %get-tuple-element.28), channel_id=1, source_target_pairs={{0,3},{1,2},{2,1},{3,0},{4,7},{5,6},{6,5},{7,4},{8,11},{9,10},{10,... | collective-permute-start | bytes 6152 | tf_op jit(solution)/shard_map/ppermute | solution.py:247
  9.3 0.6 %collective-permute-start = (f32[1,512]{1,0:T(1,128)S(1)}, f32[1,512]{1,0:T(1,128)S(1)}, u32[]{:S(2)}, u32[]{:S(2)}) collective-permute-start(f32[1,512]{1,0:T(1,128)S(1)} %get-tuple-element.28), channel_id=1, source_target_pairs={{0,1},{1,0},{2,3},{3,2},{4,5},{5,4},{6,7},{7,6},{8,9},{9,8},{10,11... | collective-permute-start | bytes 6152 | tf_op jit(solution)/shard_map/ppermute | solution.py:247
  10.0 0.9 %collective-permute-done.2 = f32[1,512]{1,0:T(1,128)S(1)} collective-permute-done((f32[1,512]{1,0:T(1,128)S(1)}, f32[1,512]{1,0:T(1,128)S(1)}, u32[]{:S(2)}, u32[]{:S(2)}) %collective-permute-start.2) | collective-permute-done | bytes 2080 | tf_op jit(solution)/shard_map/ppermute | solution.py:247
  10.9 2.9 %collective-permute-done.1 = f32[1,512]{1,0:T(1,128)S(1)} collective-permute-done((f32[1,512]{1,0:T(1,128)S(1)}, f32[1,512]{1,0:T(1,128)S(1)}, u32[]{:S(2)}, u32[]{:S(2)}) %collective-permute-start.1) | collective-permute-done | bytes 2080 | tf_op jit(solution)/shard_map/ppermute | solution.py:247
  13.9 1.3 %half.1 = (f32[512,2048]{1,0:T(8,128)S(1)}, f32[1,2048]{1,0:T(1,128)S(1)}, f32[1,2048]{1,0:T(1,128)S(1)}, f32[1,2048]{1,0:T(1,128)S(1)}, bf16[208,2048]{1,0:T(8,128)(2,1)S(1)}) custom-call(f32[64,512]{1,0:T(8,128)S(1)} %get-tuple-element.30.x_ref.own_ref, f32[1,512]{1,0:T(1,128)S(1)} %add_subtract_fusion.phi_ref, bf16[64,2048]{1,0:T(8,128)(2,1)S(1)} %get-tuple-element.31.y_ref), custom_call_target="tpu_custom_call" | custom-call | tf_op jit(solution)/shard_map/half/pallas_call | solution.py:339
  15.3 1.9 %second.1 = (f32[512,2048]{1,0:T(8,128)S(1)}, f32[1,2048]{1,0:T(1,128)S(1)}, f32[1,1024]{1,0:T(1,128)S(1)}, f32[1,2048]{1,0:T(1,128)S(1)}) custom-call(f32[512,2048]{1,0:T(8,128)S(1)} %get-tuple-element.32.b_ref, f32[1,2048]{1,0:T(1,128)S(1)} %get-tuple-element.33.top_ref, f32[1,2048]{1,0:T(1,128)S(1)} %get-tuple-element.34.sum_ref, ...), custom_call_target="tpu_custom_call" | custom-call | tf_op jit(solution)/shard_map/second/pallas_call | solution.py:354
  17.1 0.6 %collective-permute-start.5 = (f32[1,1024]{1,0:T(1,128)S(1)}, f32[1,1024]{1,0:T(1,128)S(1)}, u32[]{:S(2)}, u32[]{:S(2)}) collective-permute-start(f32[1,1024]{1,0:T(1,128)S(1)} %get-tuple-element.37.own_ref), channel_id=1, source_target_pairs={{0,4},{4,0},{1,5},{5,1},{2,6},{6,2},{3,7},{7,3},{8,12},{12,8},{9,1... | collective-permute-start | bytes 12296 | tf_op jit(solution)/shard_map/ppermute | solution.py:247
  17.7 0.8 %collective-permute-done.5.other_ref = f32[1,1024]{1,0:T(1,128)S(1)} collective-permute-done((f32[1,1024]{1,0:T(1,128)S(1)}, f32[1,1024]{1,0:T(1,128)S(1)}, u32[]{:S(2)}, u32[]{:S(2)}) %collective-permute-start.5) | collective-permute-done | bytes 4128 | tf_op jit(solution)/shard_map/ppermute | solution.py:247
  18.5 1.5 %collective-permute-start.8 = (f32[1,1024]{1,0:T(1,128)S(1)}, f32[1,1024]{1,0:T(1,128)S(1)}, u32[]{:S(2)}, u32[]{:S(2)}) collective-permute-start(f32[1,1024]{1,0:T(1,128)S(1)} %meet.1.refs_0_.after_ref), channel_id=1, source_target_pairs={{0,3},{1,2},{2,1},{3,0},{4,7},{5,6},{6,5},{7,4},{8,11},{9,10},{10,... | collective-permute-start | bytes 12296 | tf_op jit(solution)/shard_map/ppermute | solution.py:247
  20.0 0.6 %collective-permute-start.7 = (f32[1,1024]{1,0:T(1,128)S(1)}, f32[1,1024]{1,0:T(1,128)S(1)}, u32[]{:S(2)}, u32[]{:S(2)}) collective-permute-start(f32[1,1024]{1,0:T(1,128)S(1)} %meet.1.refs_0_.after_ref), channel_id=1, source_target_pairs={{0,2},{1,3},{2,0},{3,1},{4,6},{5,7},{6,4},{7,5},{8,10},{9,11},{10,... | collective-permute-start | bytes 12296 | tf_op jit(solution)/shard_map/ppermute | solution.py:247
  20.6 2.4 %collective-permute-start.6 = (f32[1,1024]{1,0:T(1,128)S(1)}, f32[1,1024]{1,0:T(1,128)S(1)}, u32[]{:S(2)}, u32[]{:S(2)}) collective-permute-start(f32[1,1024]{1,0:T(1,128)S(1)} %meet.1.refs_0_.after_ref), channel_id=1, source_target_pairs={{0,1},{1,0},{2,3},{3,2},{4,5},{5,4},{6,7},{7,6},{8,9},{9,8},{10,11... | collective-permute-start | bytes 12296 | tf_op jit(solution)/shard_map/ppermute | solution.py:247
  22.9 1.5 %split.1 = (bf16[1024,2048]{1,0:T(8,128)(2,1)S(1)}, bf16[1024,2048]{1,0:T(8,128)(2,1)S(1)}) custom-call(f32[512,2048]{1,0:T(8,128)S(1)} %get-tuple-element.32.b_ref, f32[512,2048]{1,0:T(8,128)S(1)} %get-tuple-element.38.e_ref, f32[1,2048]{1,0:T(1,128)S(1)} %get-tuple-element.39.factor_ref, f32[1,1024]{1,0:T(1,128)S(1)} %meet.1.refs_0_.after_ref), custom_call_target="tpu_custom_call" | custom-call | flops 8388608 | bytes 16777216 | tf_op jit(solution)/shard_map/split/pallas_call | solution.py:375
  24.6 0.5 %third.7 = (f32[64,512]{1,0:T(8,128)S(1)}, f32[1,512]{1,0:T(1,128)S(1)}) custom-call(bf16[144,1024]{1,0:T(8,128)(2,1)S(1)} %weights.1.weights_ref, bf16[1024,2048]{1,0:T(8,128)(2,1)S(1)} %get-tuple-element.40.high_ref, bf16[1024,2048]{1,0:T(8,128)(2,1)S(1)} %get-tuple-element.41.low_ref, f32[1,2048]{1,0:T(1,128)S(1)} %get-tuple-element.42.base_ref), custom_call_target="tpu_custom_call" | custom-call | flops 234881024 | bytes 2097152 | tf_op jit(solution)/shard_map/third/pallas_call | solution.py:394
  25.2 0.5 %third.6 = (f32[64,512]{1,0:T(8,128)S(1)}, f32[1,512]{1,0:T(1,128)S(1)}) custom-call(bf16[144,1024]{1,0:T(8,128)(2,1)S(1)} %weights.1.weights_ref, bf16[1024,2048]{1,0:T(8,128)(2,1)S(1)} %get-tuple-element.40.high_ref, bf16[1024,2048]{1,0:T(8,128)(2,1)S(1)} %get-tuple-element.41.low_ref, f32[1,2048]{1,0:T(1,128)S(1)} %get-tuple-element.42.base_ref), custom_call_target="tpu_custom_call" | custom-call | flops 234881024 | bytes 2097152 | tf_op jit(solution)/shard_map/third/pallas_call | solution.py:394
  25.7 0.5 %third.5 = (f32[64,512]{1,0:T(8,128)S(1)}, f32[1,512]{1,0:T(1,128)S(1)}) custom-call(bf16[144,1024]{1,0:T(8,128)(2,1)S(1)} %weights.1.weights_ref, bf16[1024,2048]{1,0:T(8,128)(2,1)S(1)} %get-tuple-element.40.high_ref, bf16[1024,2048]{1,0:T(8,128)(2,1)S(1)} %get-tuple-element.41.low_ref, f32[1,2048]{1,0:T(1,128)S(1)} %get-tuple-element.42.base_ref), custom_call_target="tpu_custom_call" | custom-call | flops 234881024 | bytes 2097152 | tf_op jit(solution)/shard_map/third/pallas_call | solution.py:394
  26.2 0.5 %third.4 = (f32[64,512]{1,0:T(8,128)S(1)}, f32[1,512]{1,0:T(1,128)S(1)}) custom-call(bf16[144,1024]{1,0:T(8,128)(2,1)S(1)} %weights.1.weights_ref, bf16[1024,2048]{1,0:T(8,128)(2,1)S(1)} %get-tuple-element.40.high_ref, bf16[1024,2048]{1,0:T(8,128)(2,1)S(1)} %get-tuple-element.41.low_ref, f32[1,2048]{1,0:T(1,128)S(1)} %get-tuple-element.42.base_ref), custom_call_target="tpu_custom_call" | custom-call | flops 234881024 | bytes 2097152 | tf_op jit(solution)/shard_map/third/pallas_call | solution.py:394
  26.8 2.5 %collective-permute-start.9 = (f32[64,512]{1,0:T(8,128)S(1)}, f32[64,512]{1,0:T(8,128)S(1)}, u32[]{:S(2)}, u32[]{:S(2)}) collective-permute-start(f32[64,512]{1,0:T(8,128)S(1)} %get-tuple-element.44), channel_id=1, source_target_pairs={{0,24},{8,16},{16,8},{24,0},{1,25},{9,17},{17,9},{25,1},{2,26},{10... | collective-permute-start | bytes 393224 | tf_op jit(solution)/shard_map/ppermute | solution.py:247
  29.2 0.5 %collective-permute-start.10 = (f32[64,512]{1,0:T(8,128)S(1)}, f32[64,512]{1,0:T(8,128)S(1)}, u32[]{:S(2)}, u32[]{:S(2)}) collective-permute-start(f32[64,512]{1,0:T(8,128)S(1)} %get-tuple-element.45), channel_id=1, source_target_pairs={{0,16},{8,24},{16,0},{24,8},{1,17},{9,25},{17,1},{25,9},{2,18},{10... | collective-permute-start | bytes 393224 | tf_op jit(solution)/shard_map/ppermute | solution.py:247
  29.8 0.6 %collective-permute-start.11 = (f32[64,512]{1,0:T(8,128)S(1)}, f32[64,512]{1,0:T(8,128)S(1)}, u32[]{:S(2)}, u32[]{:S(2)}) collective-permute-start(f32[64,512]{1,0:T(8,128)S(1)} %get-tuple-element.46), channel_id=1, source_target_pairs={{0,8},{8,0},{16,24},{24,16},{1,9},{9,1},{17,25},{25,17},{2,10},{10... | collective-permute-start | bytes 393224 | tf_op jit(solution)/shard_map/ppermute | solution.py:247
  30.3 2.9 %collective-permute-done.9 = f32[64,512]{1,0:T(8,128)S(1)} collective-permute-done((f32[64,512]{1,0:T(8,128)S(1)}, f32[64,512]{1,0:T(8,128)S(1)}, u32[]{:S(2)}, u32[]{:S(2)}) %collective-permute-start.9) | collective-permute-done | bytes 131104 | tf_op jit(solution)/shard_map/ppermute | solution.py:247
  33.2 2.1 %collective-permute-done.10 = f32[64,512]{1,0:T(8,128)S(1)} collective-permute-done((f32[64,512]{1,0:T(8,128)S(1)}, f32[64,512]{1,0:T(8,128)S(1)}, u32[]{:S(2)}, u32[]{:S(2)}) %collective-permute-start.10) | collective-permute-done | bytes 131104 | tf_op jit(solution)/shard_map/ppermute | solution.py:247
  35.5 1.7 %collective-permute-start.14 = (f32[64,512]{1,0:T(8,128)S(1)}, f32[64,512]{1,0:T(8,128)S(1)}, u32[]{:S(2)}, u32[]{:S(2)}) collective-permute-start(f32[64,512]{1,0:T(8,128)S(1)} %add_multiply_fusion.refs_0_), channel_id=1, source_target_pairs={{0,24},{8,16},{16,8},{24,0},{1,25},{9,17},{17,9},{25,1},{2,26},{10... | collective-permute-start | bytes 393224 | tf_op jit(solution)/shard_map/ppermute | solution.py:247
  37.2 1.3 %collective-permute-start.13 = (f32[64,512]{1,0:T(8,128)S(1)}, f32[64,512]{1,0:T(8,128)S(1)}, u32[]{:S(2)}, u32[]{:S(2)}) collective-permute-start(f32[64,512]{1,0:T(8,128)S(1)} %add_multiply_fusion.refs_0_), channel_id=1, source_target_pairs={{0,16},{8,24},{16,0},{24,8},{1,17},{9,25},{17,1},{25,9},{2,18},{10... | collective-permute-start | bytes 393224 | tf_op jit(solution)/shard_map/ppermute | solution.py:247
  38.5 0.5 %collective-permute-start.12 = (f32[64,512]{1,0:T(8,128)S(1)}, f32[64,512]{1,0:T(8,128)S(1)}, u32[]{:S(2)}, u32[]{:S(2)}) collective-permute-start(f32[64,512]{1,0:T(8,128)S(1)} %add_multiply_fusion.refs_0_), channel_id=1, source_target_pairs={{0,8},{8,0},{16,24},{24,16},{1,9},{9,1},{17,25},{25,17},{2,10},{10... | collective-permute-start | bytes 393224 | tf_op jit(solution)/shard_map/ppermute | solution.py:247
  39.0 0.5 %collective-permute-start.15 = (f32[64,512]{1,0:T(8,128)S(1)}, f32[64,512]{1,0:T(8,128)S(1)}, u32[]{:S(2)}, u32[]{:S(2)}) collective-permute-start(f32[64,512]{1,0:T(8,128)S(1)} %add_multiply_fusion.refs_0_), channel_id=1, source_target_pairs={{0,4},{4,0},{1,5},{5,1},{2,6},{6,2},{3,7},{7,3},{8,12},{12,8},{9,1... | collective-permute-start | bytes 393224 | tf_op jit(solution)/shard_map/ppermute | solution.py:247
  39.5 3.2 %collective-permute-done.14.refs_3_ = f32[64,512]{1,0:T(8,128)S(1)} collective-permute-done((f32[64,512]{1,0:T(8,128)S(1)}, f32[64,512]{1,0:T(8,128)S(1)}, u32[]{:S(2)}, u32[]{:S(2)}) %collective-permute-start.14) | collective-permute-done | bytes 131104 | tf_op jit(solution)/shard_map/ppermute | solution.py:247
  42.7 1.4 %collective-permute-done.13.refs_2_ = f32[64,512]{1,0:T(8,128)S(1)} collective-permute-done((f32[64,512]{1,0:T(8,128)S(1)}, f32[64,512]{1,0:T(8,128)S(1)}, u32[]{:S(2)}, u32[]{:S(2)}) %collective-permute-start.13) | collective-permute-done | bytes 131104 | tf_op jit(solution)/shard_map/ppermute | solution.py:247
  44.3 0.4 collective-permute-start.16
  44.7 0.6 %subtract_multiply_fusion = f32[1,512]{1,0:T(1,128)} fusion(f32[1,512]{1,0:T(1,128)S(1)} %add_subtract_fusion.phi_ref, f32[1,512]{1,0:T(1,128)S(1)} %get-tuple-element.29, f32[1,1024]{1,0:T(1,128)S(1)} %collective-permute-done.8.refs_3_, f32[1,1024]{1,0:T(1,128)S(1)} %collective-permute-done.7.refs_2_, f32[1,1024]{1,0:T(1,128)S(1)} %collective-permute-done.6.refs_1_, ...), kind=kLoop, calls=%fused_computation.9 | loop fusion | flops 4096 | bytes 14336 | tf_op jit(solution)/shard_map/mul | solution.py:443
  45.3 0.2 collective-permute-done.17.refs_6_
  45.7 1.1 %assemble.1 = (f32[64,4096]{1,0:T(8,128)}, f32[1,4096]{1,0:T(1,128)}) custom-call(f32[64,512]{1,0:T(8,128)S(1)} %add_multiply_fusion.refs_0_, f32[64,512]{1,0:T(8,128)S(1)} %collective-permute-done.12.refs_1_, f32[64,512]{1,0:T(8,128)S(1)} %collective-permute-done.13.refs_2_, f32[64,512]{1,0:T(8,128)S(1)} %collective-permute-done.14.refs_3_, ...), custom_call_target="tpu_custom_call" | custom-call | tf_op jit(solution)/shard_map/assemble/pallas_call | solution.py:420
  (26 shorter events, 0.8 us)
Async XLA Ops:
  4.2 6.7 %collective-permute-start.2 = (f32[1,512]{1,0:T(1,128)S(1)}, f32[1,512]{1,0:T(1,128)S(1)}, u32[]{:S(2)}, u32[]{:S(2)}) collective-permute-start(f32[1,512]{1,0:T(1,128)S(1)} %get-tuple-element.28), channel_id=1, source_target_pairs={{0,3},{1,2},{2,1},{3,0},{4,7},{5,6},{6,5},{7,4},{8,11},{9,10},{10,... | collective-permute-start | bytes 6152 | tf_op jit(solution)/shard_map/ppermute | solution.py:247
  9.3 4.5 %collective-permute-start.1 = (f32[1,512]{1,0:T(1,128)S(1)}, f32[1,512]{1,0:T(1,128)S(1)}, u32[]{:S(2)}, u32[]{:S(2)}) collective-permute-start(f32[1,512]{1,0:T(1,128)S(1)} %get-tuple-element.28), channel_id=1, source_target_pairs={{0,2},{1,3},{2,0},{3,1},{4,6},{5,7},{6,4},{7,5},{8,10},{9,11},{10,... | collective-permute-start | bytes 6152 | tf_op jit(solution)/shard_map/ppermute | solution.py:247
  9.3 4.5 %collective-permute-start = (f32[1,512]{1,0:T(1,128)S(1)}, f32[1,512]{1,0:T(1,128)S(1)}, u32[]{:S(2)}, u32[]{:S(2)}) collective-permute-start(f32[1,512]{1,0:T(1,128)S(1)} %get-tuple-element.28), channel_id=1, source_target_pairs={{0,1},{1,0},{2,3},{3,2},{4,5},{5,4},{6,7},{7,6},{8,9},{9,8},{10,11... | collective-permute-start | bytes 6152 | tf_op jit(solution)/shard_map/ppermute | solution.py:247
  10.0 5.3 %collective-permute-start.3 = (f32[64,512]{1,0:T(8,128)S(1)}, f32[64,512]{1,0:T(8,128)S(1)}, u32[]{:S(2)}, u32[]{:S(2)}) collective-permute-start(f32[64,512]{1,0:T(8,128)S(1)} %get-tuple-element.30.x_ref.own_ref), channel_id=1, source_target_pairs={{0,4},{4,0},{1,5},{5,1},{2,6},{6,2},{3,7},{7,3},{8,12},{12,8},{9,1... | collective-permute-start | bytes 393224 | tf_op jit(solution)/shard_map/ppermute | solution.py:247
  13.8 1.4 %collective-permute-start.4 = (f32[1,512]{1,0:T(1,128)S(1)}, f32[1,512]{1,0:T(1,128)S(1)}, u32[]{:S(2)}, u32[]{:S(2)}) collective-permute-start(f32[1,512]{1,0:T(1,128)S(1)} %add_subtract_fusion.phi_ref), channel_id=1, source_target_pairs={{0,4},{4,0},{1,5},{5,1},{2,6},{6,2},{3,7},{7,3},{8,12},{12,8},{9,1... | collective-permute-start | bytes 6152 | tf_op jit(solution)/shard_map/ppermute | solution.py:247
  17.1 1.4 %collective-permute-start.5 = (f32[1,1024]{1,0:T(1,128)S(1)}, f32[1,1024]{1,0:T(1,128)S(1)}, u32[]{:S(2)}, u32[]{:S(2)}) collective-permute-start(f32[1,1024]{1,0:T(1,128)S(1)} %get-tuple-element.37.own_ref), channel_id=1, source_target_pairs={{0,4},{4,0},{1,5},{5,1},{2,6},{6,2},{3,7},{7,3},{8,12},{12,8},{9,1... | collective-permute-start | bytes 12296 | tf_op jit(solution)/shard_map/ppermute | solution.py:247
  18.5 5.9 %collective-permute-start.8 = (f32[1,1024]{1,0:T(1,128)S(1)}, f32[1,1024]{1,0:T(1,128)S(1)}, u32[]{:S(2)}, u32[]{:S(2)}) collective-permute-start(f32[1,1024]{1,0:T(1,128)S(1)} %meet.1.refs_0_.after_ref), channel_id=1, source_target_pairs={{0,3},{1,2},{2,1},{3,0},{4,7},{5,6},{6,5},{7,4},{8,11},{9,10},{10,... | collective-permute-start | bytes 12296 | tf_op jit(solution)/shard_map/ppermute | solution.py:247
  20.0 4.5 %collective-permute-start.7 = (f32[1,1024]{1,0:T(1,128)S(1)}, f32[1,1024]{1,0:T(1,128)S(1)}, u32[]{:S(2)}, u32[]{:S(2)}) collective-permute-start(f32[1,1024]{1,0:T(1,128)S(1)} %meet.1.refs_0_.after_ref), channel_id=1, source_target_pairs={{0,2},{1,3},{2,0},{3,1},{4,6},{5,7},{6,4},{7,5},{8,10},{9,11},{10,... | collective-permute-start | bytes 12296 | tf_op jit(solution)/shard_map/ppermute | solution.py:247
  20.6 4.0 %collective-permute-start.6 = (f32[1,1024]{1,0:T(1,128)S(1)}, f32[1,1024]{1,0:T(1,128)S(1)}, u32[]{:S(2)}, u32[]{:S(2)}) collective-permute-start(f32[1,1024]{1,0:T(1,128)S(1)} %meet.1.refs_0_.after_ref), channel_id=1, source_target_pairs={{0,1},{1,0},{2,3},{3,2},{4,5},{5,4},{6,7},{7,6},{8,9},{9,8},{10,11... | collective-permute-start | bytes 12296 | tf_op jit(solution)/shard_map/ppermute | solution.py:247
  26.8 6.5 %collective-permute-start.9 = (f32[64,512]{1,0:T(8,128)S(1)}, f32[64,512]{1,0:T(8,128)S(1)}, u32[]{:S(2)}, u32[]{:S(2)}) collective-permute-start(f32[64,512]{1,0:T(8,128)S(1)} %get-tuple-element.44), channel_id=1, source_target_pairs={{0,24},{8,16},{16,8},{24,0},{1,25},{9,17},{17,9},{25,1},{2,26},{10... | collective-permute-start | bytes 393224 | tf_op jit(solution)/shard_map/ppermute | solution.py:247
  29.2 6.1 %collective-permute-start.10 = (f32[64,512]{1,0:T(8,128)S(1)}, f32[64,512]{1,0:T(8,128)S(1)}, u32[]{:S(2)}, u32[]{:S(2)}) collective-permute-start(f32[64,512]{1,0:T(8,128)S(1)} %get-tuple-element.45), channel_id=1, source_target_pairs={{0,16},{8,24},{16,0},{24,8},{1,17},{9,25},{17,1},{25,9},{2,18},{10... | collective-permute-start | bytes 393224 | tf_op jit(solution)/shard_map/ppermute | solution.py:247
  29.8 5.7 %collective-permute-start.11 = (f32[64,512]{1,0:T(8,128)S(1)}, f32[64,512]{1,0:T(8,128)S(1)}, u32[]{:S(2)}, u32[]{:S(2)}) collective-permute-start(f32[64,512]{1,0:T(8,128)S(1)} %get-tuple-element.46), channel_id=1, source_target_pairs={{0,8},{8,0},{16,24},{24,16},{1,9},{9,1},{17,25},{25,17},{2,10},{10... | collective-permute-start | bytes 393224 | tf_op jit(solution)/shard_map/ppermute | solution.py:247
  35.5 7.3 %collective-permute-start.14 = (f32[64,512]{1,0:T(8,128)S(1)}, f32[64,512]{1,0:T(8,128)S(1)}, u32[]{:S(2)}, u32[]{:S(2)}) collective-permute-start(f32[64,512]{1,0:T(8,128)S(1)} %add_multiply_fusion.refs_0_), channel_id=1, source_target_pairs={{0,24},{8,16},{16,8},{24,0},{1,25},{9,17},{17,9},{25,1},{2,26},{10... | collective-permute-start | bytes 393224 | tf_op jit(solution)/shard_map/ppermute | solution.py:247
  37.2 7.0 %collective-permute-start.13 = (f32[64,512]{1,0:T(8,128)S(1)}, f32[64,512]{1,0:T(8,128)S(1)}, u32[]{:S(2)}, u32[]{:S(2)}) collective-permute-start(f32[64,512]{1,0:T(8,128)S(1)} %add_multiply_fusion.refs_0_), channel_id=1, source_target_pairs={{0,16},{8,24},{16,0},{24,8},{1,17},{9,25},{17,1},{25,9},{2,18},{10... | collective-permute-start | bytes 393224 | tf_op jit(solution)/shard_map/ppermute | solution.py:247
  38.5 5.8 %collective-permute-start.12 = (f32[64,512]{1,0:T(8,128)S(1)}, f32[64,512]{1,0:T(8,128)S(1)}, u32[]{:S(2)}, u32[]{:S(2)}) collective-permute-start(f32[64,512]{1,0:T(8,128)S(1)} %add_multiply_fusion.refs_0_), channel_id=1, source_target_pairs={{0,8},{8,0},{16,24},{24,16},{1,9},{9,1},{17,25},{25,17},{2,10},{10... | collective-permute-start | bytes 393224 | tf_op jit(solution)/shard_map/ppermute | solution.py:247
  39.0 6.2 %collective-permute-start.19 = (f32[1,2048]{1,0:T(1,128)S(1)}, f32[1,2048]{1,0:T(1,128)S(1)}, u32[]{:S(2)}, u32[]{:S(2)}) collective-permute-start(f32[1,2048]{1,0:T(1,128)S(1)} %constant_dynamic-update-slice_fusion.refs_8_), channel_id=1, source_target_pairs={{0,4},{4,0},{1,5},{5,1},{2,6},{6,2},{3,7},{7,3},{8,12},{12,8},{9,1... | collective-permute-start | bytes 24584 | tf_op jit(solution)/shard_map/ppermute | solution.py:247
  39.0 6.2 %collective-permute-start.15 = (f32[64,512]{1,0:T(8,128)S(1)}, f32[64,512]{1,0:T(8,128)S(1)}, u32[]{:S(2)}, u32[]{:S(2)}) collective-permute-start(f32[64,512]{1,0:T(8,128)S(1)} %add_multiply_fusion.refs_0_), channel_id=1, source_target_pairs={{0,4},{4,0},{1,5},{5,1},{2,6},{6,2},{3,7},{7,3},{8,12},{12,8},{9,1... | collective-permute-start | bytes 393224 | tf_op jit(solution)/shard_map/ppermute | solution.py:247
  42.7 2.5 %collective-permute-start.18 = (f32[64,512]{1,0:T(8,128)S(1)}, f32[64,512]{1,0:T(8,128)S(1)}, u32[]{:S(2)}, u32[]{:S(2)}) collective-permute-start(f32[64,512]{1,0:T(8,128)S(1)} %collective-permute-done.14.refs_3_), channel_id=1, source_target_pairs={{0,4},{4,0},{1,5},{5,1},{2,6},{6,2},{3,7},{7,3},{8,12},{12,8},{9,1... | collective-permute-start | bytes 393224 | tf_op jit(solution)/shard_map/ppermute | solution.py:247
  44.1 1.3 %collective-permute-start.17 = (f32[64,512]{1,0:T(8,128)S(1)}, f32[64,512]{1,0:T(8,128)S(1)}, u32[]{:S(2)}, u32[]{:S(2)}) collective-permute-start(f32[64,512]{1,0:T(8,128)S(1)} %collective-permute-done.13.refs_2_), channel_id=1, source_target_pairs={{0,4},{4,0},{1,5},{5,1},{2,6},{6,2},{3,7},{7,3},{8,12},{12,8},{9,1... | collective-permute-start | bytes 393224 | tf_op jit(solution)/shard_map/ppermute | solution.py:247
  44.3 1.4 %collective-permute-start.16 = (f32[64,512]{1,0:T(8,128)S(1)}, f32[64,512]{1,0:T(8,128)S(1)}, u32[]{:S(2)}, u32[]{:S(2)}) collective-permute-start(f32[64,512]{1,0:T(8,128)S(1)} %collective-permute-done.12.refs_1_), channel_id=1, source_target_pairs={{0,4},{4,0},{1,5},{5,1},{2,6},{6,2},{3,7},{7,3},{8,12},{12,8},{9,1... | collective-permute-start | bytes 393224 | tf_op jit(solution)/shard_map/ppermute | solution.py:247

commit v7 on v6

--- a/solution.py
+++ b/solution.py
@@ -123,7 +123,7 @@
     scale, points, x_ref, phi_ref, y_ref, b_ref, peak_ref, sum_ref, base_ref, right, left
 ):
     columns = b_ref.shape[1]
-    block = min(256, columns)
+    block = min(512, columns)
     logit_block(scale, x_ref, phi_ref, left)
     y = y_ref[...]
     right[...] = jnp.concatenate([y, y, y, ones_rows(columns)], axis=0)
@@ -143,7 +143,7 @@
     e_ref, factor_ref, r_ref, base_ref, left, part_r,
 ):
     half, columns = e_ref.shape
-    block = min(256, columns)
+    block = min(512, columns)
     height = min(64, half)
     logit_block(scale, x_ref, phi_ref, left)
     for start in range(0, columns, block):
@@ -217,30 +217,45 @@
     g_ref[...] = (blur / LOG2E) * (base_ref[:, span] - jnp.log2(mass))
 
 
-def assemble_kernel(atlases, *refs):
-    own, other, g_own, g_other = refs[:atlases], refs[atlases : 2 * atlases], *refs[2 * atlases : 2 * atlases + 2]
-    out_ref, g_hbm, image, g_ref, sems = refs[2 * atlases + 2 :]
-    dims, width = own[0].shape
-    atlas = lax.axis_index("atlas")
-    row = lax.axis_index("row")
-    places = []
-    for half, slabs, duals in ((row, own, g_own), (1 - row, other, g_other)):
-        for key in range(atlases):
-            start = pl.multiple_of((half * atlases + (atlas ^ key)) * width, LANES)
-            places.append((slabs[key], start))
-            g_ref[:, pl.ds(start, width)] = duals[:, key * width : (key + 1) * width]
-    copies = [pltpu.make_async_copy(g_ref, g_hbm, sems.at[0])]
-    copies[0].start()
-    for low in range(0, dims, SUBLANES):
-        rows = slice(low, low + SUBLANES)
-        for slab, start in places:
-            image[rows, pl.ds(start, width)] = slab[rows, :]
-        copies.append(
-            pltpu.make_async_copy(image.at[rows, :], out_ref.at[rows, :], sems.at[len(copies)])
-        )
-        copies[-1].start()
+def slab_span(half, key, atlases, width):
+    slab = half * atlases + (lax.axis_index("atlas") ^ key)
+    return pl.ds(pl.multiple_of(slab * width, LANES), width)
+
+
+def copy_all(copies):
+    for copy in copies:
+        copy.start()
     for copy in copies:
         copy.wait()
+
+
+def early_kernel(order, *refs):
+    atlases = len(order)
+    slabs = refs[: atlases + 1]
+    g_own, g_other, out_hbm, g_hbm, g_ref, sems = refs[atlases + 1 :]
+    width = slabs[0].shape[1]
+    row = lax.axis_index("row")
+    places = [(row, key) for key in range(atlases)] + [(1 - row, 0)]
+    for half, duals in ((row, g_own), (1 - row, g_other)):
+        for at, key in enumerate(order):
+            span = slab_span(half, key, atlases, width)
+            g_ref[:, span] = duals[:, at * width : (at + 1) * width]
+    copies = [pltpu.make_async_copy(g_ref, g_hbm, sems.at[0])]
+    for slab, (half, key) in zip(slabs, places):
+        target = out_hbm.at[:, slab_span(half, key, atlases, width)]
+        copies.append(pltpu.make_async_copy(slab, target, sems.at[len(copies)]))
+    copy_all(copies)
+
+
+def late_kernel(atlases, *refs):
+    *slabs, in_hbm, out_hbm, sems = refs
+    del in_hbm
+    width = slabs[0].shape[1]
+    copies = []
+    for key, slab in enumerate(slabs, 1):
+        target = out_hbm.at[:, slab_span(1 - lax.axis_index("row"), key, atlases, width)]
+        copies.append(pltpu.make_async_copy(slab, target, sems.at[key - 1]))
+    copy_all(copies)
 
 
 def exchange(value, axis, size, key):
@@ -415,26 +430,36 @@
             if key:
                 arrived.append(exchange(terms[key], "atlas", atlases, key))
         sums = functools.reduce(jnp.add, arrived, terms[0]) * (1.0 / atlases)
-        slabs = [sums, *partners(sums, "atlas")]
-        duals = jnp.concatenate(duals, axis=1)
+        slabs = [sums]
+        for key in range(1, atlases):
+            slabs.append(exchange(sums, "atlas", atlases, key))
+        duals = jnp.concatenate([duals[key] for key in order], axis=1)
+        other = []
+        for slab in slabs:
+            other.append(exchange(slab, "row", 2, 1))
+        duals_other = exchange(duals, "row", 2, 1)
         updated, dual_g = pl.pallas_call(
-            functools.partial(assemble_kernel, atlases),
+            functools.partial(early_kernel, order),
             out_shape=(jax.ShapeDtypeStruct((dims, columns), jnp.float32), row_vector(columns)),
-            in_specs=[VMEM] * (2 * atlases + 2),
+            in_specs=[VMEM] * (atlases + 3),
             out_specs=(HBM, HBM),
             scratch_shapes=[
-                pltpu.VMEM((dims, columns), jnp.float32),
                 pltpu.VMEM((1, columns), jnp.float32),
-                pltpu.SemaphoreType.DMA((1 + dims // SUBLANES,)),
+                pltpu.SemaphoreType.DMA((atlases + 2,)),
             ],
             compiler_params=pltpu.CompilerParams(vmem_limit_bytes=8 << 20),
-            name="assemble",
-        )(
-            *slabs,
-            *[exchange(slab, "row", 2, 1) for slab in slabs],
-            duals,
-            exchange(duals, "row", 2, 1),
-        )
+            name="early",
+        )(*slabs, other[0], duals, duals_other)
+        updated = pl.pallas_call(
+            functools.partial(late_kernel, atlases),
+            out_shape=jax.ShapeDtypeStruct((dims, columns), jnp.float32),
+            in_specs=[VMEM] * (atlases - 1) + [HBM],
+            out_specs=HBM,
+            scratch_shapes=[pltpu.SemaphoreType.DMA((atlases - 1,))],
+            input_output_aliases={atlases - 1: 0},
+            compiler_params=pltpu.CompilerParams(vmem_limit_bytes=8 << 20),
+            name="late",
+        )(*other[1:], updated)
     else:
         moved, dual_g = third(None, share)
         updated = all_rows(lax.psum(moved, "atlas") * (1.0 / atlases))

time: 46.9 us -> 46.6 us (level)
  waiting for transfers between devices: 15 us -> 14.1 us
  Pallas kernels: 11.5 us -> 12 us
    ppermute x20, waiting for transfers between devices: 15 us -> 14.1 us  [exchange(): return lax.ppermute(value, axis, [(at, at ^ key) for at in range(size)])]
    pallas_call x1 -> x2, Pallas kernels: 1.06 us -> 1.69 us  [the longest x1 0.9 us: shards(): pl.pallas_call(functools.partial(early_kernel, order), out_shape=(jax.Sha...]
  transfers between devices with their start and end apart: 20 -> 20, of which waited for: 12 -> 10; matrix products, arithmetic and copies ran while one was open for 1% -> 1% of each run, Pallas kernels for 6% -> 9%
where the time goes in v7:
time: 46.6 us; the launch traced here: 46.4 us
  starting transfers between devices  18.8 us (40%)
  waiting for transfers between devices  14.1 us (30%)
  Pallas kernels  12 us (26%)
  between operations  0.78 us (2%)
  other arithmetic  0.67 us (1%)
    ppermute x20, starting transfers between devices, exchange(): return lax.ppermute(value, axis, [(at, at ^ key) for at in range(size)])  18.8 us
    ppermute x20, waiting for transfers between devices, exchange(): return lax.ppermute(value, axis, [(at, at ^ key) for at in range(size)])  14.1 us
    pallas_call x1, Pallas kernels, shards(): pl.pallas_call(functools.partial(first_kernel, scale), out_shape=(row_vec...  3.53 us
    pallas_call x4, Pallas kernels, third(): pl.pallas_call(functools.partial(third_kernel, key, dims), out_shape=(jax...  2.08 us
    pallas_call x1, Pallas kernels, shards(): pl.pallas_call(functools.partial(second_kernel, scale, float(total_suppor...  1.86 us
    pallas_call x1, Pallas kernels, shards(): pl.pallas_call(split_kernel, out_shape=(jax.ShapeDtypeStruct((total_cells...  1.48 us
    pallas_call x1, Pallas kernels, shards(): pl.pallas_call(functools.partial(half_kernel, scale, float(total_support)...  1.31 us
  transfers between devices with their start and end apart: 20, of which 10 were waited for; matrix products, arithmetic and copies ran while one was open for 1% of the time, Pallas kernels for 9%

profile of v7, /device:TPU:0, one launch (start us, length us, event | category | flops | bytes accessed | tf_op | source)
XLA Modules:
  0.0 46.4 jit_solution(11220024673283845768)
XLA Ops:
  0.6 3.5 %first.1 = (f32[1,512]{1,0:T(1,128)S(1)}, f32[1,512]{1,0:T(1,128)S(1)}, bf16[64,2048]{1,0:T(8,128)(2,1)S(1)}, f32[64,512]{1,0:T(8,128)S(1)}) custom-call(bf16[64,512]{1,0:T(8,128)(2,1)} %bitcast.1, bf16[64,4096]{1,0:T(8,128)(2,1)} %y_hbm.1), custom_call_target="tpu_custom_call" | custom-call | tf_op jit(solution)/shard_map/first/pallas_call | solution.py:320
  4.2 5.1 %collective-permute-start.2 = (f32[1,512]{1,0:T(1,128)S(1)}, f32[1,512]{1,0:T(1,128)S(1)}, u32[]{:S(2)}, u32[]{:S(2)}) collective-permute-start(f32[1,512]{1,0:T(1,128)S(1)} %get-tuple-element.28), channel_id=1, source_target_pairs={{0,3},{1,2},{2,1},{3,0},{4,7},{5,6},{6,5},{7,4},{8,11},{9,10},{10,... | collective-permute-start | bytes 6152 | tf_op jit(solution)/shard_map/ppermute | solution.py:262
  9.3 0.6 %collective-permute-start = (f32[1,512]{1,0:T(1,128)S(1)}, f32[1,512]{1,0:T(1,128)S(1)}, u32[]{:S(2)}, u32[]{:S(2)}) collective-permute-start(f32[1,512]{1,0:T(1,128)S(1)} %get-tuple-element.28), channel_id=1, source_target_pairs={{0,1},{1,0},{2,3},{3,2},{4,5},{5,4},{6,7},{7,6},{8,9},{9,8},{10,11... | collective-permute-start | bytes 6152 | tf_op jit(solution)/shard_map/ppermute | solution.py:262
  10.0 0.9 %collective-permute-done.2 = f32[1,512]{1,0:T(1,128)S(1)} collective-permute-done((f32[1,512]{1,0:T(1,128)S(1)}, f32[1,512]{1,0:T(1,128)S(1)}, u32[]{:S(2)}, u32[]{:S(2)}) %collective-permute-start.2) | collective-permute-done | bytes 2080 | tf_op jit(solution)/shard_map/ppermute | solution.py:262
  10.9 2.9 %collective-permute-done.1 = f32[1,512]{1,0:T(1,128)S(1)} collective-permute-done((f32[1,512]{1,0:T(1,128)S(1)}, f32[1,512]{1,0:T(1,128)S(1)}, u32[]{:S(2)}, u32[]{:S(2)}) %collective-permute-start.1) | collective-permute-done | bytes 2080 | tf_op jit(solution)/shard_map/ppermute | solution.py:262
  13.9 1.3 %half.1 = (f32[512,2048]{1,0:T(8,128)S(1)}, f32[1,2048]{1,0:T(1,128)S(1)}, f32[1,2048]{1,0:T(1,128)S(1)}, f32[1,2048]{1,0:T(1,128)S(1)}, bf16[208,2048]{1,0:T(8,128)(2,1)S(1)}) custom-call(f32[64,512]{1,0:T(8,128)S(1)} %get-tuple-element.30.x_ref.own_ref, f32[1,512]{1,0:T(1,128)S(1)} %add_subtract_fusion.phi_ref, bf16[64,2048]{1,0:T(8,128)(2,1)S(1)} %get-tuple-element.31.y_ref), custom_call_target="tpu_custom_call" | custom-call | tf_op jit(solution)/shard_map/half/pallas_call | solution.py:354
  15.2 1.9 %second.1 = (f32[512,2048]{1,0:T(8,128)S(1)}, f32[1,2048]{1,0:T(1,128)S(1)}, f32[1,1024]{1,0:T(1,128)S(1)}, f32[1,2048]{1,0:T(1,128)S(1)}) custom-call(f32[512,2048]{1,0:T(8,128)S(1)} %get-tuple-element.32.b_ref, f32[1,2048]{1,0:T(1,128)S(1)} %get-tuple-element.33.top_ref, f32[1,2048]{1,0:T(1,128)S(1)} %get-tuple-element.34.sum_ref, ...), custom_call_target="tpu_custom_call" | custom-call | tf_op jit(solution)/shard_map/second/pallas_call | solution.py:369
  17.1 0.6 %collective-permute-start.5 = (f32[1,1024]{1,0:T(1,128)S(1)}, f32[1,1024]{1,0:T(1,128)S(1)}, u32[]{:S(2)}, u32[]{:S(2)}) collective-permute-start(f32[1,1024]{1,0:T(1,128)S(1)} %get-tuple-element.37.own_ref), channel_id=1, source_target_pairs={{0,4},{4,0},{1,5},{5,1},{2,6},{6,2},{3,7},{7,3},{8,12},{12,8},{9,1... | collective-permute-start | bytes 12296 | tf_op jit(solution)/shard_map/ppermute | solution.py:262
  17.7 0.8 %collective-permute-done.5.other_ref = f32[1,1024]{1,0:T(1,128)S(1)} collective-permute-done((f32[1,1024]{1,0:T(1,128)S(1)}, f32[1,1024]{1,0:T(1,128)S(1)}, u32[]{:S(2)}, u32[]{:S(2)}) %collective-permute-start.5) | collective-permute-done | bytes 4128 | tf_op jit(solution)/shard_map/ppermute | solution.py:262
  18.5 1.5 %collective-permute-start.8 = (f32[1,1024]{1,0:T(1,128)S(1)}, f32[1,1024]{1,0:T(1,128)S(1)}, u32[]{:S(2)}, u32[]{:S(2)}) collective-permute-start(f32[1,1024]{1,0:T(1,128)S(1)} %meet.1.refs_0_.after_ref), channel_id=1, source_target_pairs={{0,3},{1,2},{2,1},{3,0},{4,7},{5,6},{6,5},{7,4},{8,11},{9,10},{10,... | collective-permute-start | bytes 12296 | tf_op jit(solution)/shard_map/ppermute | solution.py:262
  20.0 0.6 %collective-permute-start.7 = (f32[1,1024]{1,0:T(1,128)S(1)}, f32[1,1024]{1,0:T(1,128)S(1)}, u32[]{:S(2)}, u32[]{:S(2)}) collective-permute-start(f32[1,1024]{1,0:T(1,128)S(1)} %meet.1.refs_0_.after_ref), channel_id=1, source_target_pairs={{0,2},{1,3},{2,0},{3,1},{4,6},{5,7},{6,4},{7,5},{8,10},{9,11},{10,... | collective-permute-start | bytes 12296 | tf_op jit(solution)/shard_map/ppermute | solution.py:262
  20.5 2.4 %collective-permute-start.6 = (f32[1,1024]{1,0:T(1,128)S(1)}, f32[1,1024]{1,0:T(1,128)S(1)}, u32[]{:S(2)}, u32[]{:S(2)}) collective-permute-start(f32[1,1024]{1,0:T(1,128)S(1)} %meet.1.refs_0_.after_ref), channel_id=1, source_target_pairs={{0,1},{1,0},{2,3},{3,2},{4,5},{5,4},{6,7},{7,6},{8,9},{9,8},{10,11... | collective-permute-start | bytes 12296 | tf_op jit(solution)/shard_map/ppermute | solution.py:262
  22.9 1.5 %split.1 = (bf16[1024,2048]{1,0:T(8,128)(2,1)S(1)}, bf16[1024,2048]{1,0:T(8,128)(2,1)S(1)}) custom-call(f32[512,2048]{1,0:T(8,128)S(1)} %get-tuple-element.32.b_ref, f32[512,2048]{1,0:T(8,128)S(1)} %get-tuple-element.38.e_ref, f32[1,2048]{1,0:T(1,128)S(1)} %get-tuple-element.39.factor_ref, f32[1,1024]{1,0:T(1,128)S(1)} %meet.1.refs_0_.after_ref), custom_call_target="tpu_custom_call" | custom-call | flops 8388608 | bytes 16777216 | tf_op jit(solution)/shard_map/split/pallas_call | solution.py:390
  24.6 0.5 %third.7 = (f32[64,512]{1,0:T(8,128)S(1)}, f32[1,512]{1,0:T(1,128)S(1)}) custom-call(bf16[144,1024]{1,0:T(8,128)(2,1)S(1)} %weights.1.weights_ref, bf16[1024,2048]{1,0:T(8,128)(2,1)S(1)} %get-tuple-element.40.high_ref, bf16[1024,2048]{1,0:T(8,128)(2,1)S(1)} %get-tuple-element.41.low_ref, f32[1,2048]{1,0:T(1,128)S(1)} %get-tuple-element.42.base_ref), custom_call_target="tpu_custom_call" | custom-call | flops 234881024 | bytes 2097152 | tf_op jit(solution)/shard_map/third/pallas_call | solution.py:409
  25.1 0.5 %third.6 = (f32[64,512]{1,0:T(8,128)S(1)}, f32[1,512]{1,0:T(1,128)S(1)}) custom-call(bf16[144,1024]{1,0:T(8,128)(2,1)S(1)} %weights.1.weights_ref, bf16[1024,2048]{1,0:T(8,128)(2,1)S(1)} %get-tuple-element.40.high_ref, bf16[1024,2048]{1,0:T(8,128)(2,1)S(1)} %get-tuple-element.41.low_ref, f32[1,2048]{1,0:T(1,128)S(1)} %get-tuple-element.42.base_ref), custom_call_target="tpu_custom_call" | custom-call | flops 234881024 | bytes 2097152 | tf_op jit(solution)/shard_map/third/pallas_call | solution.py:409
  25.7 0.5 %third.5 = (f32[64,512]{1,0:T(8,128)S(1)}, f32[1,512]{1,0:T(1,128)S(1)}) custom-call(bf16[144,1024]{1,0:T(8,128)(2,1)S(1)} %weights.1.weights_ref, bf16[1024,2048]{1,0:T(8,128)(2,1)S(1)} %get-tuple-element.40.high_ref, bf16[1024,2048]{1,0:T(8,128)(2,1)S(1)} %get-tuple-element.41.low_ref, f32[1,2048]{1,0:T(1,128)S(1)} %get-tuple-element.42.base_ref), custom_call_target="tpu_custom_call" | custom-call | flops 234881024 | bytes 2097152 | tf_op jit(solution)/shard_map/third/pallas_call | solution.py:409
  26.2 2.5 %collective-permute-start.9 = (f32[64,512]{1,0:T(8,128)S(1)}, f32[64,512]{1,0:T(8,128)S(1)}, u32[]{:S(2)}, u32[]{:S(2)}) collective-permute-start(f32[64,512]{1,0:T(8,128)S(1)} %get-tuple-element.44), channel_id=1, source_target_pairs={{0,24},{8,16},{16,8},{24,0},{1,25},{9,17},{17,9},{25,1},{2,26},{10... | collective-permute-start | bytes 393224 | tf_op jit(solution)/shard_map/ppermute | solution.py:262
  28.7 0.5 %collective-permute-start.10 = (f32[64,512]{1,0:T(8,128)S(1)}, f32[64,512]{1,0:T(8,128)S(1)}, u32[]{:S(2)}, u32[]{:S(2)}) collective-permute-start(f32[64,512]{1,0:T(8,128)S(1)} %get-tuple-element.45), channel_id=1, source_target_pairs={{0,16},{8,24},{16,0},{24,8},{1,17},{9,25},{17,1},{25,9},{2,18},{10... | collective-permute-start | bytes 393224 | tf_op jit(solution)/shard_map/ppermute | solution.py:262
  29.2 0.6 %collective-permute-start.11 = (f32[64,512]{1,0:T(8,128)S(1)}, f32[64,512]{1,0:T(8,128)S(1)}, u32[]{:S(2)}, u32[]{:S(2)}) collective-permute-start(f32[64,512]{1,0:T(8,128)S(1)} %get-tuple-element.46), channel_id=1, source_target_pairs={{0,8},{8,0},{16,24},{24,16},{1,9},{9,1},{17,25},{25,17},{2,10},{10... | collective-permute-start | bytes 393224 | tf_op jit(solution)/shard_map/ppermute | solution.py:262
  29.8 0.5 %third.4 = (f32[64,512]{1,0:T(8,128)S(1)}, f32[1,512]{1,0:T(1,128)S(1)}) custom-call(bf16[144,1024]{1,0:T(8,128)(2,1)S(1)} %weights.1.weights_ref, bf16[1024,2048]{1,0:T(8,128)(2,1)S(1)} %get-tuple-element.40.high_ref, bf16[1024,2048]{1,0:T(8,128)(2,1)S(1)} %get-tuple-element.41.low_ref, f32[1,2048]{1,0:T(1,128)S(1)} %get-tuple-element.42.base_ref), custom_call_target="tpu_custom_call" | custom-call | flops 234881024 | bytes 2097152 | tf_op jit(solution)/shard_map/third/pallas_call | solution.py:409
  30.3 2.4 %collective-permute-done.9 = f32[64,512]{1,0:T(8,128)S(1)} collective-permute-done((f32[64,512]{1,0:T(8,128)S(1)}, f32[64,512]{1,0:T(8,128)S(1)}, u32[]{:S(2)}, u32[]{:S(2)}) %collective-permute-start.9) | collective-permute-done | bytes 131104 | tf_op jit(solution)/shard_map/ppermute | solution.py:262
  32.7 2.1 %collective-permute-done.10 = f32[64,512]{1,0:T(8,128)S(1)} collective-permute-done((f32[64,512]{1,0:T(8,128)S(1)}, f32[64,512]{1,0:T(8,128)S(1)}, u32[]{:S(2)}, u32[]{:S(2)}) %collective-permute-start.10) | collective-permute-done | bytes 131104 | tf_op jit(solution)/shard_map/ppermute | solution.py:262
  34.9 1.7 %collective-permute-start.14 = (f32[64,512]{1,0:T(8,128)S(1)}, f32[64,512]{1,0:T(8,128)S(1)}, u32[]{:S(2)}, u32[]{:S(2)}) collective-permute-start(f32[64,512]{1,0:T(8,128)S(1)} %add_multiply_fusion.refs_0_), channel_id=1, source_target_pairs={{0,24},{8,16},{16,8},{24,0},{1,25},{9,17},{17,9},{25,1},{2,26},{10... | collective-permute-start | bytes 393224 | tf_op jit(solution)/shard_map/ppermute | solution.py:262
  36.6 1.3 %collective-permute-start.13 = (f32[64,512]{1,0:T(8,128)S(1)}, f32[64,512]{1,0:T(8,128)S(1)}, u32[]{:S(2)}, u32[]{:S(2)}) collective-permute-start(f32[64,512]{1,0:T(8,128)S(1)} %add_multiply_fusion.refs_0_), channel_id=1, source_target_pairs={{0,16},{8,24},{16,0},{24,8},{1,17},{9,25},{17,1},{25,9},{2,18},{10... | collective-permute-start | bytes 393224 | tf_op jit(solution)/shard_map/ppermute | solution.py:262
  37.9 0.5 %collective-permute-start.12 = (f32[64,512]{1,0:T(8,128)S(1)}, f32[64,512]{1,0:T(8,128)S(1)}, u32[]{:S(2)}, u32[]{:S(2)}) collective-permute-start(f32[64,512]{1,0:T(8,128)S(1)} %add_multiply_fusion.refs_0_), channel_id=1, source_target_pairs={{0,8},{8,0},{16,24},{24,16},{1,9},{9,1},{17,25},{25,17},{2,10},{10... | collective-permute-start | bytes 393224 | tf_op jit(solution)/shard_map/ppermute | solution.py:262
  38.5 0.5 %collective-permute-start.15 = (f32[64,512]{1,0:T(8,128)S(1)}, f32[64,512]{1,0:T(8,128)S(1)}, u32[]{:S(2)}, u32[]{:S(2)}) collective-permute-start(f32[64,512]{1,0:T(8,128)S(1)} %add_multiply_fusion.refs_0_), channel_id=1, source_target_pairs={{0,4},{4,0},{1,5},{5,1},{2,6},{6,2},{3,7},{7,3},{8,12},{12,8},{9,1... | collective-permute-start | bytes 393224 | tf_op jit(solution)/shard_map/ppermute | solution.py:262
  39.0 3.2 %collective-permute-done.14.refs_3_ = f32[64,512]{1,0:T(8,128)S(1)} collective-permute-done((f32[64,512]{1,0:T(8,128)S(1)}, f32[64,512]{1,0:T(8,128)S(1)}, u32[]{:S(2)}, u32[]{:S(2)}) %collective-permute-start.14) | collective-permute-done | bytes 131104 | tf_op jit(solution)/shard_map/ppermute | solution.py:262
  42.2 1.4 %collective-permute-done.13.refs_2_ = f32[64,512]{1,0:T(8,128)S(1)} collective-permute-done((f32[64,512]{1,0:T(8,128)S(1)}, f32[64,512]{1,0:T(8,128)S(1)}, u32[]{:S(2)}, u32[]{:S(2)}) %collective-permute-start.13) | collective-permute-done | bytes 131104 | tf_op jit(solution)/shard_map/ppermute | solution.py:262
  43.7 0.4 collective-permute-start.17
  44.1 0.6 %subtract_multiply_fusion = f32[1,512]{1,0:T(1,128)} fusion(f32[1,512]{1,0:T(1,128)S(1)} %add_subtract_fusion.phi_ref, f32[1,512]{1,0:T(1,128)S(1)} %get-tuple-element.29, f32[1,1024]{1,0:T(1,128)S(1)} %collective-permute-done.8.refs_3_, f32[1,1024]{1,0:T(1,128)S(1)} %collective-permute-done.7.refs_2_, f32[1,1024]{1,0:T(1,128)S(1)} %collective-permute-done.6.refs_1_, ...), kind=kLoop, calls=%fused_computation.9 | loop fusion | flops 4096 | bytes 14336 | tf_op jit(solution)/shard_map/mul | solution.py:468
  44.7 0.9 %early.1 = (f32[64,4096]{1,0:T(8,128)}, f32[1,4096]{1,0:T(1,128)}) custom-call(f32[64,512]{1,0:T(8,128)S(1)} %add_multiply_fusion.refs_0_, f32[64,512]{1,0:T(8,128)S(1)} %collective-permute-done.12.refs_1_, f32[64,512]{1,0:T(8,128)S(1)} %collective-permute-done.13.refs_2_, f32[64,512]{1,0:T(8,128)S(1)} %collective-permute-done.14.refs_3_, ...), custom_call_target="tpu_custom_call" | custom-call | tf_op jit(solution)/shard_map/early/pallas_call | solution.py:441
  45.7 0.8 %late.1 = f32[64,4096]{1,0:T(8,128)} custom-call(f32[64,512]{1,0:T(8,128)S(1)} %collective-permute-done.17.refs_0_, f32[64,512]{1,0:T(8,128)S(1)} %collective-permute-done.18.refs_1_, f32[64,512]{1,0:T(8,128)S(1)} %collective-permute-done.19.refs_2_, f32[64,4096]{1,0:T(8,128)} %get-tuple-element.52.refs_3_), custom_call_target="tpu_custom_call", output_to_operand_aliasing={{}: (3, {})} | custom-call | tf_op jit(solution)/shard_map/late/pallas_call | solution.py:453
  (27 shorter events, 0.6 us)
Async XLA Ops:
  4.2 6.7 %collective-permute-start.2 = (f32[1,512]{1,0:T(1,128)S(1)}, f32[1,512]{1,0:T(1,128)S(1)}, u32[]{:S(2)}, u32[]{:S(2)}) collective-permute-start(f32[1,512]{1,0:T(1,128)S(1)} %get-tuple-element.28), channel_id=1, source_target_pairs={{0,3},{1,2},{2,1},{3,0},{4,7},{5,6},{6,5},{7,4},{8,11},{9,10},{10,... | collective-permute-start | bytes 6152 | tf_op jit(solution)/shard_map/ppermute | solution.py:262
  9.3 4.5 %collective-permute-start.1 = (f32[1,512]{1,0:T(1,128)S(1)}, f32[1,512]{1,0:T(1,128)S(1)}, u32[]{:S(2)}, u32[]{:S(2)}) collective-permute-start(f32[1,512]{1,0:T(1,128)S(1)} %get-tuple-element.28), channel_id=1, source_target_pairs={{0,2},{1,3},{2,0},{3,1},{4,6},{5,7},{6,4},{7,5},{8,10},{9,11},{10,... | collective-permute-start | bytes 6152 | tf_op jit(solution)/shard_map/ppermute | solution.py:262
  9.3 4.5 %collective-permute-start = (f32[1,512]{1,0:T(1,128)S(1)}, f32[1,512]{1,0:T(1,128)S(1)}, u32[]{:S(2)}, u32[]{:S(2)}) collective-permute-start(f32[1,512]{1,0:T(1,128)S(1)} %get-tuple-element.28), channel_id=1, source_target_pairs={{0,1},{1,0},{2,3},{3,2},{4,5},{5,4},{6,7},{7,6},{8,9},{9,8},{10,11... | collective-permute-start | bytes 6152 | tf_op jit(solution)/shard_map/ppermute | solution.py:262
  10.0 5.3 %collective-permute-start.3 = (f32[64,512]{1,0:T(8,128)S(1)}, f32[64,512]{1,0:T(8,128)S(1)}, u32[]{:S(2)}, u32[]{:S(2)}) collective-permute-start(f32[64,512]{1,0:T(8,128)S(1)} %get-tuple-element.30.x_ref.own_ref), channel_id=1, source_target_pairs={{0,4},{4,0},{1,5},{5,1},{2,6},{6,2},{3,7},{7,3},{8,12},{12,8},{9,1... | collective-permute-start | bytes 393224 | tf_op jit(solution)/shard_map/ppermute | solution.py:262
  13.8 1.4 %collective-permute-start.4 = (f32[1,512]{1,0:T(1,128)S(1)}, f32[1,512]{1,0:T(1,128)S(1)}, u32[]{:S(2)}, u32[]{:S(2)}) collective-permute-start(f32[1,512]{1,0:T(1,128)S(1)} %add_subtract_fusion.phi_ref), channel_id=1, source_target_pairs={{0,4},{4,0},{1,5},{5,1},{2,6},{6,2},{3,7},{7,3},{8,12},{12,8},{9,1... | collective-permute-start | bytes 6152 | tf_op jit(solution)/shard_map/ppermute | solution.py:262
  17.1 1.4 %collective-permute-start.5 = (f32[1,1024]{1,0:T(1,128)S(1)}, f32[1,1024]{1,0:T(1,128)S(1)}, u32[]{:S(2)}, u32[]{:S(2)}) collective-permute-start(f32[1,1024]{1,0:T(1,128)S(1)} %get-tuple-element.37.own_ref), channel_id=1, source_target_pairs={{0,4},{4,0},{1,5},{5,1},{2,6},{6,2},{3,7},{7,3},{8,12},{12,8},{9,1... | collective-permute-start | bytes 12296 | tf_op jit(solution)/shard_map/ppermute | solution.py:262
  18.5 5.9 %collective-permute-start.8 = (f32[1,1024]{1,0:T(1,128)S(1)}, f32[1,1024]{1,0:T(1,128)S(1)}, u32[]{:S(2)}, u32[]{:S(2)}) collective-permute-start(f32[1,1024]{1,0:T(1,128)S(1)} %meet.1.refs_0_.after_ref), channel_id=1, source_target_pairs={{0,3},{1,2},{2,1},{3,0},{4,7},{5,6},{6,5},{7,4},{8,11},{9,10},{10,... | collective-permute-start | bytes 12296 | tf_op jit(solution)/shard_map/ppermute | solution.py:262
  20.0 4.5 %collective-permute-start.7 = (f32[1,1024]{1,0:T(1,128)S(1)}, f32[1,1024]{1,0:T(1,128)S(1)}, u32[]{:S(2)}, u32[]{:S(2)}) collective-permute-start(f32[1,1024]{1,0:T(1,128)S(1)} %meet.1.refs_0_.after_ref), channel_id=1, source_target_pairs={{0,2},{1,3},{2,0},{3,1},{4,6},{5,7},{6,4},{7,5},{8,10},{9,11},{10,... | collective-permute-start | bytes 12296 | tf_op jit(solution)/shard_map/ppermute | solution.py:262
  20.5 4.0 %collective-permute-start.6 = (f32[1,1024]{1,0:T(1,128)S(1)}, f32[1,1024]{1,0:T(1,128)S(1)}, u32[]{:S(2)}, u32[]{:S(2)}) collective-permute-start(f32[1,1024]{1,0:T(1,128)S(1)} %meet.1.refs_0_.after_ref), channel_id=1, source_target_pairs={{0,1},{1,0},{2,3},{3,2},{4,5},{5,4},{6,7},{7,6},{8,9},{9,8},{10,11... | collective-permute-start | bytes 12296 | tf_op jit(solution)/shard_map/ppermute | solution.py:262
  26.2 6.5 %collective-permute-start.9 = (f32[64,512]{1,0:T(8,128)S(1)}, f32[64,512]{1,0:T(8,128)S(1)}, u32[]{:S(2)}, u32[]{:S(2)}) collective-permute-start(f32[64,512]{1,0:T(8,128)S(1)} %get-tuple-element.44), channel_id=1, source_target_pairs={{0,24},{8,16},{16,8},{24,0},{1,25},{9,17},{17,9},{25,1},{2,26},{10... | collective-permute-start | bytes 393224 | tf_op jit(solution)/shard_map/ppermute | solution.py:262
  28.7 6.1 %collective-permute-start.10 = (f32[64,512]{1,0:T(8,128)S(1)}, f32[64,512]{1,0:T(8,128)S(1)}, u32[]{:S(2)}, u32[]{:S(2)}) collective-permute-start(f32[64,512]{1,0:T(8,128)S(1)} %get-tuple-element.45), channel_id=1, source_target_pairs={{0,16},{8,24},{16,0},{24,8},{1,17},{9,25},{17,1},{25,9},{2,18},{10... | collective-permute-start | bytes 393224 | tf_op jit(solution)/shard_map/ppermute | solution.py:262
  29.2 5.6 %collective-permute-start.11 = (f32[64,512]{1,0:T(8,128)S(1)}, f32[64,512]{1,0:T(8,128)S(1)}, u32[]{:S(2)}, u32[]{:S(2)}) collective-permute-start(f32[64,512]{1,0:T(8,128)S(1)} %get-tuple-element.46), channel_id=1, source_target_pairs={{0,8},{8,0},{16,24},{24,16},{1,9},{9,1},{17,25},{25,17},{2,10},{10... | collective-permute-start | bytes 393224 | tf_op jit(solution)/shard_map/ppermute | solution.py:262
  34.9 7.3 %collective-permute-start.14 = (f32[64,512]{1,0:T(8,128)S(1)}, f32[64,512]{1,0:T(8,128)S(1)}, u32[]{:S(2)}, u32[]{:S(2)}) collective-permute-start(f32[64,512]{1,0:T(8,128)S(1)} %add_multiply_fusion.refs_0_), channel_id=1, source_target_pairs={{0,24},{8,16},{16,8},{24,0},{1,25},{9,17},{17,9},{25,1},{2,26},{10... | collective-permute-start | bytes 393224 | tf_op jit(solution)/shard_map/ppermute | solution.py:262
  36.6 7.0 %collective-permute-start.13 = (f32[64,512]{1,0:T(8,128)S(1)}, f32[64,512]{1,0:T(8,128)S(1)}, u32[]{:S(2)}, u32[]{:S(2)}) collective-permute-start(f32[64,512]{1,0:T(8,128)S(1)} %add_multiply_fusion.refs_0_), channel_id=1, source_target_pairs={{0,16},{8,24},{16,0},{24,8},{1,17},{9,25},{17,1},{25,9},{2,18},{10... | collective-permute-start | bytes 393224 | tf_op jit(solution)/shard_map/ppermute | solution.py:262
  37.9 5.8 %collective-permute-start.12 = (f32[64,512]{1,0:T(8,128)S(1)}, f32[64,512]{1,0:T(8,128)S(1)}, u32[]{:S(2)}, u32[]{:S(2)}) collective-permute-start(f32[64,512]{1,0:T(8,128)S(1)} %add_multiply_fusion.refs_0_), channel_id=1, source_target_pairs={{0,8},{8,0},{16,24},{24,16},{1,9},{9,1},{17,25},{25,17},{2,10},{10... | collective-permute-start | bytes 393224 | tf_op jit(solution)/shard_map/ppermute | solution.py:262
  38.5 6.2 %collective-permute-start.16 = (f32[1,2048]{1,0:T(1,128)S(1)}, f32[1,2048]{1,0:T(1,128)S(1)}, u32[]{:S(2)}, u32[]{:S(2)}) collective-permute-start(f32[1,2048]{1,0:T(1,128)S(1)} %constant_dynamic-update-slice_fusion.refs_5_), channel_id=1, source_target_pairs={{0,4},{4,0},{1,5},{5,1},{2,6},{6,2},{3,7},{7,3},{8,12},{12,8},{9,1... | collective-permute-start | bytes 24584 | tf_op jit(solution)/shard_map/ppermute | solution.py:262
  38.5 6.2 %collective-permute-start.15 = (f32[64,512]{1,0:T(8,128)S(1)}, f32[64,512]{1,0:T(8,128)S(1)}, u32[]{:S(2)}, u32[]{:S(2)}) collective-permute-start(f32[64,512]{1,0:T(8,128)S(1)} %add_multiply_fusion.refs_0_), channel_id=1, source_target_pairs={{0,4},{4,0},{1,5},{5,1},{2,6},{6,2},{3,7},{7,3},{8,12},{12,8},{9,1... | collective-permute-start | bytes 393224 | tf_op jit(solution)/shard_map/ppermute | solution.py:262
  42.2 3.4 %collective-permute-start.19 = (f32[64,512]{1,0:T(8,128)S(1)}, f32[64,512]{1,0:T(8,128)S(1)}, u32[]{:S(2)}, u32[]{:S(2)}) collective-permute-start(f32[64,512]{1,0:T(8,128)S(1)} %collective-permute-done.14.refs_3_), channel_id=1, source_target_pairs={{0,4},{4,0},{1,5},{5,1},{2,6},{6,2},{3,7},{7,3},{8,12},{12,8},{9,1... | collective-permute-start | bytes 393224 | tf_op jit(solution)/shard_map/ppermute | solution.py:262
  43.6 2.0 %collective-permute-start.18 = (f32[64,512]{1,0:T(8,128)S(1)}, f32[64,512]{1,0:T(8,128)S(1)}, u32[]{:S(2)}, u32[]{:S(2)}) collective-permute-start(f32[64,512]{1,0:T(8,128)S(1)} %collective-permute-done.13.refs_2_), channel_id=1, source_target_pairs={{0,4},{4,0},{1,5},{5,1},{2,6},{6,2},{3,7},{7,3},{8,12},{12,8},{9,1... | collective-permute-start | bytes 393224 | tf_op jit(solution)/shard_map/ppermute | solution.py:262
  43.7 1.9 %collective-permute-start.17 = (f32[64,512]{1,0:T(8,128)S(1)}, f32[64,512]{1,0:T(8,128)S(1)}, u32[]{:S(2)}, u32[]{:S(2)}) collective-permute-start(f32[64,512]{1,0:T(8,128)S(1)} %collective-permute-done.12.refs_1_), channel_id=1, source_target_pairs={{0,4},{4,0},{1,5},{5,1},{2,6},{6,2},{3,7},{7,3},{8,12},{12,8},{9,1... | collective-permute-start | bytes 393224 | tf_op jit(solution)/shard_map/ppermute | solution.py:262
